TPU v7x, 32 devices: a whole 2x2x4 slice. The times are simulated.
32 devices in a mesh: fsdp: 2 (over y), ctx: 4 (over x, core), tp: 4 (over z).
Axes of the slice: x: 2, y: 2, z: 4, core: 2. Of those that a mesh axis runs over, the one named last changes fastest.
Arguments:
- tokens: bfloat16 [4, 2048, 2048], P('fsdp', 'ctx', 'tp'), may hold values from -6 to 6
- lengths: int32 [4], P('fsdp'), may hold values from 1024 to 2048, as said below
- cotangent: bfloat16 [4, 2048, 2048], P('fsdp', 'ctx', 'tp'), may hold values from -6 to 6
- first_gain: bfloat16 [2048], P(('fsdp', 'ctx')), may hold values from 0.25 to 1.75
- first_shift: bfloat16 [2048], P(('fsdp', 'ctx')), may hold values from -1.75 to 1.75
- joined_weight: bfloat16 [2048, 8, 768], P(('fsdp', 'ctx'), 'tp'), may hold values from -0.125 to 0.125
- joined_bias: bfloat16 [8, 768], P('tp', ('fsdp', 'ctx')), may hold values from -1.75 to 1.75
- output_weight: bfloat16 [2048, 8, 256], P(('fsdp', 'ctx'), 'tp'), may hold values from -0.75 to 0.75
- output_bias: bfloat16 [2048], P(('fsdp', 'ctx')), may hold values from -1.75 to 1.75
- second_gain: bfloat16 [2048], P(('fsdp', 'ctx')), may hold values from 0.25 to 1.75
- second_shift: bfloat16 [2048], P(('fsdp', 'ctx')), may hold values from -1.75 to 1.75
- inner_weight: bfloat16 [2048, 8192], P(('fsdp', 'ctx'), 'tp'), may hold values from -0.125 to 0.125
- inner_bias: bfloat16 [256, 32], P('tp', ('fsdp', 'ctx')), may hold values from -3 to 3
- outer_weight: bfloat16 [2048, 8192], P(('fsdp', 'ctx'), 'tp'), may hold values from -0.0625 to 0.0625
- outer_bias: bfloat16 [2048], P(('fsdp', 'ctx')), may hold values from -1.75 to 1.75
Outputs:
- layer_out: bfloat16 [4, 2048, 2048], P('fsdp', 'ctx', 'tp')
- tokens_grad: float32 [4, 2048, 2048], P('fsdp', 'ctx', 'tp')
- first_gain_grad: float32 [2048], P(('fsdp', 'ctx'))
- first_shift_grad: float32 [2048], P(('fsdp', 'ctx'))
- joined_weight_grad: float32 [2048, 8, 768], P(('fsdp', 'ctx'), 'tp')
- joined_bias_grad: float32 [8, 768], P('tp', ('fsdp', 'ctx'))
- output_weight_grad: float32 [2048, 8, 256], P(('fsdp', 'ctx'), 'tp')
- output_bias_grad: float32 [2048], P(('fsdp', 'ctx'))
- second_gain_grad: float32 [2048], P(('fsdp', 'ctx'))
- second_shift_grad: float32 [2048], P(('fsdp', 'ctx'))
- inner_weight_grad: float32 [2048, 8192], P(('fsdp', 'ctx'), 'tp')
- inner_bias_grad: float32 [256, 32], P('tp', ('fsdp', 'ctx'))
- outer_weight_grad: float32 [2048, 8192], P(('fsdp', 'ctx'), 'tp')
- outer_bias_grad: float32 [2048], P(('fsdp', 'ctx'))
Inputs may be any that keep to these rules, and one draw needn't show every extreme that they name: `lengths`: positions at or past a sequence's length are padding. In every draw some sequence has the full length 2048 and another has exactly 1024.
All inputs are finite; a program needn't handle non-finite values.
Results may differ from a plain program's by a relative error of at most 0.018.
Values may be sent and summed in bfloat16 or wider, within the bound.
No kernel may reach another device: no remote copies, remote signals or barrier semaphores. Data moves between devices by JAX's collectives and lax.ppermute only.
A program may use at most 256 MiB of HBM per device.

v0:
```python
import jax
import jax.numpy as jnp
from jax import lax
from jax.sharding import PartitionSpec as P

HEAD = 256
ROTARY = 64


def normalize(rows):
    center = jnp.mean(rows, axis=-1, keepdims=True)
    shifted = rows - center
    inverse = lax.rsqrt(jnp.mean(shifted * shifted, axis=-1, keepdims=True) + 1e-05)
    return (shifted * inverse, inverse)


def rotate(values, cosine, sine):
    half = cosine.shape[-1]
    front = values[..., :half]
    back = values[..., half : 2 * half]
    return jnp.concatenate(
        [front * cosine - back * sine, back * cosine + front * sine, values[..., 2 * half :]],
        axis=-1,
    )


def gelu_slope(upper):
    return (
        0.5 * (1.0 + lax.erf(upper * 0.7071067811865476))
        + upper * jnp.exp(-0.5 * upper * upper) * 0.3989422804014327
    )


def attention_probs(query_part, key_part, allowed_part):
    scores = jnp.einsum(
        "ihd,jhd->hij", query_part, key_part, preferred_element_type=jnp.float32
    ) * HEAD ** (-0.5)
    scores = jnp.where(allowed_part[None], scores, -1e30)
    largest = jnp.max(scores, axis=-1, keepdims=True)
    weights = jnp.exp(scores - largest)
    return weights / jnp.sum(weights, axis=-1, keepdims=True)


def forward_one(item):
    query_part, key_part, value_part, allowed_part = item
    probs = attention_probs(query_part, key_part, allowed_part)
    return jnp.einsum(
        "hij,jhd->ihd", probs.astype(jnp.bfloat16), value_part, preferred_element_type=jnp.float32
    ).astype(jnp.bfloat16)


def backward_one(item):
    query_part, key_part, value_part, allowed_part, grad_part = item
    probs = attention_probs(query_part, key_part, allowed_part)
    low_probs = probs.astype(jnp.bfloat16)
    prob_grad = jnp.einsum(
        "ihd,jhd->hij", grad_part, value_part, preferred_element_type=jnp.float32
    )
    row_total = jnp.sum(probs * prob_grad, axis=-1, keepdims=True)
    score_grad = (probs * (prob_grad - row_total)).astype(jnp.bfloat16)
    query_grad = jnp.einsum(
        "hij,jhd->ihd", score_grad, key_part, preferred_element_type=jnp.float32
    ) * HEAD ** (-0.5)
    key_grad = jnp.einsum(
        "hij,ihd->jhd", score_grad, query_part, preferred_element_type=jnp.float32
    ) * HEAD ** (-0.5)
    value_grad = jnp.einsum(
        "hij,ihd->jhd", low_probs, grad_part, preferred_element_type=jnp.float32
    )
    return (query_grad, key_grad, value_grad)


def body(
    tokens,
    lengths,
    cotangent,
    first_gain,
    first_shift,
    joined_weight,
    joined_bias,
    output_weight,
    output_bias,
    second_gain,
    second_shift,
    inner_weight,
    inner_bias,
    outer_weight,
    outer_bias,
):
    gathered = (
        lax.all_gather(first_gain, ("fsdp", "ctx"), axis=0, tiled=True),
        lax.all_gather(first_shift, ("fsdp", "ctx"), axis=0, tiled=True),
        lax.all_gather(joined_weight, ("fsdp", "ctx"), axis=0, tiled=True),
        lax.all_gather(joined_bias, ("fsdp", "ctx"), axis=1, tiled=True),
        lax.all_gather(output_weight, ("fsdp", "ctx"), axis=0, tiled=True),
        lax.all_gather(output_bias, ("fsdp", "ctx"), axis=0, tiled=True),
        lax.all_gather(second_gain, ("fsdp", "ctx"), axis=0, tiled=True),
        lax.all_gather(second_shift, ("fsdp", "ctx"), axis=0, tiled=True),
        lax.all_gather(inner_weight, ("fsdp", "ctx"), axis=0, tiled=True),
        lax.all_gather(inner_bias, ("fsdp", "ctx"), axis=1, tiled=True),
        lax.all_gather(outer_weight, ("fsdp", "ctx"), axis=0, tiled=True),
        lax.all_gather(outer_bias, ("fsdp", "ctx"), axis=0, tiled=True),
    )
    (
        whole_first_gain,
        whole_first_shift,
        whole_joined_weight,
        whole_joined_bias,
        whole_output_weight,
        whole_output_bias,
        whole_second_gain,
        whole_second_shift,
        whole_inner_weight,
        whole_inner_bias,
        whole_outer_weight,
        whole_outer_bias,
    ) = gathered
    seqs_here, local_len, width_part = tokens.shape
    whole_rows, whole_cot = (
        lax.all_gather(tokens, "tp", axis=2, tiled=True),
        lax.all_gather(cotangent, "tp", axis=2, tiled=True),
    )
    width = whole_rows.shape[2]
    count = seqs_here * local_len
    positions = lax.axis_index("ctx") * local_len + jnp.arange(local_len, dtype=jnp.int32)
    valid = (positions[None, :] < lengths[:, None]).astype(jnp.float32)
    rows = whole_rows.reshape(count, width).astype(jnp.float32)
    normed, inverse = normalize(rows)
    first_in = (
        normed * whole_first_gain.astype(jnp.float32) + whole_first_shift.astype(jnp.float32)
    ).astype(jnp.bfloat16)
    second_in = (
        normed * whole_second_gain.astype(jnp.float32) + whole_second_shift.astype(jnp.float32)
    ).astype(jnp.bfloat16)
    joined = jnp.einsum(
        "tc,chk->thk", first_in, whole_joined_weight, preferred_element_type=jnp.float32
    ) + whole_joined_bias.astype(jnp.float32)
    heads_here = joined.shape[1]
    half = ROTARY // 2
    frequency = 1.0 / 10000.0 ** (jnp.arange(half, dtype=jnp.float32) * 2.0 / ROTARY)
    angles = positions.astype(jnp.float32)[:, None] * frequency[None, :]
    cosine = jnp.tile(jnp.cos(angles), (seqs_here, 1))[:, None, :]
    sine = jnp.tile(jnp.sin(angles), (seqs_here, 1))[:, None, :]
    query = rotate(joined[..., :HEAD], cosine, sine).astype(jnp.bfloat16)
    keys = rotate(joined[..., HEAD : 2 * HEAD], cosine, sine).astype(jnp.bfloat16)
    values = joined[..., 2 * HEAD :].astype(jnp.bfloat16)
    key_all, value_all = (
        lax.all_gather(
            keys.reshape(seqs_here, local_len, heads_here, HEAD), "ctx", axis=1, tiled=True
        ),
        lax.all_gather(
            values.reshape(seqs_here, local_len, heads_here, HEAD), "ctx", axis=1, tiled=True
        ),
    )
    key_pos = jnp.arange(key_all.shape[1], dtype=jnp.int32)
    allowed = (key_pos[None, None, :] <= positions[None, :, None]) & (
        key_pos[None, None, :] < lengths[:, None, None]
    )
    query_seq = query.reshape(seqs_here, local_len, heads_here, HEAD)
    context = lax.map(forward_one, (query_seq, key_all, value_all, allowed)).reshape(
        count, heads_here, HEAD
    )
    attention_part = jnp.einsum(
        "thd,ehd->te", context, whole_output_weight, preferred_element_type=jnp.float32
    )
    upper = jnp.dot(
        second_in, whole_inner_weight, preferred_element_type=jnp.float32
    ) + whole_inner_bias.reshape(-1).astype(jnp.float32)
    active = jax.nn.gelu(upper, approximate=False).astype(jnp.bfloat16)
    feed_part = jnp.einsum(
        "tf,ef->te", active, whole_outer_weight, preferred_element_type=jnp.float32
    )
    summed = lax.psum_scatter(
        (attention_part + feed_part).reshape(seqs_here, local_len, width).astype(jnp.bfloat16),
        "tp",
        scatter_dimension=2,
        tiled=True,
    ).astype(jnp.float32)
    bias_sum = whole_output_bias.astype(jnp.float32) + whole_outer_bias.astype(jnp.float32)
    own_start = lax.axis_index("tp") * width_part
    own_bias = lax.dynamic_slice_in_dim(bias_sum, own_start, width_part)
    layer_out = (valid[:, :, None] * (tokens.astype(jnp.float32) + summed + own_bias)).astype(
        jnp.bfloat16
    )
    (
        back_first_gain,
        back_joined_weight,
        back_output_weight,
        back_second_gain,
        back_inner_weight,
        back_outer_weight,
    ) = (
        lax.all_gather(first_gain, ("fsdp", "ctx"), axis=0, tiled=True),
        lax.all_gather(joined_weight, ("fsdp", "ctx"), axis=0, tiled=True),
        lax.all_gather(output_weight, ("fsdp", "ctx"), axis=0, tiled=True),
        lax.all_gather(second_gain, ("fsdp", "ctx"), axis=0, tiled=True),
        lax.all_gather(inner_weight, ("fsdp", "ctx"), axis=0, tiled=True),
        lax.all_gather(outer_weight, ("fsdp", "ctx"), axis=0, tiled=True),
    )
    grad_rows = (
        (whole_cot.astype(jnp.float32) * valid[:, :, None])
        .astype(jnp.bfloat16)
        .reshape(count, width)
    )
    bias_grad = jnp.sum(grad_rows, axis=0, dtype=jnp.float32)
    output_weight_grad = jnp.einsum(
        "te,thd->ehd", grad_rows, context, preferred_element_type=jnp.float32
    )
    outer_weight_grad = jnp.einsum(
        "te,tf->ef", grad_rows, active, preferred_element_type=jnp.float32
    )
    context_grad = jnp.einsum(
        "te,ehd->thd", grad_rows, back_output_weight, preferred_element_type=jnp.float32
    ).astype(jnp.bfloat16)
    active_grad = jnp.dot(grad_rows, back_outer_weight, preferred_element_type=jnp.float32)
    upper_grad = (active_grad * gelu_slope(upper)).astype(jnp.bfloat16)
    inner_bias_grad = jnp.sum(upper_grad, axis=0, dtype=jnp.float32).reshape(whole_inner_bias.shape)
    inner_weight_grad = jnp.einsum(
        "tc,tf->cf", second_in, upper_grad, preferred_element_type=jnp.float32
    )
    second_in_grad = jnp.einsum(
        "tf,cf->tc", upper_grad, back_inner_weight, preferred_element_type=jnp.float32
    )
    query_grad, key_grad, value_grad = lax.map(
        backward_one,
        (
            query_seq,
            key_all,
            value_all,
            allowed,
            context_grad.reshape(seqs_here, local_len, heads_here, HEAD),
        ),
    )
    key_own, value_own = (
        lax.psum_scatter(
            key_grad.astype(jnp.bfloat16), "ctx", scatter_dimension=1, tiled=True
        ).astype(jnp.float32),
        lax.psum_scatter(
            value_grad.astype(jnp.bfloat16), "ctx", scatter_dimension=1, tiled=True
        ).astype(jnp.float32),
    )
    joined_grad = jnp.concatenate(
        [
            rotate(query_grad.reshape(count, heads_here, HEAD), cosine, -sine),
            rotate(key_own.reshape(count, heads_here, HEAD), cosine, -sine),
            value_own.reshape(count, heads_here, HEAD),
        ],
        axis=-1,
    ).astype(jnp.bfloat16)
    joined_bias_grad = jnp.sum(joined_grad, axis=0, dtype=jnp.float32)
    joined_weight_grad = jnp.einsum(
        "tc,thk->chk", first_in, joined_grad, preferred_element_type=jnp.float32
    )
    first_in_grad = jnp.einsum(
        "thk,chk->tc", joined_grad, back_joined_weight, preferred_element_type=jnp.float32
    )
    first_share, second_share = (
        lax.psum_scatter(
            first_in_grad.astype(jnp.bfloat16), "tp", scatter_dimension=1, tiled=True
        ).astype(jnp.float32),
        lax.psum_scatter(
            second_in_grad.astype(jnp.bfloat16), "tp", scatter_dimension=1, tiled=True
        ).astype(jnp.float32),
    )
    normed_own = lax.dynamic_slice_in_dim(normed, own_start, width_part, 1)
    first_scaled = first_share * lax.dynamic_slice_in_dim(
        back_first_gain.astype(jnp.float32), own_start, width_part
    )
    second_scaled = second_share * lax.dynamic_slice_in_dim(
        back_second_gain.astype(jnp.float32), own_start, width_part
    )
    row_terms = jnp.stack(
        [
            jnp.sum(first_scaled, axis=1),
            jnp.sum(first_scaled * normed_own, axis=1),
            jnp.sum(second_scaled, axis=1),
            jnp.sum(second_scaled * normed_own, axis=1),
        ],
        axis=1,
    )
    column_own = jnp.stack(
        [
            jnp.sum(first_share * normed_own, axis=0),
            jnp.sum(first_share, axis=0),
            jnp.sum(second_share * normed_own, axis=0),
            jnp.sum(second_share, axis=0),
        ],
        axis=0,
    )
    column_terms = lax.dynamic_update_slice_in_dim(
        jnp.zeros((4, width), jnp.float32), column_own, own_start, 1
    )
    row_sums, column_sums = (
        lax.psum(row_terms.astype(jnp.bfloat16), "tp").astype(jnp.float32),
        lax.psum(column_terms.astype(jnp.bfloat16), "tp").astype(jnp.float32),
    )
    means = row_sums / width
    own_rows = lax.dynamic_slice_in_dim(grad_rows, own_start, width_part, 1).astype(jnp.float32)
    own_grad = (
        own_rows
        + inverse * (first_scaled - means[:, 0:1] - normed_own * means[:, 1:2])
        + inverse * (second_scaled - means[:, 2:3] - normed_own * means[:, 3:4])
    )
    tokens_grad = own_grad.reshape(seqs_here, local_len, width_part)
    first_gain_sum = column_sums[0]
    first_shift_sum = column_sums[1]
    second_gain_sum = column_sums[2]
    second_shift_sum = column_sums[3]
    results = (
        lax.psum_scatter(
            first_gain_sum.astype(jnp.bfloat16), ("fsdp", "ctx"), scatter_dimension=0, tiled=True
        ).astype(jnp.float32),
        lax.psum_scatter(
            first_shift_sum.astype(jnp.bfloat16), ("fsdp", "ctx"), scatter_dimension=0, tiled=True
        ).astype(jnp.float32),
        lax.psum_scatter(
            joined_weight_grad.astype(jnp.bfloat16),
            ("fsdp", "ctx"),
            scatter_dimension=0,
            tiled=True,
        ).astype(jnp.float32),
        lax.psum_scatter(
            joined_bias_grad.astype(jnp.bfloat16), ("fsdp", "ctx"), scatter_dimension=1, tiled=True
        ).astype(jnp.float32),
        lax.psum_scatter(
            output_weight_grad.astype(jnp.bfloat16),
            ("fsdp", "ctx"),
            scatter_dimension=0,
            tiled=True,
        ).astype(jnp.float32),
        lax.psum_scatter(
            bias_grad.astype(jnp.bfloat16), ("fsdp", "ctx"), scatter_dimension=0, tiled=True
        ).astype(jnp.float32),
        lax.psum_scatter(
            second_gain_sum.astype(jnp.bfloat16), ("fsdp", "ctx"), scatter_dimension=0, tiled=True
        ).astype(jnp.float32),
        lax.psum_scatter(
            second_shift_sum.astype(jnp.bfloat16), ("fsdp", "ctx"), scatter_dimension=0, tiled=True
        ).astype(jnp.float32),
        lax.psum_scatter(
            inner_weight_grad.astype(jnp.bfloat16), ("fsdp", "ctx"), scatter_dimension=0, tiled=True
        ).astype(jnp.float32),
        lax.psum_scatter(
            inner_bias_grad.astype(jnp.bfloat16), ("fsdp", "ctx"), scatter_dimension=1, tiled=True
        ).astype(jnp.float32),
        lax.psum_scatter(
            outer_weight_grad.astype(jnp.bfloat16), ("fsdp", "ctx"), scatter_dimension=0, tiled=True
        ).astype(jnp.float32),
        lax.psum_scatter(
            bias_grad.astype(jnp.bfloat16), ("fsdp", "ctx"), scatter_dimension=0, tiled=True
        ).astype(jnp.float32),
    )
    return (layer_out, tokens_grad) + tuple(results)


def solution(mesh):
    return jax.shard_map(
        body,
        mesh=mesh,
        in_specs=(
            P("fsdp", "ctx", "tp"),
            P("fsdp"),
            P("fsdp", "ctx", "tp"),
            P(("fsdp", "ctx")),
            P(("fsdp", "ctx")),
            P(("fsdp", "ctx"), "tp", None),
            P("tp", ("fsdp", "ctx")),
            P(("fsdp", "ctx"), "tp", None),
            P(("fsdp", "ctx")),
            P(("fsdp", "ctx")),
            P(("fsdp", "ctx")),
            P(("fsdp", "ctx"), "tp"),
            P("tp", ("fsdp", "ctx")),
            P(("fsdp", "ctx"), "tp"),
            P(("fsdp", "ctx")),
        ),
        out_specs=(
            P("fsdp", "ctx", "tp"),
            P("fsdp", "ctx", "tp"),
            P(("fsdp", "ctx")),
            P(("fsdp", "ctx")),
            P(("fsdp", "ctx"), "tp", None),
            P("tp", ("fsdp", "ctx")),
            P(("fsdp", "ctx"), "tp", None),
            P(("fsdp", "ctx")),
            P(("fsdp", "ctx")),
            P(("fsdp", "ctx")),
            P(("fsdp", "ctx"), "tp"),
            P("tp", ("fsdp", "ctx")),
            P(("fsdp", "ctx"), "tp"),
            P(("fsdp", "ctx")),
        ),
        check_vma=False,
    )
```

profile of v0, /device:TPU:0, one launch (start us, length us, event | category | flops | bytes accessed | tf_op | source)
XLA Modules:
  0.0 1079.1 jit_solution(15421667100661152163)
XLA Ops:
  14.2 10.3 all-gather
  25.2 8.8 all-gather.1
  34.1 7.9 all-gather.2
  42.6 50.5 %all-gather.17.cloned.1.call-done = bf16[2,512,2048]{2,1,0:T(8,128)(2,1)} async-done(((bf16[2,512,512]{2,1,0:T(8,128)(2,1)}), bf16[2,512,2048]{2,1,0:T(8,128)(2,1)}) %all-gather.17.cloned.1.call-update) | async-done | bytes 4194320 | tf_op jit(solution)/shard_map/all_gather | solution.py:120
  104.2 36.5 %all-gather.19.cloned.1.call-done = bf16[2048,2,768]{0,2,1:T(8,128)(2,1)} async-done(((bf16[256,2,768]{0,2,1:T(8,128)(2,1)}), bf16[2048,2,768]{0,2,1:T(8,128)(2,1)}) %all-gather.19.cloned.1.call-update) | async-done | bytes 6291472 | tf_op jit(solution)/shard_map/all_gather | solution.py:93
  140.8 14.7 %fusion.114 = (bf16[1024,2,768]{0,2,1:T(8,128)(2,1)}, f32[1024,2,768]{0,2,1:T(8,128)S(1)}) fusion(f32[2,768]{1,0:T(2,128)S(1)} %bitcast.265, bf16[2048,2,768]{0,2,1:T(8,128)(2,1)} %all-gather.19.cloned.1.call-done, f32[1024,2048]{1,0:T(8,128)} %fusion.75, f32[2048]{0:T(1024)S(1)} %bitcast.261, f32[2048]{0:T(1024)S(1)} %bitcast.251), kind=kOutput, calls=%fused_computation.178 | convolution fusion | flops 6451888128 | bytes 24139776 | tf_op jit(solution)/shard_map/tc,chk->thk/dot_general | solution.py:135
  173.7 49.4 %all-gather.31.cloned.1.call-done = bf16[2,512,2048]{2,1,0:T(8,128)(2,1)} async-done(((bf16[2,512,512]{2,1,0:T(8,128)(2,1)}), bf16[2,512,2048]{2,1,0:T(8,128)(2,1)}) %all-gather.31.cloned.1.call-update) | async-done | bytes 4194320 | tf_op jit(solution)/shard_map/all_gather | solution.py:121
  223.1 5.7 fusion.109
  228.9 23.0 %all-gather.25.cloned.1.call-done = bf16[2048,2,256]{2,0,1:T(8,128)(2,1)} async-done(((bf16[256,2,256]{2,0,1:T(8,128)(2,1)}), bf16[2048,2,256]{2,0,1:T(8,128)(2,1)}) %all-gather.25.cloned.1.call-update) | async-done | bytes 2097168 | tf_op jit(solution)/shard_map/all_gather | solution.py:95
  251.9 6.2 convolution_convert_fusion.4
  263.1 25.3 %all-gather.23.cloned.1.call-done = bf16[2,2048,2,256]{3,1,2,0:T(8,128)(2,1)} async-done(((bf16[2,512,2,256]{3,1,2,0:T(8,128)(2,1)}), bf16[2,2048,2,256]{3,1,2,0:T(8,128)(2,1)}) %all-gather.23.cloned.1.call-update) | async-done | bytes 4194320 | tf_op jit(solution)/shard_map/all_gather | solution.py:148
  288.4 36.5 %all-gather.21.cloned.1.call-done = bf16[2,2048,2,256]{3,1,2,0:T(8,128)(2,1)} async-done(((bf16[2,512,2,256]{3,1,2,0:T(8,128)(2,1)}), bf16[2,2048,2,256]{3,1,2,0:T(8,128)(2,1)}) %all-gather.21.cloned.1.call-update) | async-done | bytes 4194320 | tf_op jit(solution)/shard_map/all_gather | solution.py:151
  324.9 97.6 %while.25 = (s32[]{:T(128)}, f32[2,512,2,256]{1,0,3,2:T(2,128)}, bf16[2,2048,2,256]{1,3,2,0:T(8,128)(2,1)}, bf16[2,2048,2,256]{1,3,2,0:T(8,128)(2,1)}, bf16[2,20...) while((s32[]{:T(128)}, f32[2,512,2,256]{1,0,3,2:T(2,128)}, ...), condition=%wide.region_11.12_spmd, body=%wide.region_7.11_spmd.sunk | while | flops 5401478144 | bytes 184578352 | solution.py:224
  325.1 6.2 fusion.169
  331.4 10.5 fusion.170
  354.5 19.6 %dynamic_update_slice.30 = f32[2,512,2,256]{1,0,3,2:T(2,128)} dynamic-update-slice(f32[2,512,2,256]{1,0,3,2:T(2,128)} %get-tuple-element.442, f32[1,512,2,256]{1,0,3,2:T(1,128)S(1)} %copy.192, s32[]{:T(128)} %get-tuple-element.441, s32[]{:T(128)} %constant.73.clone.1..sunk, s32[]{:T(128)} %constant.73.clone.1..sunk, s32[]{:T(128)} %constant.73.clone.1..sunk) | dynamic-update-slice | bytes 2097156 | tf_op jit(solution)/shard_map/while/body/jit(dynamic_update_index_in_dim)/dynamic_update_slice | solution.py:224
  374.2 6.3 fusion.169
  380.6 9.5 fusion.170
  402.7 19.7 %dynamic_update_slice.30 = f32[2,512,2,256]{1,0,3,2:T(2,128)} dynamic-update-slice(f32[2,512,2,256]{1,0,3,2:T(2,128)} %get-tuple-element.442, f32[1,512,2,256]{1,0,3,2:T(1,128)S(1)} %copy.192, s32[]{:T(128)} %get-tuple-element.441, s32[]{:T(128)} %constant.73.clone.1..sunk, s32[]{:T(128)} %constant.73.clone.1..sunk, s32[]{:T(128)} %constant.73.clone.1..sunk) | dynamic-update-slice | bytes 2097156 | tf_op jit(solution)/shard_map/while/body/jit(dynamic_update_index_in_dim)/dynamic_update_slice | solution.py:224
  423.3 8.8 all-gather.3
  432.1 8.0 all-gather.5
  440.3 8.8 all-gather.4
  449.1 32.2 %while.24 = (s32[]{:T(128)}, bf16[2,512,2,256]{1,3,2,0:T(8,128)(2,1)}, bf16[2,2048,2,256]{3,1,2,0:T(8,128)(2,1)}, pred[2,512,2048]{2,1,0:T(8,128)(4,1)}, bf16[2,...) while((s32[]{:T(128)}, bf16[2,512,2,256]{1,3,2,0:T(8,128)(2,1)}, ...), condition=%wide.region_5.6_spmd, body=%wide.region_2.5_spmd.sunk | while | flops 2164525056 | bytes 50341996 | solution.py:160
  452.4 6.0 fusion.159
  458.4 7.1 fusion.160
  468.6 6.0 fusion.159
  474.6 6.7 fusion.160
  481.3 6.2 bitcast_convert_fusion.1
  487.6 32.0 %fusion.67 = (bf16[1024,2048]{1,0:T(8,128)(2,1)}, f32[1024,2048]{1,0:T(8,128)}) fusion(f32[2048]{0:T(1024)S(1)} %reshape.309, bf16[2048,2048]{1,0:T(8,128)(2,1)} %all-gather.27.cloned.1.call-done, f32[1024,2048]{1,0:T(8,128)} %fusion.75, f32[2048]{0:T(1024)S(1)} %bitcast.263, f32[2048]{0:T(1024)S(1)} %bitcast.254), kind=kOutput, calls=%fused_computation.69 | convolution fusion | flops 8734638080 | bytes 29384704 | tf_op jit(solution)/shard_map/dot_general | solution.py:166
  519.6 14.6 %fusion.116 = f32[1024,2048]{1,0:T(8,128)} fusion(bf16[1024,2048]{1,0:T(8,128)(2,1)} %get-tuple-element.295, bf16[2048,2048]{1,0:T(8,128)(2,1)} %all-gather.29.cloned.1.call-done), kind=kOutput, calls=%fused_computation.180 | convolution fusion | flops 8589934592 | bytes 20971520 | tf_op jit(solution)/shard_map/tf,ef->te/dot_general | solution.py:170
  534.8 8.4 fusion.74
  543.9 18.8 %fusion.115 = (bf16[2048]{0:T(1024)(128)(2,1)}, bf16[1024,2048]{1,0:T(8,128)(2,1)}) fusion(f32[1024,2048]{1,0:T(8,128)} %get-tuple-element.296, f32[2048]{0:T(1024)S(1)} %reshape.309, bf16[1024,2048]{1,0:T(8,128)(2,1)} %bitcast.225, bf16[2048,2048]{1,0:T(8,128)(2,1)} %all-gather.29.cloned.1.call-done), kind=kOutput, calls=%fused_computation.179 | convolution fusion | flops 8615098368 | bytes 25178112 | tf_op jit(solution)/shard_map/dot_general | solution.py:215
  577.5 5.8 concatenate.34
  584.7 15.2 %convolution_convert_fusion.1 = bf16[2048,2048]{1,0:T(8,128)(2,1)} fusion(bf16[1024,2048]{1,0:T(8,128)(2,1)} %get-tuple-element.300, f32[1024,2048]{1,0:T(8,128)} %fusion.75, f32[2048]{0:T(1024)S(1)} %bitcast.264, f32[2048]{0:T(1024)S(1)} %bitcast.255), kind=kOutput, calls=%fused_computation.101 | convolution fusion | flops 8600420352 | bytes 20987904 | tf_op jit(solution)/shard_map/tc,tf->cf/dot_general | solution.py:218
  600.0 14.0 %convolution_convert_fusion = bf16[2048,2048]{1,0:T(8,128)(2,1)} fusion(bf16[1024,2048]{1,0:T(8,128)(2,1)} %bitcast.226, bf16[1024,2048]{1,0:T(8,128)(2,1)} %get-tuple-element.295), kind=kOutput, calls=%fused_computation.100 | convolution fusion | flops 8594128896 | bytes 16777216 | tf_op jit(solution)/shard_map/te,tf->ef/dot_general | solution.py:209
  614.1 14.2 %convolution_convert_fusion.3 = bf16[1024,2048]{1,0:T(8,128)(2,1)} fusion(bf16[1024,2048]{1,0:T(8,128)(2,1)} %get-tuple-element.300, bf16[2048,2048]{1,0:T(8,128)(2,1)} %all-gather.27.cloned.1.call-done), kind=kOutput, calls=%fused_computation.110 | convolution fusion | flops 8592031744 | bytes 16777216 | tf_op jit(solution)/shard_map/tf,cf->tc/dot_general | solution.py:221
  628.4 11.0 %bitcast_convert_fusion = bf16[1024,2048]{1,0:T(8,128)(2,1)} fusion(bf16[1024,2,768]{2,0,1:T(8,128)(2,1)S(1)} %concatenate.34, bf16[2048,2,768]{0,2,1:T(8,128)(2,1)} %all-gather.19.cloned.1.call-done), kind=kOutput, calls=%fused_computation.76 | convolution fusion | flops 6444548096 | bytes 13631488 | tf_op jit(solution)/shard_map/thk,chk->tc/dot_general | solution.py:254
  639.6 12.3 %convolution_convert_fusion.2 = bf16[2048,2,768]{2,0,1:T(8,128)(2,1)} fusion(bf16[1024,2,768]{2,0,1:T(8,128)(2,1)S(1)} %concatenate.34, f32[1024,2048]{1,0:T(8,128)} %fusion.75, f32[2048]{0:T(1024)S(1)} %bitcast.262, f32[2048]{0:T(1024)S(1)} %bitcast.252), kind=kOutput, calls=%fused_computation.102 | convolution fusion | flops 6451888128 | bytes 17842176 | tf_op jit(solution)/shard_map/tc,thk->chk/dot_general | solution.py:251
  654.0 9.0 all-gather.6
  663.0 9.0 all-gather.7
  677.1 16.4 %reduce-scatter.32.cloned.1.call-done = bf16[96,2]{1,0:T(8,128)(2,1)} async-done(((bf16[768,2]{1,0:T(8,128)(2,1)}), bf16[96,2]{1,0:T(8,128)(2,1)}) %reduce-scatter.32.cloned.1.call-update) | async-done | bytes 400
  695.0 73.6 %reduce-scatter.28.cloned.1.call-done = bf16[256,2048]{1,0:T(8,128)(2,1)} async-done(((bf16[2048,2048]{1,0:T(8,128)(2,1)}), bf16[256,2048]{1,0:T(8,128)(2,1)}) %reduce-scatter.28.cloned.1.call-update) | async-done | bytes 1048592 | tf_op jit(solution)/shard_map/reduce_scatter | solution.py:340
  771.4 71.8 %reduce-scatter.30.cloned.1.call-done = bf16[256,2048]{1,0:T(8,128)(2,1)} async-done(((bf16[2048,2048]{1,0:T(8,128)(2,1)}), bf16[256,2048]{1,0:T(8,128)(2,1)}) %reduce-scatter.30.cloned.1.call-update) | async-done | bytes 1048592 | tf_op jit(solution)/shard_map/reduce_scatter | solution.py:346
  846.0 76.3 %reduce-scatter.22.cloned.1.call-done = bf16[1024,512]{1,0:T(8,128)(2,1)} async-done(((bf16[1024,2048]{1,0:T(8,128)(2,1)}), bf16[1024,512]{1,0:T(8,128)(2,1)}) %reduce-scatter.22.cloned.1.call-update) | async-done | bytes 1048592 | tf_op jit(solution)/shard_map/reduce_scatter | solution.py:261
  922.3 79.4 %reduce-scatter.20.cloned.1.call-done = bf16[1024,512]{1,0:T(8,128)(2,1)} async-done(((bf16[1024,2048]{1,0:T(8,128)(2,1)}), bf16[1024,512]{1,0:T(8,128)(2,1)}) %reduce-scatter.20.cloned.1.call-update) | async-done | bytes 1048592 | tf_op jit(solution)/shard_map/reduce_scatter | solution.py:258
  1005.5 18.2 %all-reduce.7 = (bf16[1024,4]{0,1:T(4,128)(2,1)S(1)}, bf16[4,2048]{1,0:T(4,128)(2,1)S(1)}) all-reduce(bf16[1024,4]{0,1:T(4,128)(2,1)S(1)} %pad_maximum_fusion.2, bf16[4,2048]{1,0:T(4,128)(2,1)S(1)} %maximum_dynamic-update-slice_fusion), channel_id=1, replica_groups=mesh['fsdp'=2,'ctx'=4,'tp'=4] {'tp'}, use_global_device_ids=true, to_apply=%region_20.21 | all-reduce | flops 12288 | bytes 49152 | tf_op jit(solution)/shard_map/psum | solution.py:294
  1023.8 23.8 %all-reduce.6 = (bf16[2048]{0:T(1024)(128)(2,1)S(1)}, bf16[2048]{0:T(1024)(128)(2,1)S(1)}, bf16[2048]{0:T(1024)(128)(2,1)S(1)}, bf16[2048]{0:T(1024)(128)(2,1)S(...) all-reduce(bf16[2048]{0:T(1024)(128)(2,1)S(1)} %get-tuple-element.2, ...), channel_id=7, replica_groups=mesh['fsdp'=2,'ctx'=4,'tp'=4] {'fsdp','ctx'}, use_global_device_ids=true, to_apply=%region_26.27.clone | all-reduce | flops 12288 | bytes 49152
  1054.4 13.7 %reduce-scatter.24.cloned.1.call-done = bf16[256,2,768]{2,0,1:T(8,128)(2,1)} async-done(((bf16[2048,2,768]{2,0,1:T(8,128)(2,1)}), bf16[256,2,768]{2,0,1:T(8,128)(2,1)}) %reduce-scatter.24.cloned.1.call-update) | async-done | bytes 786448 | tf_op jit(solution)/shard_map/reduce_scatter | solution.py:316
  (244 shorter events, 119.8 us)
Async XLA Ops:
  7.2 85.9 %all-gather.17.cloned.1.call-start = ((), (), s32[]{:S(2)}) async-start(), calls=%async_computation.10 | async-start | bytes 5242880 | tf_op jit(solution)/shard_map/all_gather | solution.py:120
  7.9 132.8 %all-gather.19.cloned.1.call-start = ((), (), s32[]{:S(2)}) async-start(), calls=%async_computation.11 | async-start | bytes 7077888 | tf_op jit(solution)/shard_map/all_gather | solution.py:93
  11.0 212.1 %all-gather.31.cloned.1.call-start = ((), (), s32[]{:S(2)}) async-start(), calls=%async_computation.18 | async-start | bytes 5242880 | tf_op jit(solution)/shard_map/all_gather | solution.py:121
  11.7 240.2 %all-gather.25.cloned.1.call-start = ((), (), s32[]{:S(2)}) async-start(), calls=%async_computation.14 | async-start | bytes 2359296 | tf_op jit(solution)/shard_map/all_gather | solution.py:95
  13.5 274.9 %all-gather.23.cloned.1.call-start = ((), (), s32[]{:S(2)}) async-start(), calls=%async_computation.13 | async-start | bytes 5242880 | tf_op jit(solution)/shard_map/all_gather | solution.py:148
  24.6 116.2 %copy-start.17 = (f32[8,1,256]{2,1,0:T(1,128)}, f32[8,1,256]{2,1,0:T(1,128)S(1)}, u32[]{:S(2)}) copy-start(f32[8,1,256]{2,1,0:T(1,128)S(1)} %convert_element_type.274) | copy-start | bytes 24580
  34.1 106.7 %copy-start.19 = (f32[8,1,256]{2,1,0:T(1,128)}, f32[8,1,256]{2,1,0:T(1,128)S(1)}, u32[]{:S(2)}) copy-start(f32[8,1,256]{2,1,0:T(1,128)S(1)} %convert_element_type.275) | copy-start | bytes 24580
  42.5 113.0 %copy-start.6 = (f32[4,8,2,512]{3,1,2,0:T(8,128)}, f32[4,8,2,512]{3,1,2,0:T(8,128)S(1)}, u32[]{:S(2)}) copy-start(f32[4,8,2,512]{3,1,2,0:T(8,128)S(1)} %copy.188) | copy-start | bytes 393220
  42.6 112.9 %copy-start.8 = (f32[4,8,2,512]{3,1,2,0:T(8,128)}, f32[4,8,2,512]{3,1,2,0:T(8,128)S(1)}, u32[]{:S(2)}) copy-start(f32[4,8,2,512]{3,1,2,0:T(8,128)S(1)} %copy.189) | copy-start | bytes 393220
  93.1 7.0 copy-start.3
  159.3 11.0 %copy-start.23 = (s32[2]{0:T(128)S(1)}, s32[2]{0:T(128)}, u32[]{:S(2)}) copy-start(s32[2]{0:T(128)} %param.20) | copy-start | bytes 28
  163.8 161.1 %all-gather.21.cloned.1.call-start = ((), (), s32[]{:S(2)}) async-start(), calls=%async_computation.12 | async-start | bytes 5242880 | tf_op jit(solution)/shard_map/all_gather | solution.py:151
  168.7 318.9 %all-gather.27.cloned.1.call-start = ((), (), s32[]{:S(2)}) async-start(), calls=%async_computation.15 | async-start | bytes 9437184 | tf_op jit(solution)/shard_map/all_gather | solution.py:99
  169.4 350.2 %all-gather.29.cloned.1.call-start = ((), (), s32[]{:S(2)}) async-start(), calls=%async_computation.16 | async-start | bytes 9437184 | tf_op jit(solution)/shard_map/all_gather | solution.py:101
  170.2 397.0 %reduce-scatter.16.cloned.1.call-start = ((), (), s32[]{:S(2)}) async-start(), calls=%async_computation.19 | async-start | bytes 5242880 | tf_op jit(solution)/shard_map/reduce_scatter | solution.py:235
  170.4 52.8 %copy-start.12 = (f32[2,512]{1,0:T(2,128)}, f32[2,512]{1,0:T(2,128)S(1)}, u32[]{:S(2)}) copy-start(f32[2,512]{1,0:T(2,128)S(1)} %compare_convert_fusion) | copy-start | bytes 12292
  228.9 29.2 %copy-start.11 = (bf16[1024,2,32]{0,2,1:T(8,128)(2,1)S(1)}, bf16[1024,2,32]{0,2,1:T(8,128)(2,1)}, u32[]{:S(2)}) copy-start(bf16[1024,2,32]{0,2,1:T(8,128)(2,1)} %get-tuple-element.277) | copy-start | bytes 393220
  325.1 6.3 copy-start.1
  342.0 4.0 copy-start.25
  342.0 4.0 copy-start.30
  374.2 6.4 copy-start.1
  390.1 4.1 copy-start.25
  390.1 4.1 copy-start.30
  422.6 9.5 copy-start.24
  422.6 17.7 %copy-start.27 = (bf16[256]{0:T(256)(128)(2,1)S(1)}, bf16[256]{0:T(256)(128)(2,1)}, u32[]{:S(2)}) copy-start(bf16[256]{0:T(256)(128)(2,1)} %param.29) | copy-start | bytes 1540
  422.6 152.6 %reduce-scatter.18.cloned.1.call-start = ((), (), s32[]{:S(2)}) async-start(), calls=%async_computation.20 | async-start | bytes 5242880 | tf_op jit(solution)/shard_map/reduce_scatter | solution.py:238
  423.2 249.0 %reduce-scatter.26.cloned.1.call-start = ((), (), s32[]{:S(2)}) async-start(), calls=%async_computation.24 | async-start | bytes 2359296 | tf_op jit(solution)/shard_map/reduce_scatter | solution.py:325
  449.1 3.2 copy-start.2
  487.5 186.7 %reduce-scatter.14.cloned.1.call-start = ((), (), s32[]{:S(2)}) async-start(), calls=%async_computation.17 | async-start | bytes 5242880 | tf_op jit(solution)/shard_map/reduce_scatter | solution.py:173
  519.6 14.6 %copy-start.10 = (bf16[2,512,2,256]{1,3,2,0:T(8,128)(2,1)S(1)}, bf16[2,512,2,256]{1,3,2,0:T(8,128)(2,1)}, u32[]{:S(2)}) copy-start(bf16[2,512,2,256]{1,3,2,0:T(8,128)(2,1)} %get-tuple-element.95) | copy-start | bytes 3145732
  534.8 8.5 copy-start.9
  543.2 150.4 %reduce-scatter.32.cloned.1.call-start = ((), (), s32[]{:S(2)}) async-start(), calls=%async_computation.27 | async-start | bytes 221184
  562.7 6.2 copy-start.7
  584.7 183.9 %reduce-scatter.28.cloned.1.call-start = ((), (), s32[]{:S(2)}) async-start(), calls=%async_computation.25 | async-start | bytes 9437184 | tf_op jit(solution)/shard_map/reduce_scatter | solution.py:340
  600.0 243.3 %reduce-scatter.30.cloned.1.call-start = ((), (), s32[]{:S(2)}) async-start(), calls=%async_computation.26 | async-start | bytes 9437184 | tf_op jit(solution)/shard_map/reduce_scatter | solution.py:346
  614.1 308.2 %reduce-scatter.22.cloned.1.call-start = ((), (), s32[]{:S(2)}) async-start(), calls=%async_computation.22 | async-start | bytes 5242880 | tf_op jit(solution)/shard_map/reduce_scatter | solution.py:261
  628.3 11.2 %copy-start.18 = (f32[8,1,256]{2,1,0:T(1,128)S(1)}, f32[8,1,256]{2,1,0:T(1,128)}, u32[]{:S(2)}) copy-start(f32[8,1,256]{2,1,0:T(1,128)} %copy-done.17) | copy-start | bytes 24580
  628.3 11.2 %copy-start.20 = (f32[8,1,256]{2,1,0:T(1,128)S(1)}, f32[8,1,256]{2,1,0:T(1,128)}, u32[]{:S(2)}) copy-start(f32[8,1,256]{2,1,0:T(1,128)} %copy-done.19) | copy-start | bytes 24580
  628.4 373.3 %reduce-scatter.20.cloned.1.call-start = ((), (), s32[]{:S(2)}) async-start(), calls=%async_computation.21 | async-start | bytes 5242880 | tf_op jit(solution)/shard_map/reduce_scatter | solution.py:258
  639.4 12.6 %copy-start.31 = (u32[32]{0:T(128)S(1)}, u32[32]{0:T(128)}, u32[]{:S(2)}) copy-start(u32[32]{0:T(128)} %constant.155) | copy-start | bytes 388
  639.5 14.5 %copy-start.28 = (bf16[256]{0:T(256)(128)(2,1)S(1)}, bf16[256]{0:T(256)(128)(2,1)}, u32[]{:S(2)}) copy-start(bf16[256]{0:T(256)(128)(2,1)} %param.27) | copy-start | bytes 1540
  639.5 14.5 %copy-start.29 = (bf16[256]{0:T(256)(128)(2,1)S(1)}, bf16[256]{0:T(256)(128)(2,1)}, u32[]{:S(2)}) copy-start(bf16[256]{0:T(256)(128)(2,1)} %param.33) | copy-start | bytes 1540
  639.5 32.6 %copy-start.21 = (bf16[2048]{0:T(1024)(128)(2,1)S(1)}, bf16[2048]{0:T(1024)(128)(2,1)}, u32[]{:S(2)}) copy-start(bf16[2048]{0:T(1024)(128)(2,1)} %get-tuple-element.299) | copy-start | bytes 12292
  639.5 34.7 %copy-start.13 = (f32[2,512]{1,0:T(2,128)S(1)}, f32[2,512]{1,0:T(2,128)}, u32[]{:S(2)}) copy-start(f32[2,512]{1,0:T(2,128)} %copy-done.12) | copy-start | bytes 12292
  639.5 428.6 %reduce-scatter.24.cloned.1.call-start = ((), (), s32[]{:S(2)}) async-start(), calls=%async_computation.23 | async-start | bytes 7077888 | tf_op jit(solution)/shard_map/reduce_scatter | solution.py:316
  651.9 371.9 %copy-start.16 = (bf16[2048]{0:T(1024)(128)(2,1)S(1)}, bf16[2048]{0:T(1024)(128)(2,1)}, u32[]{:S(2)}) copy-start(bf16[2048]{0:T(1024)(128)(2,1)} %get-tuple-element.267) | copy-start | bytes 12292
  651.9 398.4 %copy-start.15 = (f32[1,4,2,128]{3,1,2,0:T(4,128)S(1)}, f32[1,4,2,128]{3,1,2,0:T(4,128)}, u32[]{:S(2)}) copy-start(f32[1,4,2,128]{3,1,2,0:T(4,128)} %copy-done.14) | copy-start | bytes 12292
  1049.0 22.8 %copy-start.22 = (f32[256]{0:T(256)}, f32[256]{0:T(256)S(1)}, u32[]{:S(2)}) copy-start(f32[256]{0:T(256)S(1)} %get-tuple-element.490) | copy-start | bytes 3076
  (9 other events, 19.1 us)
Sparse Core Ops, SparseCore 0:
  9.6 83.4 all-gather.16
  95.5 45.1 all-gather.18
  142.3 80.7 all-gather.30
  225.5 26.4 all-gather.24
  253.9 34.4 all-gather.22
  290.4 34.4 all-gather.20
  326.8 54.3 all-gather.26
  383.1 54.3 all-gather.28
  440.1 44.5 reduce-scatter.15
  487.2 44.4 reduce-scatter.17
  535.6 41.2 reduce-scatter.25
  579.1 76.7 reduce-scatter.13
  659.5 33.9 reduce-scatter.31
  697.3 71.2 reduce-scatter.27
  771.9 71.2 reduce-scatter.29
  845.5 76.7 reduce-scatter.21
  924.4 77.2 reduce-scatter.19
  1005.3 62.7 reduce-scatter.23
where the time goes:
time: 1090 us; the launch traced here: 1080 us
  waiting for transfers between devices  556 us (51%)
  matrix products  218 us (20%)
  blocking collectives  113 us (10%)
  local copies, waits for them, and re-layouts  91.6 us (8%)
  other arithmetic  82.3 us (8%)
  between operations  16.8 us (2%)
    reduce_scatter x1, waiting for transfers between devices, body(): lax.psum_scatter(first_in_grad.astype(jnp.bfloat16), 'tp', scatter_dimens...  79.4 us
    reduce_scatter x1, waiting for transfers between devices, body(): lax.psum_scatter(second_in_grad.astype(jnp.bfloat16), 'tp', scatter_dimen...  76.3 us
    reduce_scatter x1, waiting for transfers between devices, body(): lax.psum_scatter(inner_weight_grad.astype(jnp.bfloat16), ('fsdp', 'ctx'),...  73.6 us
    reduce_scatter x1, waiting for transfers between devices, body(): lax.psum_scatter(outer_weight_grad.astype(jnp.bfloat16), ('fsdp', 'ctx'),...  71.8 us
    all_gather x1, waiting for transfers between devices, body(): lax.all_gather(tokens, 'tp', axis=2, tiled=True)  50.5 us
    all_gather x1, waiting for transfers between devices, body(): lax.all_gather(cotangent, 'tp', axis=2, tiled=True)  49.4 us
    dynamic_update_slice x4, local copies, waits for them, and re-layouts, body(): lax.map(backward_one, (query_seq, key_all, value_all, allowed, context_gr...  41.5 us
    all_gather x1, waiting for transfers between devices, body(): lax.all_gather(joined_weight, ('fsdp', 'ctx'), axis=0, tiled=True)  36.5 us
  transfers between devices with their start and end apart: 18, of which 12 were waited for; matrix products, arithmetic and copies ran while one was open for 36% of the time, Pallas kernels for 0%

commit v1 on v0

v1 whole, which is shorter than its diff:
```python
import functools

import jax
import jax.numpy as jnp
from jax import lax
from jax.experimental import pallas as pl
from jax.experimental.pallas import tpu as pltpu
from jax.sharding import PartitionSpec as P

HEAD = 256
ROTARY = 64
F32 = jnp.float32
BF16 = jnp.bfloat16
VMEM_LIMIT = 56 << 20
NN = (((1,), (0,)), ((), ()))
NT = (((1,), (1,)), ((), ()))
TN = (((0,), (0,)), ((), ()))


def dot(a, b, dims):
    return lax.dot_general(a, b, dims, preferred_element_type=F32)


def params(*semantics):
    return pltpu.CompilerParams(
        dimension_semantics=semantics or None, vmem_limit_bytes=VMEM_LIMIT
    )


def cost(flops, moved, transcendentals=0):
    return pl.CostEstimate(flops=flops, bytes_accessed=moved, transcendentals=transcendentals)


def line_gather(piece, axis):
    size = lax.axis_size(axis)
    up = [(i, i + 1) for i in range(size - 1)]
    down = [(i + 1, i) for i in range(size - 1)]
    right, left = [], []
    a = b = piece
    for _ in range(size - 1):
        a = lax.ppermute(a, axis, up)
        b = lax.ppermute(b, axis, down)
        right.append(a)
        left.append(b)
    return [(right[s - 1], left[size - s - 1]) for s in range(1, size)]


def norm_kernel(size, me_ref, own, *refs):
    pairs = refs[: 2 * (size - 1)]
    gains, first_out, second_out, token_out, stat_out, work = refs[2 * (size - 1) :]
    part = own.shape[1]
    me = me_ref[0]
    for s in range(size):
        if s == 0:
            piece = own[...].astype(F32)
        else:
            piece = pairs[2 * s - 2][...].astype(F32) + pairs[2 * s - 1][...].astype(F32)
        at = lax.rem(me - s + size, size)
        work[:, pl.ds(pl.multiple_of(at * part, part), part)] = piece
    rows = work[...]
    token_out[...] = rows.astype(BF16)
    width = rows.shape[1]
    center = jnp.sum(rows, axis=1, keepdims=True) * (1.0 / width)
    shifted = rows - center
    inverse = lax.rsqrt(jnp.sum(shifted * shifted, axis=1, keepdims=True) * (1.0 / width) + 1e-05)
    normed = shifted * inverse
    first_out[...] = (normed * gains[0:1, :] + gains[1:2, :]).astype(BF16)
    second_out[...] = (normed * gains[2:3, :] + gains[3:4, :]).astype(BF16)
    lane = lax.broadcasted_iota(jnp.int32, stat_out.shape, 1)
    stat_out[...] = jnp.where(lane == 0, center, inverse)


def norm_call(me, own, pairs, gains, tile=128):
    count, part = own.shape
    size = len(pairs) + 1
    width = part * size
    flat = [p for pair in pairs for p in pair]
    block = pl.BlockSpec((tile, part), lambda i, *_: (i, 0))
    wide = pl.BlockSpec((tile, width), lambda i, *_: (i, 0))
    return pl.pallas_call(
        functools.partial(norm_kernel, size),
        grid_spec=pltpu.PrefetchScalarGridSpec(
            num_scalar_prefetch=1,
            grid=(count // tile,),
            in_specs=[block] * (1 + len(flat)) + [pl.BlockSpec((4, width), lambda i, *_: (0, 0))],
            out_specs=[wide, wide, wide, pl.BlockSpec((tile, 128), lambda i, *_: (i, 0))],
            scratch_shapes=[pltpu.VMEM((tile, width), F32)],
        ),
        out_shape=[
            jax.ShapeDtypeStruct((count, width), BF16),
            jax.ShapeDtypeStruct((count, width), BF16),
            jax.ShapeDtypeStruct((count, width), BF16),
            jax.ShapeDtypeStruct((count, 128), F32),
        ],
        compiler_params=params("arbitrary"),
        cost_estimate=cost(count * width * 16, count * width * 10),
        name="norm",
    )(me, own, *flat, gains)


def cot_kernel(size, local_len, tile, me_ref, len_ref, own, *refs):
    pairs = refs[: 2 * (size - 1)]
    rows_out, sum_out = refs[2 * (size - 1) :]
    part = own.shape[1]
    me, ctx = me_ref[0], me_ref[1]
    step = pl.program_id(0)
    start = step * tile
    seq = start // local_len
    length = len_ref[seq]
    position = ctx * local_len + lax.rem(start, local_len)
    position = position + lax.broadcasted_iota(jnp.int32, (tile, 1), 0)
    keep = position < length

    @pl.when(step == 0)
    def _():
        sum_out[...] = jnp.zeros_like(sum_out)

    for s in range(size):
        if s == 0:
            piece = own[...].astype(F32)
        else:
            piece = pairs[2 * s - 2][...].astype(F32) + pairs[2 * s - 1][...].astype(F32)
        piece = jnp.where(keep, piece, 0.0)
        at = lax.rem(me - s + size, size)
        cols = pl.ds(pl.multiple_of(at * part, part), part)
        rows_out[:, cols] = piece.astype(BF16)
        sum_out[0:1, cols] += jnp.sum(piece, axis=0, keepdims=True)


def cot_call(places, lengths, own, pairs, local_len, tile=256):
    count, part = own.shape
    size = len(pairs) + 1
    width = part * size
    flat = [p for pair in pairs for p in pair]
    block = pl.BlockSpec((tile, part), lambda i, *_: (i, 0))
    return pl.pallas_call(
        functools.partial(cot_kernel, size, local_len, tile),
        grid_spec=pltpu.PrefetchScalarGridSpec(
            num_scalar_prefetch=2,
            grid=(count // tile,),
            in_specs=[block] * (1 + len(flat)),
            out_specs=[
                pl.BlockSpec((tile, width), lambda i, *_: (i, 0)),
                pl.BlockSpec((8, width), lambda i, *_: (0, 0)),
            ],
        ),
        out_shape=[
            jax.ShapeDtypeStruct((count, width), BF16),
            jax.ShapeDtypeStruct((8, width), F32),
        ],
        compiler_params=params("arbitrary"),
        cost_estimate=cost(count * width * 4, count * width * 6),
        name="cotangent_rows",
    )(places, lengths, own, *flat)


def joined_kernel(seqs, rows_ref, weight_ref, bias_ref, table_ref, query_ref, pair_ref):
    kind = lax.rem(pl.program_id(0), 3)
    out = dot(rows_ref[...], weight_ref[...], NN) + bias_ref[0:1, :]

    def turned():
        front = out[:, :128]
        up = pltpu.roll(front, 128 - ROTARY // 2, 1)
        down = pltpu.roll(front, ROTARY // 2, 1)
        table = table_ref[...]
        if seqs > 1:
            table = jnp.concatenate([table] * seqs, axis=0)
        front = front * table[:, :128] + up * table[:, 128:256] + down * table[:, 256:]
        return jnp.concatenate([front, out[:, 128:]], axis=1)

    @pl.when(kind == 0)
    def _():
        query_ref[...] = (turned().astype(BF16).astype(F32) * HEAD ** (-0.5)).astype(BF16)

    @pl.when(kind == 1)
    def _():
        pair_ref[...] = turned().astype(BF16)

    @pl.when(kind == 2)
    def _():
        pair_ref[...] = out.astype(BF16)


def joined_call(rows, weight, bias, table, seqs, heads):
    count, width = rows.shape
    return pl.pallas_call(
        functools.partial(joined_kernel, seqs),
        grid=(3 * heads,),
        in_specs=[
            pl.BlockSpec((count, width), lambda j: (0, 0)),
            pl.BlockSpec((width, HEAD), lambda j: (0, j)),
            pl.BlockSpec((8, HEAD), lambda j: (0, j)),
            pl.BlockSpec(table.shape, lambda j: (0, 0)),
        ],
        out_specs=[
            pl.BlockSpec((count, HEAD), lambda j: (0, j // 3)),
            pl.BlockSpec((count, HEAD), lambda j: (0, 2 * (j // 3) + (j % 3) // 2)),
        ],
        out_shape=[
            jax.ShapeDtypeStruct((count, heads * HEAD), BF16),
            jax.ShapeDtypeStruct((count, 2 * heads * HEAD), BF16),
        ],
        compiler_params=params("arbitrary"),
        cost_estimate=cost(6 * heads * HEAD * count * width, 2 * (count + 3 * heads * HEAD) * width),
        name="joined",
    )(rows, weight, jnp.broadcast_to(bias.reshape(1, -1), (8, bias.size)), table)


def visit(slot, local_len, half, block, place, length):
    first_key = block * local_len
    last_query = place * local_len + (half + 1) * (local_len // 2) - 1
    return (block >= 0) & (first_key <= last_query) & (first_key < length)


def masked(scores, first_key, first_query, length, axis_key):
    shape = scores.shape
    key = first_key + lax.broadcasted_iota(jnp.int32, shape, axis_key)
    query = first_query + lax.broadcasted_iota(jnp.int32, shape, 1 - axis_key)
    return (key <= query) & (key < length)


def forward_kernel(slots, local_len, info, lens, query_ref, *refs):
    pair_refs = refs[:slots]
    context_ref, lse_ref, top, total, acc = refs[slots:]
    seq = pl.program_id(0)
    length = lens[seq]
    place = info[slots]
    top[...] = jnp.full_like(top, -1e30)
    total[...] = jnp.zeros_like(total)
    acc[...] = jnp.zeros_like(acc)
    query = query_ref[...]
    for slot in range(slots):
        block = info[slot]
        first_key = block * local_len

        @pl.when((block >= 0) & (block <= place) & (first_key < length))
        def _():
            keys = pair_refs[slot][:, :HEAD]
            vals = pair_refs[slot][:, HEAD:]
            scores = dot(query, keys, NT)
            ok = masked(scores, first_key, place * local_len, length, 1)
            scores = jnp.where(ok, scores, -1e30)
            best = jnp.maximum(top[...], jnp.max(scores, axis=1, keepdims=True))
            scale = jnp.exp(top[...] - best)
            weights = jnp.exp(scores - best[:, :1])
            weights = jnp.where(ok, weights, 0.0)
            total[...] = total[...] * scale + jnp.sum(weights, axis=1, keepdims=True)
            acc[...] = acc[...] * scale[:, :1] + dot(weights.astype(BF16), vals, NN)
            top[...] = best

    context_ref[...] = (acc[...] / total[:, :1]).astype(BF16)
    lse_ref[...] = top[...] + jnp.log(total[...])


def forward_call(info, lengths, query, pairs, seqs, heads):
    count = query.shape[0]
    local_len = count // seqs
    slots = len(pairs)
    return pl.pallas_call(
        functools.partial(forward_kernel, slots, local_len),
        grid_spec=pltpu.PrefetchScalarGridSpec(
            num_scalar_prefetch=2,
            grid=(seqs, heads),
            in_specs=[pl.BlockSpec((local_len, HEAD), lambda s, h, *_: (s, h))]
            + [pl.BlockSpec((local_len, 2 * HEAD), lambda s, h, *_: (s, h))] * slots,
            out_specs=[
                pl.BlockSpec((local_len, HEAD), lambda s, h, *_: (s, h)),
                pl.BlockSpec((local_len, 128), lambda s, h, *_: (s, h)),
            ],
            scratch_shapes=[
                pltpu.VMEM((local_len, 128), F32),
                pltpu.VMEM((local_len, 128), F32),
                pltpu.VMEM((local_len, HEAD), F32),
            ],
        ),
        out_shape=[
            jax.ShapeDtypeStruct((count, heads * HEAD), BF16),
            jax.ShapeDtypeStruct((count, heads * 128), F32),
        ],
        compiler_params=params("arbitrary", "arbitrary"),
        cost_estimate=cost(
            4 * count * heads * HEAD * local_len * slots,
            4 * count * heads * HEAD * slots,
            count * heads * local_len * slots,
        ),
        name="attention_forward",
    )(info, lengths, query, *pairs)


def backward_kernel(slots, local_len, info, lens, query_ref, context_ref, grad_ref, lse_ref, *refs):
    pair_refs = refs[:slots]
    query_out = refs[slots]
    pair_outs = refs[slots + 1 : 2 * slots + 1]
    acc = refs[2 * slots + 1]
    seq = pl.program_id(0)
    length = lens[seq]
    place = info[slots]
    query = query_ref[...]
    grad = grad_ref[...]
    lse = lse_ref[:, :1]
    shared = jnp.sum(grad.astype(F32) * context_ref[...].astype(F32), axis=1, keepdims=True)
    acc[...] = jnp.zeros_like(acc)
    for slot in range(slots):
        block = info[slot]
        first_key = block * local_len
        seen = (block >= 0) & (block <= place) & (first_key < length)

        @pl.when(seen)
        def _():
            keys = pair_refs[slot][:, :HEAD]
            vals = pair_refs[slot][:, HEAD:]
            scores = dot(query, keys, NT)
            ok = masked(scores, first_key, place * local_len, length, 1)
            probs = jnp.where(ok, jnp.exp(scores - lse), 0.0)
            prob_grad = dot(grad, vals, NT)
            score_grad = (probs * (prob_grad - shared)).astype(BF16)
            acc[...] += dot(score_grad, keys, NN)
            pair_outs[slot][:, :HEAD] = dot(score_grad, query, TN).astype(BF16)
            pair_outs[slot][:, HEAD:] = dot(probs.astype(BF16), grad, TN).astype(BF16)

        @pl.when(jnp.logical_not(seen))
        def _():
            pair_outs[slot][...] = jnp.zeros_like(pair_outs[slot])

    query_out[...] = (acc[...] * HEAD ** (-0.5)).astype(BF16)


def backward_call(info, lengths, query, context, grad, lse, pairs, seqs, heads):
    count = query.shape[0]
    local_len = count // seqs
    slots = len(pairs)
    one = pl.BlockSpec((local_len, HEAD), lambda s, h, *_: (s, h))
    two = pl.BlockSpec((local_len, 2 * HEAD), lambda s, h, *_: (s, h))
    return pl.pallas_call(
        functools.partial(backward_kernel, slots, local_len),
        grid_spec=pltpu.PrefetchScalarGridSpec(
            num_scalar_prefetch=2,
            grid=(seqs, heads),
            in_specs=[one, one, one, pl.BlockSpec((local_len, 128), lambda s, h, *_: (s, h))]
            + [two] * slots,
            out_specs=[one] + [two] * slots,
            scratch_shapes=[pltpu.VMEM((local_len, HEAD), F32)],
        ),
        out_shape=[jax.ShapeDtypeStruct((count, heads * HEAD), BF16)]
        + [jax.ShapeDtypeStruct((count, 2 * heads * HEAD), BF16)] * slots,
        compiler_params=params("arbitrary", "arbitrary"),
        cost_estimate=cost(
            10 * count * heads * HEAD * local_len * slots,
            8 * count * heads * HEAD * slots,
            count * heads * local_len * slots,
        ),
        name="attention_backward",
    )(info, lengths, query, context, grad, lse, *pairs)


def share_pairs(own, axis):
    swap = [(0, 1), (1, 0), (2, 3), (3, 2)]
    sibling = lax.ppermute(own, axis, swap)
    below = lax.ppermute(own, axis, [(0, 2), (1, 3)])
    below_sibling = lax.ppermute(below, axis, [(2, 3), (3, 2)])
    return [own, sibling, below, below_sibling]


def return_pairs(grads, axis):
    own, sibling, below, below_sibling = grads
    from_sibling = lax.ppermute(sibling, axis, [(1, 0), (3, 2)])
    crossed = lax.ppermute(below_sibling, axis, [(2, 3), (3, 2)])
    lower = (below.astype(F32) + crossed.astype(F32)).astype(BF16)
    above = lax.ppermute(lower, axis, [(2, 0), (3, 1)])
    return [own, from_sibling, above]


def gelu_parts(upper):
    phi = 0.5 * (1.0 + lax.erf(upper * 0.7071067811865476))
    slope = phi + upper * jnp.exp(-0.5 * upper * upper) * 0.3989422804014327
    return upper * phi, slope


def body(
    tokens,
    lengths,
    cotangent,
    first_gain,
    first_shift,
    joined_weight,
    joined_bias,
    output_weight,
    output_bias,
    second_gain,
    second_shift,
    inner_weight,
    inner_bias,
    outer_weight,
    outer_bias,
):
    group = ("fsdp", "ctx")
    seqs, local_len, part = tokens.shape
    count = seqs * local_len
    ranks = lax.axis_size("tp")
    width = part * ranks
    shards = lax.axis_size("fsdp") * lax.axis_size("ctx")
    rows_part = width // shards
    heads = joined_weight.shape[1]
    hidden = inner_weight.shape[1]
    me, ctx = lax.axis_index("tp"), lax.axis_index("ctx")

    pack_a = jnp.concatenate([joined_weight.reshape(rows_part, -1), inner_weight], axis=1)
    pack_b = jnp.concatenate([output_weight.reshape(rows_part, -1), outer_weight], axis=1)
    whole_a = lax.all_gather(pack_a, group, axis=0, tiled=True)
    whole_b = lax.all_gather(pack_b, group, axis=0, tiled=True)
    joined_width = heads * 3 * HEAD
    inner = whole_a[:, joined_width:]
    output = whole_b[:, : heads * HEAD]
    outer = whole_b[:, heads * HEAD :]

    own_tokens = tokens.reshape(count, part)
    own_cot = cotangent.reshape(count, part)
    token_pairs = line_gather(own_tokens, "tp")
    own_cot_late, _ = lax.optimization_barrier((own_cot, token_pairs))
    cot_pairs = line_gather(own_cot_late, "tp")

    vectors = [first_gain, first_shift, second_gain, second_shift, output_bias, outer_bias]
    flat = jnp.concatenate(vectors + [joined_bias.reshape(-1), inner_bias.reshape(-1)])
    small = lax.all_gather(flat, group, axis=0, tiled=False).reshape(shards, -1).astype(F32)
    whole = [small[:, i * rows_part : (i + 1) * rows_part].reshape(width) for i in range(6)]
    at = 6 * rows_part
    whole_joined_bias = (
        small[:, at : at + joined_bias.size]
        .reshape((shards,) + joined_bias.shape)
        .transpose(1, 0, 2)
        .reshape(-1)
    )
    at += joined_bias.size
    whole_inner_bias = (
        small[:, at:].reshape((shards,) + inner_bias.shape).transpose(1, 0, 2).reshape(-1)
    )
    gains = jnp.stack(whole[:4])

    places = jnp.stack([me, ctx]).astype(jnp.int32)
    first_in, second_in, rows, stats = norm_call(places[:1], own_tokens, token_pairs, gains)
    center, inverse = stats[:, 0:1], stats[:, 1:2]
    positions = ctx * local_len + jnp.arange(local_len, dtype=jnp.int32)
    half = ROTARY // 2
    frequency = 1.0 / 10000.0 ** (jnp.arange(half, dtype=F32) * 2.0 / ROTARY)
    angles = positions.astype(F32)[:, None] * frequency[None, :]
    cosine, sine = jnp.cos(angles), jnp.sin(angles)
    ones = jnp.ones((local_len, 128 - ROTARY), F32)
    nothing = jnp.zeros((local_len, half), F32)
    blank = jnp.zeros((local_len, 128 - ROTARY), F32)
    table = jnp.concatenate(
        [cosine, cosine, ones, -sine, nothing, blank, nothing, sine, blank], axis=1
    )
    query, pair = joined_call(first_in, whole_a, whole_joined_bias, table, seqs, heads)
    pairs = share_pairs(pair, "ctx")
    low, odd = ctx - 2, ctx + 1 - 2 * lax.rem(ctx, 2)
    info = jnp.stack([ctx, odd, low, jnp.where(low >= 0, odd - 2, -1), ctx]).astype(jnp.int32)
    upper = dot(second_in, inner, NN) + whole_inner_bias
    active, slope = gelu_parts(upper)
    active = active.astype(BF16)
    context, lse = forward_call(info, lengths, query, pairs, seqs, heads)
    branch = dot(active, outer, NT) + dot(context, output, NT)
    summed = lax.psum_scatter(
        branch.astype(BF16), "tp", scatter_dimension=1, tiled=True
    ).astype(F32)
    own_start = me * part
    own_bias = lax.dynamic_slice_in_dim(whole[4] + whole[5], own_start, part)
    valid = (positions[None, :] < lengths[:, None]).astype(F32).reshape(count, 1)
    layer_out = (valid * (own_tokens.astype(F32) + summed + own_bias)).astype(BF16)

    grad_rows, bias_sums = cot_call(places, lengths, own_cot_late, cot_pairs, local_len)
    bias_grad = bias_sums[0]
    context_grad = dot(grad_rows, output, NN).astype(BF16)
    upper_grad = (dot(grad_rows, outer, NN) * slope).astype(BF16)
    outer_grad = dot(grad_rows, active, TN).astype(BF16)
    inner_grad = dot(second_in, upper_grad, TN).astype(BF16)
    output_grad = dot(grad_rows, context, TN).astype(BF16)
    inner_bias_grad = jnp.sum(upper_grad, axis=0, dtype=F32)
    second_in_grad = dot(upper_grad, inner, NT)
    query_grad, *pair_grads = backward_call(
        info, lengths, query, context, context_grad, lse, pairs, seqs, heads
    )
    sums = return_pairs(pair_grads, "ctx")
    pair_grad = sum(p.astype(F32) for p in sums).reshape(count, heads, 2, HEAD)
    cos_rows = jnp.tile(cosine, (seqs, 1))[:, None, :]
    sin_rows = jnp.tile(sine, (seqs, 1))[:, None, :]

    def turn_back(v):
        front, back = v[..., :half], v[..., half : 2 * half]
        return jnp.concatenate(
            [
                front * cos_rows + back * sin_rows,
                back * cos_rows - front * sin_rows,
                v[..., 2 * half :],
            ],
            axis=-1,
        )

    joined_grad = (
        jnp.stack(
            [
                turn_back(query_grad.astype(F32).reshape(count, heads, HEAD)),
                turn_back(pair_grad[:, :, 0]),
                pair_grad[:, :, 1],
            ],
            axis=2,
        )
        .astype(BF16)
        .reshape(count, joined_width)
    )
    joined_bias_grad = jnp.sum(joined_grad, axis=0, dtype=F32)
    first_in_grad = dot(joined_grad, whole_a[:, :joined_width], NT)
    joined_grad_weight = dot(first_in, joined_grad, TN).astype(BF16)

    normed = (rows.astype(F32) - center) * inverse
    column = jnp.stack(
        [
            jnp.sum(first_in_grad * normed, axis=0),
            jnp.sum(first_in_grad, axis=0),
            jnp.sum(second_in_grad * normed, axis=0),
            jnp.sum(second_in_grad, axis=0),
        ]
    )
    scaled = first_in_grad * whole[0] + second_in_grad * whole[2]
    row_terms = jnp.stack([jnp.sum(scaled, axis=1), jnp.sum(scaled * normed, axis=1)])
    share = lax.psum_scatter(scaled.astype(BF16), "tp", scatter_dimension=1, tiled=True)
    means = lax.psum(row_terms, "tp") / width
    own_normed = (own_tokens.astype(F32) - center) * inverse
    own_rows = lax.dynamic_slice_in_dim(grad_rows, own_start, part, 1).astype(F32)
    tokens_grad = own_rows + inverse * (
        share.astype(F32) - means[0][:, None] - own_normed * means[1][:, None]
    )

    def scatter(v):
        return lax.psum_scatter(v, group, scatter_dimension=0, tiled=True).astype(F32)

    outer_out = scatter(outer_grad)
    inner_out = scatter(inner_grad)
    output_out = scatter(output_grad)
    joined_out = scatter(joined_grad_weight)
    column = lax.psum(column, "tp")
    small_grads = jnp.concatenate(
        [column.reshape(-1), bias_grad, joined_bias_grad, inner_bias_grad]
    )
    small_sums = lax.psum(small_grads, group)
    place = lax.axis_index("fsdp") * lax.axis_size("ctx") + ctx
    vector = lax.dynamic_slice_in_dim(
        small_sums[: 5 * width].reshape(5, width), place * rows_part, rows_part, 1
    )
    joined_bias_out = lax.dynamic_slice_in_dim(
        small_sums[5 * width : 5 * width + joined_width].reshape(heads, 3 * HEAD),
        place * joined_bias.shape[1],
        joined_bias.shape[1],
        1,
    )
    inner_bias_out = lax.dynamic_slice_in_dim(
        small_sums[5 * width + joined_width :].reshape(inner_bias.shape[0], -1),
        place * inner_bias.shape[1],
        inner_bias.shape[1],
        1,
    )
    return (
        layer_out.reshape(tokens.shape),
        tokens_grad.reshape(tokens.shape),
        vector[0],
        vector[1],
        joined_out.reshape(joined_weight.shape),
        joined_bias_out,
        output_out.reshape(output_weight.shape),
        vector[4],
        vector[2],
        vector[3],
        inner_out,
        inner_bias_out,
        outer_out,
        vector[4],
    )


def solution(mesh):
    both = ("fsdp", "ctx")
    return jax.shard_map(
        body,
        mesh=mesh,
        in_specs=(
            P("fsdp", "ctx", "tp"),
            P("fsdp"),
            P("fsdp", "ctx", "tp"),
            P(both),
            P(both),
            P(both, "tp", None),
            P("tp", both),
            P(both, "tp", None),
            P(both),
            P(both),
            P(both),
            P(both, "tp"),
            P("tp", both),
            P(both, "tp"),
            P(both),
        ),
        out_specs=(
            P("fsdp", "ctx", "tp"),
            P("fsdp", "ctx", "tp"),
            P(both),
            P(both),
            P(both, "tp", None),
            P("tp", both),
            P(both, "tp", None),
            P(both),
            P(both),
            P(both),
            P(both, "tp"),
            P("tp", both),
            P(both, "tp"),
            P(both),
        ),
        check_vma=False,
    )
```

time: 1090 us -> 707 us (0.65)
  waiting for transfers between devices: 556 us -> 299 us
  matrix products: 218 us -> 122 us
  Pallas kernels: 0 us -> 55.6 us
  starting transfers between devices: 1.25 us -> 51.1 us
  local copies, waits for them, and re-layouts: 91.6 us -> 45.3 us
  other arithmetic: 82.3 us -> 37.9 us
  blocking collectives: 113 us -> 71.3 us
    all_gather x8 -> x2, waiting for transfers between devices: 221 us -> 0.04 us  [the longest x1 0.02 us: body(): whole_a = lax.all_gather(pack_a, group, axis=0, tiled=True)]
    reduce_scatter x9 -> x6, waiting for transfers between devices: 315 us -> 145 us  [the longest x1 79.5 us: body(): lax.psum_scatter(scaled.astype(BF16), 'tp', scatter_dimension=1, tiled=True)]
    ppermute x0 -> x18, waiting for transfers between devices: none -> 154 us  [the longest x1 63.5 us: return_pairs(): above = lax.ppermute(lower, axis, [(2, 0), (3, 1)])]
    dot_general x26 -> x11, matrix products: 218 us -> 122 us  [dot(): return lax.dot_general(a, b, dims, preferred_element_type=F32)]
    all_gather x8 -> x0, blocking collectives: 70.7 us -> none  [the longest x1 10.3 us: body(): lax.all_gather(first_gain, ('fsdp', 'ctx'), axis=0, tiled=True)]
    pallas_call x0 -> x5, Pallas kernels: none -> 55.6 us  [the longest x1 13.5 us: joined_call(): pl.pallas_call(functools.partial(joined_kernel, seqs), grid=(3 * heads,),...]
    ppermute x0 -> x18, starting transfers between devices: none -> 50.2 us  [the longest x6 32.5 us: line_gather(): a = lax.ppermute(a, axis, up)]
    dynamic_update_slice x4 -> x0, local copies, waits for them, and re-layouts: 41.5 us -> none  [body(): lax.map(backward_one, (query_seq, key_all, value_all, allowed, context_gr...]
  transfers between devices with their start and end apart: 18 -> 26, of which waited for: 12 -> 8; matrix products, arithmetic and copies ran while one was open for 36% -> 28% of each run, Pallas kernels for 0% -> 8%
where the time goes in v1:
time: 707 us; the launch traced here: 699 us
  waiting for transfers between devices  299 us (42%)
  matrix products  122 us (17%)
  blocking collectives  71.3 us (10%)
  Pallas kernels  55.6 us (8%)
  starting transfers between devices  51.1 us (7%)
  local copies, waits for them, and re-layouts  45.3 us (6%)
  other arithmetic  37.9 us (5%)
  between operations  16.2 us (2%)
    dot_general x11, matrix products, dot(): return lax.dot_general(a, b, dims, preferred_element_type=F32)  122 us
    reduce_scatter x1, waiting for transfers between devices, body(): lax.psum_scatter(scaled.astype(BF16), 'tp', scatter_dimension=1, tiled=True)  79.5 us
    ppermute x1, waiting for transfers between devices, return_pairs(): above = lax.ppermute(lower, axis, [(2, 0), (3, 1)])  63.5 us
    reduce_scatter x4, waiting for transfers between devices, scatter(): lax.psum_scatter(v, group, scatter_dimension=0, tiled=True).astype(F32)  62.4 us
    ppermute x6, waiting for transfers between devices, line_gather(): b = lax.ppermute(b, axis, down)  61.2 us
    ppermute x6, starting transfers between devices, line_gather(): a = lax.ppermute(a, axis, up)  32.5 us
    ppermute x1, waiting for transfers between devices, share_pairs(): below = lax.ppermute(own, axis, [(0, 2), (1, 3)])  29.6 us
    psum x1, blocking collectives, body(): small_sums = lax.psum(small_grads, group)  24.6 us
  transfers between devices with their start and end apart: 26, of which 8 were waited for; matrix products, arithmetic and copies ran while one was open for 28% of the time, Pallas kernels for 8%

profile of v1, /device:TPU:0, one launch (start us, length us, event | category | flops | bytes accessed | tf_op | source)
XLA Modules:
  0.0 698.5 jit_solution(15049760972472944405)
XLA Ops:
  8.7 2.6 pad_maximum_fusion
  14.0 5.6 collective-permute-start
  19.6 21.2 %collective-permute-done.1.refs_5_ = bf16[1024,512]{1,0:T(8,128)(2,1)S(1)} collective-permute-done((bf16[1024,512]{1,0:T(8,128)(2,1)S(1)}, bf16[1024,512]{1,0:T(8,128)(2,1)S(1)}, u32[]{:S(2)}, u32[]{:S(2)}) %collective-permute-start.1) | collective-permute-done | bytes 1048608 | tf_op jit(solution)/shard_map/ppermute | solution.py:42
  42.1 5.5 collective-permute-start.4
  47.6 19.6 %collective-permute-done.2.refs_3_ = bf16[1024,512]{1,0:T(8,128)(2,1)} collective-permute-done((bf16[1024,512]{1,0:T(8,128)(2,1)S(1)}, bf16[1024,512]{1,0:T(8,128)(2,1)}, u32[]{:S(2)}, u32[]{:S(2)}) %collective-permute-start.2) | collective-permute-done | bytes 1048608 | tf_op jit(solution)/shard_map/ppermute | solution.py:42
  68.5 5.6 collective-permute-start.5
  76.1 23.0 %all-reduce = bf16[15872]{0:T(1024)(128)(2,1)S(1)} all-reduce(bf16[15872]{0:T(1024)(128)(2,1)S(1)} %dynamic-update-slice), channel_id=2, replica_groups=mesh['fsdp'=2,'ctx'=4,'tp'=4] {'fsdp','ctx'}, use_global_device_ids=true, to_apply=%add | all-reduce | flops 15872 | bytes 63488
  102.1 5.6 collective-permute-start.9
  110.6 11.6 %norm.1 = (bf16[1024,2048]{1,0:T(8,128)(2,1)}, bf16[1024,2048]{1,0:T(8,128)(2,1)}, bf16[1024,2048]{1,0:T(8,128)(2,1)}, f32[1024,128]{1,0:T(8,128)}) custom-call(s32[1]{0:T(128)} %bitcast.1.me_ref, bf16[1024,512]{1,0:T(8,128)(2,1)} %bitcast.101, bf16[1024,512]{1,0:T(8,128)(2,1)} %copy-done.14, bf16[1024,512]{1,0:T(8,128)(2,1)} %collective-permute-done.3.refs_1_, ...), custom_call_target="tpu_custom_call" | custom-call | flops 33554432 | bytes 20971520 | tf_op jit(solution)/shard_map/norm/pallas_call | solution.py:80
  122.9 13.5 %joined.1 = (bf16[1024,512]{1,0:T(8,128)(2,1)}, bf16[1024,1024]{1,0:T(8,128)(2,1)}) custom-call(bf16[1024,2048]{1,0:T(8,128)(2,1)} %get-tuple-element.31.rows_ref, bf16[2048,3584]{1,0:T(8,128)(2,1)} %all-gather.4.cloned.1.call-done.weight_ref, f32[8,1536]{1,0:T(8,128)} %broadcast_in_dim.22.bias_ref, f32[512,384]{1,0:T(8,128)} %concatenate.24.table_ref), custom_call_target="tpu_custom_call" | custom-call | flops 6442450944 | bytes 10485760 | tf_op jit(solution)/shard_map/joined/pallas_call | solution.py:186
  136.4 2.7 collective-permute-start.7
  140.4 4.6 collective-permute-start.13
  145.0 20.5 %collective-permute-done.11.refs_3_ = bf16[1024,512]{1,0:T(8,128)(2,1)S(1)} collective-permute-done((bf16[1024,512]{1,0:T(8,128)(2,1)}, bf16[1024,512]{1,0:T(8,128)(2,1)S(1)}, u32[]{:S(2)}, u32[]{:S(2)}) %collective-permute-start.11) | collective-permute-done | bytes 1048608 | tf_op jit(solution)/shard_map/ppermute | solution.py:42
  166.7 5.6 collective-permute-start.14
  172.3 29.6 %collective-permute-done.7.refs_2_ = bf16[1024,1024]{1,0:T(8,128)(2,1)} collective-permute-done((bf16[1024,1024]{1,0:T(8,128)(2,1)}, bf16[1024,1024]{1,0:T(8,128)(2,1)}, u32[]{:S(2)}, u32[]{:S(2)}) %collective-permute-start.7) | collective-permute-done | bytes 2097184 | tf_op jit(solution)/shard_map/ppermute | solution.py:359
  201.9 2.2 collective-permute-start.8
  206.0 7.7 %cotangent_rows.1 = (bf16[1024,2048]{1,0:T(8,128)(2,1)}, f32[8,2048]{1,0:T(8,128)}) custom-call(s32[2]{0:T(128)} %pad_add_fusion.me_ref, s32[2]{0:T(128)} %lens.3, bf16[1024,512]{1,0:T(8,128)(2,1)} %bitcast.109, bf16[1024,512]{1,0:T(8,128)(2,1)} %collective-permute-done.9.refs_0_, bf16[1024,512]{1,0:T(8,128)(2,1)} %collective-permute-done.12.refs_1_, ...), custom_call_target="tpu_custom_call" | custom-call | flops 8388608 | bytes 12582912 | tf_op jit(solution)/shard_map/cotangent_rows/pallas_call | solution.py:136
  213.7 14.4 %multiply_convert_fusion = (bf16[1024,2048]{1,0:T(8,128)(2,1)}, f32[1024,2048]{1,0:T(8,128)}) fusion(f32[2048]{0:T(1024)S(1)} %add.115, bf16[1024,2048]{1,0:T(8,128)(2,1)S(1)} %copy-done.29, bf16[2048,3584]{1,0:T(8,128)(2,1)} %all-gather.4.cloned.1.call-done.weight_ref), kind=kOutput, calls=%fused_computation.14 | convolution fusion | flops 8602517504 | bytes 25174016 | tf_op jit(solution)/shard_map/dot_general | solution.py:21
  228.2 10.6 %attention_forward.1 = (bf16[1024,512]{1,0:T(8,128)(2,1)}, f32[1024,256]{1,0:T(8,128)}) custom-call(s32[5]{0:T(128)} %stack.65.info, s32[2]{0:T(128)} %lens.3, bf16[1024,512]{1,0:T(8,128)(2,1)} %get-tuple-element.32.query_ref, bf16[1024,1024]{1,0:T(8,128)(2,1)} %get-tuple-element.33.refs_0_, bf16[1024,1024]{1,0:T(8,128)(2,1)} %collective-permute-done.6.refs_1_, ...), custom_call_target="tpu_custom_call" | custom-call | flops 4294967296 | bytes 8388608 | tf_op jit(solution)/shard_map/attention_forward/pallas_call | solution.py:259
  238.7 5.0 convolution_convert_fusion.3
  244.0 16.9 %convert_reduce_fusion = (f32[2048]{0:T(1024)}, bf16[1024,2048]{1,0:T(8,128)(2,1)S(1)}) fusion(f32[1024,2048]{1,0:T(8,128)} %get-tuple-element.132, f32[2048]{0:T(1024)S(1)} %add.115, bf16[1024,2048]{1,0:T(8,128)(2,1)} %get-tuple-element.36, bf16[2048,2560]{1,0:T(8,128)(2,1)} %all-gather.6.cloned.1.call-done), kind=kOutput, calls=%fused_computation.7 | convolution fusion | flops 8617195520 | bytes 25182208 | tf_op jit(solution)/shard_map/dot_general | solution.py:21
  262.9 11.4 %convolution_convert_fusion.1 = bf16[2048,2048]{1,0:T(8,128)(2,1)} fusion(bf16[1024,2048]{1,0:T(8,128)(2,1)S(1)} %copy-done.30, bf16[1024,2048]{1,0:T(8,128)(2,1)S(1)} %get-tuple-element.134), kind=kOutput, calls=%fused_computation.17 | convolution fusion | flops 8594128896 | bytes 16777216 | tf_op jit(solution)/shard_map/dot_general | solution.py:21
  274.8 14.1 %convolution_convert_fusion = bf16[2048,2048]{1,0:T(8,128)(2,1)} fusion(bf16[1024,2048]{1,0:T(8,128)(2,1)} %get-tuple-element.36, bf16[1024,2048]{1,0:T(8,128)(2,1)} %get-tuple-element.131), kind=kOutput, calls=%fused_computation.16 | convolution fusion | flops 8594128896 | bytes 16777216 | tf_op jit(solution)/shard_map/dot_general | solution.py:21
  288.9 6.2 fusion.29.grad_ref
  295.1 12.2 %attention_backward.1 = (bf16[1024,512]{1,0:T(8,128)(2,1)}, bf16[1024,1024]{1,0:T(8,128)(2,1)}, bf16[1024,1024]{1,0:T(8,128)(2,1)}, bf16[1024,1024]{1,0:T(8,128)(2,1)}, bf16[1024,1024]{1,0:T(8,128)(2,1)}) custom-call(s32[5]{0:T(128)} %stack.65.info, s32[2]{0:T(128)} %lens.3, bf16[1024,512]{1,0:T(8,128)(2,1)} %get-tuple-element.32.query_ref, ...), custom_call_target="tpu_custom_call" | custom-call | flops 10737418240 | bytes 16777216 | tf_op jit(solution)/shard_map/attention_backward/pallas_call | solution.py:334
  307.4 2.3 collective-permute-start.16
  309.7 11.4 %fusion.8 = f32[1024,2048]{1,0:T(8,128)S(1)} fusion(bf16[1024,2048]{1,0:T(8,128)(2,1)S(1)} %copy-done.35, bf16[2048,2560]{1,0:T(8,128)(2,1)} %all-gather.6.cloned.1.call-done), kind=kOutput, calls=%fused_computation.21 | convolution fusion | flops 8589934592 | bytes 20971520 | tf_op jit(solution)/shard_map/dot_general | solution.py:21
  321.1 6.0 add_convert_fusion
  328.7 4.4 add_convert_fusion.1
  335.6 14.8 %fusion.10 = f32[1024,2048]{1,0:T(8,128)} fusion(bf16[1024,2048]{1,0:T(8,128)(2,1)} %copy-done.34, bf16[2048,3584]{1,0:T(8,128)(2,1)} %all-gather.4.cloned.1.call-done.weight_ref), kind=kOutput, calls=%fused_computation.23 | convolution fusion | flops 8589934592 | bytes 20971520 | tf_op jit(solution)/shard_map/dot_general | solution.py:21
  352.0 63.5 %collective-permute-done.17 = bf16[1024,1024]{1,0:T(8,128)(2,1)} collective-permute-done((bf16[1024,1024]{1,0:T(8,128)(2,1)}, bf16[1024,1024]{1,0:T(8,128)(2,1)}, u32[]{:S(2)}, u32[]{:S(2)}) %collective-permute-start.17) | collective-permute-done | bytes 2097184 | tf_op jit(solution)/shard_map/ppermute | solution.py:369
  415.5 6.3 convert_add_fusion
  421.8 6.6 reshape.221
  428.4 5.7 slice.159
  434.1 4.7 copy.72
  438.9 4.4 copy.71
  448.3 10.4 %fusion.14 = f32[1024,2048]{1,0:T(8,128)S(1)} fusion(bf16[1024,1536]{0,1:T(8,128)(2,1)S(1)} %bitcast.105, bf16[2048,3584]{1,0:T(8,128)(2,1)} %all-gather.4.cloned.1.call-done.weight_ref), kind=kOutput, calls=%fused_computation.27 | convolution fusion | flops 6442450944 | bytes 17825792 | tf_op jit(solution)/shard_map/dot_general | solution.py:21
  458.8 7.2 %fusion.36 = (f32[1024]{0:T(1024)S(1)}, f32[1024]{0:T(1024)S(1)}, f32[2048]{0:T(1024)S(1)}, f32[2048]{0:T(1024)S(1)}, f32[2048]{0:T(1024)S(1)}, /*index=5*/f32[2048]{0:T(1024)S(1)}, bf16[1024,2048]{1,0:T(8,128)(2,1)}) fusion(f32[1024]{0:T(1024)S(1)} %get-tuple-element.99, f32[1024]{0:T(1024)S(1)} %get-tuple-element.98, bf16[1024,2048]{1,0:T(8,128)(2,1)S(1)} %copy-done.1, ...), kind=kLoop, calls=%fused_computation.83 | loop fusion | flops 33544192 | bytes 25231360 | tf_op jit(solution)/shard_map/reduce_sum | solution.py:524
  467.8 11.4 %convolution_convert_fusion.2 = bf16[2048,1536]{1,0:T(8,128)(2,1)} fusion(bf16[1024,2048]{1,0:T(8,128)(2,1)} %get-tuple-element.31.rows_ref, bf16[1024,1536]{0,1:T(8,128)(2,1)S(1)} %bitcast.106), kind=kOutput, calls=%fused_computation.18 | convolution fusion | flops 6445596672 | bytes 13631488 | tf_op jit(solution)/shard_map/dot_general | solution.py:21
  483.1 23.7 %all-reduce.1 = (f32[2,1024]{1,0:T(2,128)S(1)}, f32[8192]{0:T(1024)S(1)}) all-reduce(f32[2,1024]{1,0:T(2,128)S(1)} %pad_maximum_fusion.4, f32[8192]{0:T(1024)S(1)} %bitcast.120), channel_id=1, replica_groups=mesh['fsdp'=2,'ctx'=4,'tp'=4] {'tp'}, use_global_device_ids=true, to_apply=%region_4.5 | all-reduce | flops 10240 | bytes 81920 | tf_op jit(solution)/shard_map/psum | solution.py:526
  506.8 24.6 %psum.23 = f32[13824]{0:T(1024)S(1)} all-reduce(f32[13824]{0:T(1024)S(1)} %pad_maximum_fusion.2), channel_id=1, replica_groups=mesh['fsdp'=2,'ctx'=4,'tp'=4] {'fsdp','ctx'}, use_global_device_ids=true, to_apply=%region_12.13 | all-reduce | flops 13824 | bytes 110592 | tf_op jit(solution)/shard_map/psum | solution.py:544
  533.7 2.8 convert_element_type.136
  536.5 2.8 convert_element_type.138
  539.3 2.8 reduce-scatter.7.cloned.1.call-done
  542.1 79.5 %reduce-scatter.9.cloned.1.call-done = bf16[1024,512]{1,0:T(8,128)(2,1)} async-done(((bf16[1024,2048]{1,0:T(8,128)(2,1)}), bf16[1024,512]{1,0:T(8,128)(2,1)}) %reduce-scatter.9.cloned.1.call-update) | async-done | bytes 1048592 | tf_op jit(solution)/shard_map/reduce_scatter | solution.py:525
  621.5 3.7 fusion.25
  625.3 62.3 %reduce-scatter.11.cloned.1.call-done = bf16[256,1536]{1,0:T(8,128)(2,1)} async-done(((bf16[2048,1536]{1,0:T(8,128)(2,1)}), bf16[256,1536]{1,0:T(8,128)(2,1)}) %reduce-scatter.11.cloned.1.call-update) | async-done | bytes 786448 | tf_op jit(solution)/shard_map/reduce_scatter | solution.py:534
  687.6 3.0 reshape.235
  (196 shorter events, 40.7 us)
Async XLA Ops:
  7.2 115.1 %all-gather.4.cloned.1.call-start = ((), (), s32[]{:S(2)}) async-start(), calls=%async_computation.6 | async-start | bytes 16515072 | tf_op jit(solution)/shard_map/all_gather | solution.py:409
  8.6 65.5 %copy-start.31 = (bf16[2,96]{1,0:T(2,128)(2,1)S(1)}, bf16[2,96]{1,0:T(2,128)(2,1)}, u32[]{:S(2)}) copy-start(bf16[2,96]{1,0:T(2,128)(2,1)} %param.21) | copy-start | bytes 1156
  8.6 65.6 %copy-start.22 = (bf16[64,4]{0,1:T(4,128)(2,1)S(1)}, bf16[64,4]{0,1:T(4,128)(2,1)}, u32[]{:S(2)}) copy-start(bf16[64,4]{0,1:T(4,128)(2,1)} %param.27) | copy-start | bytes 1540
  8.6 65.8 %copy-start.32 = (u32[32]{0:T(128)S(1)}, u32[32]{0:T(128)}, u32[]{:S(2)}) copy-start(u32[32]{0:T(128)} %constant.72) | copy-start | bytes 388
  8.6 67.1 %copy-start.23 = (bf16[256]{0:T(256)(128)(2,1)S(1)}, bf16[256]{0:T(256)(128)(2,1)}, u32[]{:S(2)}) copy-start(bf16[256]{0:T(256)(128)(2,1)} %param.18) | copy-start | bytes 1540
  8.6 67.1 %copy-start.24 = (bf16[256]{0:T(256)(128)(2,1)S(1)}, bf16[256]{0:T(256)(128)(2,1)}, u32[]{:S(2)}) copy-start(bf16[256]{0:T(256)(128)(2,1)} %param.19) | copy-start | bytes 1540
  8.6 67.1 %copy-start.25 = (bf16[256]{0:T(256)(128)(2,1)S(1)}, bf16[256]{0:T(256)(128)(2,1)}, u32[]{:S(2)}) copy-start(bf16[256]{0:T(256)(128)(2,1)} %param.24) | copy-start | bytes 1540
  8.6 67.1 %copy-start.26 = (bf16[256]{0:T(256)(128)(2,1)S(1)}, bf16[256]{0:T(256)(128)(2,1)}, u32[]{:S(2)}) copy-start(bf16[256]{0:T(256)(128)(2,1)} %param.25) | copy-start | bytes 1540
  8.7 67.0 %copy-start.27 = (bf16[256]{0:T(256)(128)(2,1)S(1)}, bf16[256]{0:T(256)(128)(2,1)}, u32[]{:S(2)}) copy-start(bf16[256]{0:T(256)(128)(2,1)} %param.23) | copy-start | bytes 1540
  8.7 67.0 %copy-start.28 = (bf16[256]{0:T(256)(128)(2,1)S(1)}, bf16[256]{0:T(256)(128)(2,1)}, u32[]{:S(2)}) copy-start(bf16[256]{0:T(256)(128)(2,1)} %param.29) | copy-start | bytes 1540
  11.3 89.4 %copy-start.10 = (bf16[2,512,512]{2,1,0:T(8,128)(2,1)S(1)}, bf16[2,512,512]{2,1,0:T(8,128)(2,1)}, u32[]{:S(2)}) copy-start(bf16[2,512,512]{2,1,0:T(8,128)(2,1)} %param.17) | copy-start | bytes 3145732
  11.3 232.7 %all-gather.6.cloned.1.call-start = ((), (), s32[]{:S(2)}) async-start(), calls=%async_computation.7 | async-start | bytes 11796480 | tf_op jit(solution)/shard_map/all_gather | solution.py:410
  12.6 468.3 %reduce-scatter.13.cloned.1.call-start = ((), (), s32[]{:S(2)}) async-start(), calls=%async_computation.11 | async-start | bytes 2359296 | tf_op jit(solution)/shard_map/reduce_scatter | solution.py:534
  12.7 28.1 %collective-permute-start.1 = (bf16[1024,512]{1,0:T(8,128)(2,1)S(1)}, bf16[1024,512]{1,0:T(8,128)(2,1)S(1)}, u32[]{:S(2)}, u32[]{:S(2)}) collective-permute-start(bf16[1024,512]{1,0:T(8,128)(2,1)S(1)} %bitcast.102), channel_id=1, source_target_pairs={{1,0},{2,1},{3,2},{5,4},{6,5},{7,6},{9,8},{10,9},{11,10},{13,12},{... | collective-permute-start | bytes 3145736 | tf_op jit(solution)/shard_map/ppermute | solution.py:42
  14.0 28.1 %collective-permute-start = (bf16[1024,512]{1,0:T(8,128)(2,1)S(1)}, bf16[1024,512]{1,0:T(8,128)(2,1)S(1)}, u32[]{:S(2)}, u32[]{:S(2)}) collective-permute-start(bf16[1024,512]{1,0:T(8,128)(2,1)S(1)} %bitcast.103), channel_id=1, source_target_pairs={{0,1},{1,2},{2,3},{4,5},{5,6},{6,7},{8,9},{9,10},{10,11},{12,13},{... | collective-permute-start | bytes 3145736 | tf_op jit(solution)/shard_map/ppermute | solution.py:41
  40.8 59.0 %copy-start.13 = (bf16[1024,512]{1,0:T(8,128)(2,1)}, bf16[1024,512]{1,0:T(8,128)(2,1)S(1)}, u32[]{:S(2)}) copy-start(bf16[1024,512]{1,0:T(8,128)(2,1)S(1)} %collective-permute-done.1.refs_5_) | copy-start | bytes 3145732
  40.8 26.4 %collective-permute-start.2 = (bf16[1024,512]{1,0:T(8,128)(2,1)S(1)}, bf16[1024,512]{1,0:T(8,128)(2,1)}, u32[]{:S(2)}, u32[]{:S(2)}) collective-permute-start(bf16[1024,512]{1,0:T(8,128)(2,1)S(1)} %collective-permute-done.1.refs_5_), channel_id=1, source_target_pairs={{1,0},{2,1},{3,2},{5,4},{6,5},{7,6},{9,8},{10,9},{11,10},{13,12},{... | collective-permute-start | bytes 3145736 | tf_op jit(solution)/shard_map/ppermute | solution.py:42
  42.1 25.1 %copy-start.14 = (bf16[1024,512]{1,0:T(8,128)(2,1)}, bf16[1024,512]{1,0:T(8,128)(2,1)S(1)}, u32[]{:S(2)}) copy-start(bf16[1024,512]{1,0:T(8,128)(2,1)S(1)} %collective-permute-done.refs_0_) | copy-start | bytes 3145732
  42.1 26.4 %collective-permute-start.4 = (bf16[1024,512]{1,0:T(8,128)(2,1)S(1)}, bf16[1024,512]{1,0:T(8,128)(2,1)}, u32[]{:S(2)}, u32[]{:S(2)}) collective-permute-start(bf16[1024,512]{1,0:T(8,128)(2,1)S(1)} %collective-permute-done.refs_0_), channel_id=1, source_target_pairs={{0,1},{1,2},{2,3},{4,5},{5,6},{6,7},{8,9},{9,10},{10,11},{12,13},{... | collective-permute-start | bytes 3145736 | tf_op jit(solution)/shard_map/ppermute | solution.py:41
  67.2 33.5 %collective-permute-start.3 = (bf16[1024,512]{1,0:T(8,128)(2,1)}, bf16[1024,512]{1,0:T(8,128)(2,1)}, u32[]{:S(2)}, u32[]{:S(2)}) collective-permute-start(bf16[1024,512]{1,0:T(8,128)(2,1)} %collective-permute-done.2.refs_3_), channel_id=1, source_target_pairs={{1,0},{2,1},{3,2},{5,4},{6,5},{7,6},{9,8},{10,9},{11,10},{13,12},{... | collective-permute-start | bytes 3145736 | tf_op jit(solution)/shard_map/ppermute | solution.py:42
  68.5 32.2 %collective-permute-start.5 = (bf16[1024,512]{1,0:T(8,128)(2,1)}, bf16[1024,512]{1,0:T(8,128)(2,1)}, u32[]{:S(2)}, u32[]{:S(2)}) collective-permute-start(bf16[1024,512]{1,0:T(8,128)(2,1)} %collective-permute-done.4.refs_2_), channel_id=1, source_target_pairs={{0,1},{1,2},{2,3},{4,5},{5,6},{6,7},{8,9},{9,10},{10,11},{12,13},{... | collective-permute-start | bytes 3145736 | tf_op jit(solution)/shard_map/ppermute | solution.py:41
  100.8 38.3 %collective-permute-start.10 = (bf16[1024,512]{1,0:T(8,128)(2,1)S(1)}, bf16[1024,512]{1,0:T(8,128)(2,1)}, u32[]{:S(2)}, u32[]{:S(2)}) collective-permute-start(bf16[1024,512]{1,0:T(8,128)(2,1)S(1)} %bitcast.110), channel_id=1, source_target_pairs={{1,0},{2,1},{3,2},{5,4},{6,5},{7,6},{9,8},{10,9},{11,10},{13,12},{... | collective-permute-start | bytes 3145736 | tf_op jit(solution)/shard_map/ppermute | solution.py:42
  102.1 38.3 %collective-permute-start.9 = (bf16[1024,512]{1,0:T(8,128)(2,1)S(1)}, bf16[1024,512]{1,0:T(8,128)(2,1)}, u32[]{:S(2)}, u32[]{:S(2)}) collective-permute-start(bf16[1024,512]{1,0:T(8,128)(2,1)S(1)} %bitcast.111), channel_id=1, source_target_pairs={{0,1},{1,2},{2,3},{4,5},{5,6},{6,7},{8,9},{9,10},{10,11},{12,13},{... | collective-permute-start | bytes 3145736 | tf_op jit(solution)/shard_map/ppermute | solution.py:41
  136.4 65.5 %collective-permute-start.7 = (bf16[1024,1024]{1,0:T(8,128)(2,1)}, bf16[1024,1024]{1,0:T(8,128)(2,1)}, u32[]{:S(2)}, u32[]{:S(2)}) collective-permute-start(bf16[1024,1024]{1,0:T(8,128)(2,1)} %get-tuple-element.33.refs_0_), channel_id=1, source_target_pairs={{0,8},{4,12},{1,9},{5,13},{2,10},{6,14},{3,11},{7,15},{16,24},{20,... | collective-permute-start | bytes 6291464 | tf_op jit(solution)/shard_map/ppermute | solution.py:359
  139.1 26.4 %collective-permute-start.11 = (bf16[1024,512]{1,0:T(8,128)(2,1)}, bf16[1024,512]{1,0:T(8,128)(2,1)S(1)}, u32[]{:S(2)}, u32[]{:S(2)}) collective-permute-start(bf16[1024,512]{1,0:T(8,128)(2,1)} %collective-permute-done.10.refs_5_), channel_id=1, source_target_pairs={{1,0},{2,1},{3,2},{5,4},{6,5},{7,6},{9,8},{10,9},{11,10},{13,12},{... | collective-permute-start | bytes 3145736 | tf_op jit(solution)/shard_map/ppermute | solution.py:42
  140.4 26.4 %collective-permute-start.13 = (bf16[1024,512]{1,0:T(8,128)(2,1)}, bf16[1024,512]{1,0:T(8,128)(2,1)S(1)}, u32[]{:S(2)}, u32[]{:S(2)}) collective-permute-start(bf16[1024,512]{1,0:T(8,128)(2,1)} %collective-permute-done.9.refs_0_), channel_id=1, source_target_pairs={{0,1},{1,2},{2,3},{4,5},{5,6},{6,7},{8,9},{9,10},{10,11},{12,13},{... | collective-permute-start | bytes 3145736 | tf_op jit(solution)/shard_map/ppermute | solution.py:41
  165.4 40.6 %copy-start.11 = (bf16[1024,512]{1,0:T(8,128)(2,1)}, bf16[1024,512]{1,0:T(8,128)(2,1)S(1)}, u32[]{:S(2)}) copy-start(bf16[1024,512]{1,0:T(8,128)(2,1)S(1)} %collective-permute-done.11.refs_3_) | copy-start | bytes 3145732
  165.4 40.6 %collective-permute-start.12 = (bf16[1024,512]{1,0:T(8,128)(2,1)S(1)}, bf16[1024,512]{1,0:T(8,128)(2,1)}, u32[]{:S(2)}, u32[]{:S(2)}) collective-permute-start(bf16[1024,512]{1,0:T(8,128)(2,1)S(1)} %collective-permute-done.11.refs_3_), channel_id=1, source_target_pairs={{1,0},{2,1},{3,2},{5,4},{6,5},{7,6},{9,8},{10,9},{11,10},{13,12},{... | collective-permute-start | bytes 3145736 | tf_op jit(solution)/shard_map/ppermute | solution.py:42
  166.7 39.3 %copy-start.12 = (bf16[1024,512]{1,0:T(8,128)(2,1)}, bf16[1024,512]{1,0:T(8,128)(2,1)S(1)}, u32[]{:S(2)}) copy-start(bf16[1024,512]{1,0:T(8,128)(2,1)S(1)} %collective-permute-done.13.refs_2_) | copy-start | bytes 3145732
  166.7 39.3 %collective-permute-start.14 = (bf16[1024,512]{1,0:T(8,128)(2,1)S(1)}, bf16[1024,512]{1,0:T(8,128)(2,1)}, u32[]{:S(2)}, u32[]{:S(2)}) collective-permute-start(bf16[1024,512]{1,0:T(8,128)(2,1)S(1)} %collective-permute-done.13.refs_2_), channel_id=1, source_target_pairs={{0,1},{1,2},{2,3},{4,5},{5,6},{6,7},{8,9},{9,10},{10,11},{12,13},{... | collective-permute-start | bytes 3145736 | tf_op jit(solution)/shard_map/ppermute | solution.py:41
  172.3 55.8 %collective-permute-start.6 = (bf16[1024,1024]{1,0:T(8,128)(2,1)}, bf16[1024,1024]{1,0:T(8,128)(2,1)}, u32[]{:S(2)}, u32[]{:S(2)}) collective-permute-start(bf16[1024,1024]{1,0:T(8,128)(2,1)} %get-tuple-element.33.refs_0_), channel_id=1, source_target_pairs={{0,4},{4,0},{8,12},{12,8},{1,5},{5,1},{9,13},{13,9},{2,6},{6,2},{1... | collective-permute-start | bytes 6291464 | tf_op jit(solution)/shard_map/ppermute | solution.py:358
  201.9 26.2 %collective-permute-start.8 = (bf16[1024,1024]{1,0:T(8,128)(2,1)}, bf16[1024,1024]{1,0:T(8,128)(2,1)}, u32[]{:S(2)}, u32[]{:S(2)}) collective-permute-start(bf16[1024,1024]{1,0:T(8,128)(2,1)} %collective-permute-done.7.refs_2_), channel_id=1, source_target_pairs={{8,12},{12,8},{9,13},{13,9},{10,14},{14,10},{11,15},{15,11},{24,28... | collective-permute-start | bytes 6291464 | tf_op jit(solution)/shard_map/ppermute | solution.py:360
  243.7 290.0 %reduce-scatter.15.cloned.1.call-start = ((), (), s32[]{:S(2)}) async-start(), calls=%async_computation.12 | async-start | bytes 9437184 | tf_op jit(solution)/shard_map/reduce_scatter | solution.py:534
  244.0 18.9 %copy-start.30 = (bf16[1024,2048]{1,0:T(8,128)(2,1)S(1)}, bf16[1024,2048]{1,0:T(8,128)(2,1)}, u32[]{:S(2)}) copy-start(bf16[1024,2048]{1,0:T(8,128)(2,1)} %get-tuple-element.30) | copy-start | bytes 12582916
  274.4 262.1 %reduce-scatter.17.cloned.1.call-start = ((), (), s32[]{:S(2)}) async-start(), calls=%async_computation.13 | async-start | bytes 9437184 | tf_op jit(solution)/shard_map/reduce_scatter | solution.py:534
  288.9 253.2 %reduce-scatter.7.cloned.1.call-start = ((), (), s32[]{:S(2)}) async-start(), calls=%async_computation.8 | async-start | bytes 5242880 | tf_op jit(solution)/shard_map/reduce_scatter | solution.py:462
  295.1 14.6 %copy-start.35 = (bf16[1024,2048]{1,0:T(8,128)(2,1)S(1)}, bf16[1024,2048]{1,0:T(8,128)(2,1)}, u32[]{:S(2)}) copy-start(bf16[1024,2048]{1,0:T(8,128)(2,1)} %get-tuple-element.131) | copy-start | bytes 12582916
  307.4 13.7 %copy-start.33 = (bf16[1024,512]{1,0:T(8,128)(2,1)S(1)}, bf16[1024,512]{1,0:T(8,128)(2,1)}, u32[]{:S(2)}) copy-start(bf16[1024,512]{1,0:T(8,128)(2,1)} %get-tuple-element.34.context_ref) | copy-start | bytes 3145732
  307.4 21.2 %collective-permute-start.16 = (bf16[1024,1024]{1,0:T(8,128)(2,1)}, bf16[1024,1024]{1,0:T(8,128)(2,1)}, u32[]{:S(2)}, u32[]{:S(2)}) collective-permute-start(bf16[1024,1024]{1,0:T(8,128)(2,1)} %get-tuple-element.43), channel_id=1, source_target_pairs={{8,12},{12,8},{9,13},{13,9},{10,14},{14,10},{11,15},{15,11},{24,28... | collective-permute-start | bytes 6291464 | tf_op jit(solution)/shard_map/ppermute | solution.py:367
  327.2 294.4 %reduce-scatter.9.cloned.1.call-start = ((), (), s32[]{:S(2)}) async-start(), calls=%async_computation.9 | async-start | bytes 5242880 | tf_op jit(solution)/shard_map/reduce_scatter | solution.py:525
  327.2 24.8 %collective-permute-start.15 = (bf16[1024,1024]{1,0:T(8,128)(2,1)}, bf16[1024,1024]{1,0:T(8,128)(2,1)}, u32[]{:S(2)}, u32[]{:S(2)}) collective-permute-start(bf16[1024,1024]{1,0:T(8,128)(2,1)} %get-tuple-element.41), channel_id=1, source_target_pairs={{4,0},{12,8},{5,1},{13,9},{6,2},{14,10},{7,3},{15,11},{20,16},{28,... | collective-permute-start | bytes 6291464 | tf_op jit(solution)/shard_map/ppermute | solution.py:366
  333.1 82.4 %collective-permute-start.17 = (bf16[1024,1024]{1,0:T(8,128)(2,1)}, bf16[1024,1024]{1,0:T(8,128)(2,1)}, u32[]{:S(2)}, u32[]{:S(2)}) collective-permute-start(bf16[1024,1024]{1,0:T(8,128)(2,1)} %add_convert_fusion.1), channel_id=1, source_target_pairs={{8,0},{12,4},{9,1},{13,5},{10,2},{14,6},{11,3},{15,7},{24,16},{28,... | collective-permute-start | bytes 6291464 | tf_op jit(solution)/shard_map/ppermute | solution.py:369
  335.6 14.8 %copy-start.8 = (bf16[1024,512]{1,0:T(8,128)(2,1)S(1)}, bf16[1024,512]{1,0:T(8,128)(2,1)}, u32[]{:S(2)}) copy-start(bf16[1024,512]{1,0:T(8,128)(2,1)} %get-tuple-element.39) | copy-start | bytes 3145732
  350.9 70.9 %copy-start = (f32[1024,512]{0,1:T(8,128)}, f32[1024,512]{0,1:T(8,128)S(1)}, u32[]{:S(2)}) copy-start(f32[1024,512]{0,1:T(8,128)S(1)} %copy.70) | copy-start | bytes 6291460
  466.0 221.6 %reduce-scatter.11.cloned.1.call-start = ((), (), s32[]{:S(2)}) async-start(), calls=%async_computation.10 | async-start | bytes 7077888 | tf_op jit(solution)/shard_map/reduce_scatter | solution.py:534
  479.3 27.5 %copy-start.18 = (f32[2048]{0:T(1024)S(1)}, f32[2048]{0:T(1024)}, u32[]{:S(2)}) copy-start(f32[2048]{0:T(1024)} %get-tuple-element.133) | copy-start | bytes 24580
  479.3 142.2 %copy-start.3 = (bf16[2,512,512]{2,1,0:T(8,128)(2,1)S(1)}, bf16[2,512,512]{2,1,0:T(8,128)(2,1)}, u32[]{:S(2)}) copy-start(bf16[2,512,512]{2,1,0:T(8,128)(2,1)} %param.15) | copy-start | bytes 3145732
  532.2 158.4 %copy-start.20 = (f32[1,256]{1,0:T(1,128)}, f32[1,256]{1,0:T(1,128)S(1)}, u32[]{:S(2)}) copy-start(f32[1,256]{1,0:T(1,128)S(1)} %get-tuple-element.115) | copy-start | bytes 3076
  (17 other events, 92.9 us)
Sparse Core Ops, SparseCore 0:
  11.5 83.9 all-gather.3
  97.9 78.0 all-gather.5
  243.8 56.6 reduce-scatter.12
  304.3 82.4 reduce-scatter.14
  390.1 71.3 reduce-scatter.16
  463.7 78.3 reduce-scatter.6
  544.4 77.1 reduce-scatter.8
  625.3 62.2 reduce-scatter.10

commit v2 on v1

v2 whole, which is shorter than its diff:
```python
import functools

import jax
import jax.numpy as jnp
from jax import lax
from jax.experimental import pallas as pl
from jax.experimental.pallas import tpu as pltpu
from jax.sharding import PartitionSpec as P

HEAD = 256
ROTARY = 64
F32 = jnp.float32
BF16 = jnp.bfloat16
VMEM_LIMIT = 40 << 20
SHARE = 1
NN = (((1,), (0,)), ((), ()))
NT = (((1,), (1,)), ((), ()))
TN = (((0,), (0,)), ((), ()))


def dot(a, b, dims):
    return lax.dot_general(a, b, dims, preferred_element_type=F32)


def after(value, *earlier):
    return lax.optimization_barrier((value, earlier))[0]


def params(*semantics):
    return pltpu.CompilerParams(
        dimension_semantics=semantics or None, vmem_limit_bytes=VMEM_LIMIT
    )


def cost(flops, moved, transcendentals=0):
    return pl.CostEstimate(
        flops=flops // SHARE, bytes_accessed=moved // SHARE, transcendentals=0
    )


def line_gather(piece, axis):
    size = lax.axis_size(axis)
    up = [(i, i + 1) for i in range(size - 1)]
    down = [(i + 1, i) for i in range(size - 1)]
    right, left = [], []
    a = b = piece
    for _ in range(size - 1):
        a = lax.ppermute(a, axis, up)
        b = lax.ppermute(b, axis, down)
        right.append(a)
        left.append(b)
    pairs = [(right[s - 1], left[size - s - 1]) for s in range(1, size)]
    return pairs, list(zip(right, left))


def send_chunks(chunks, axis):
    size = lax.axis_size(axis)
    return [chunks[0]] + [
        lax.ppermute(chunks[k], axis, [(i, (i + k) % size) for i in range(size)])
        for k in range(1, size)
    ]


def norm_kernel(size, me_ref, own, *refs):
    pairs = refs[: 2 * (size - 1)]
    gains, first_out, second_out, token_out, stat_out, work = refs[2 * (size - 1) :]
    part = own.shape[1]
    me = me_ref[0]
    for s in range(size):
        if s == 0:
            piece = own[...].astype(F32)
        else:
            piece = pairs[2 * s - 2][...].astype(F32) + pairs[2 * s - 1][...].astype(F32)
        at = lax.rem(me - s + size, size)
        work[:, pl.ds(pl.multiple_of(at * part, part), part)] = piece
    rows = work[...]
    token_out[...] = rows.astype(BF16)
    width = rows.shape[1]
    center = jnp.sum(rows, axis=1, keepdims=True) * (1.0 / width)
    shifted = rows - center
    inverse = lax.rsqrt(jnp.sum(shifted * shifted, axis=1, keepdims=True) * (1.0 / width) + 1e-05)
    normed = shifted * inverse
    first_out[...] = (normed * gains[0:1, :] + gains[1:2, :]).astype(BF16)
    second_out[...] = (normed * gains[2:3, :] + gains[3:4, :]).astype(BF16)
    lane = lax.broadcasted_iota(jnp.int32, stat_out.shape, 1)
    stat_out[...] = jnp.where(lane == 0, center, inverse)


def norm_call(me, own, pairs, gains, tile=128):
    count, part = own.shape
    size = len(pairs) + 1
    width = part * size
    flat = [p for pair in pairs for p in pair]
    block = pl.BlockSpec((tile, part), lambda i, *_: (i, 0))
    wide = pl.BlockSpec((tile, width), lambda i, *_: (i, 0))
    return pl.pallas_call(
        functools.partial(norm_kernel, size),
        grid_spec=pltpu.PrefetchScalarGridSpec(
            num_scalar_prefetch=1,
            grid=(count // tile,),
            in_specs=[block] * (1 + len(flat)) + [pl.BlockSpec((4, width), lambda i, *_: (0, 0))],
            out_specs=[wide, wide, wide, pl.BlockSpec((tile, 128), lambda i, *_: (i, 0))],
            scratch_shapes=[pltpu.VMEM((tile, width), F32)],
        ),
        out_shape=[
            jax.ShapeDtypeStruct((count, width), BF16),
            jax.ShapeDtypeStruct((count, width), BF16),
            jax.ShapeDtypeStruct((count, width), BF16),
            jax.ShapeDtypeStruct((count, 128), F32),
        ],
        compiler_params=params("arbitrary"),
        cost_estimate=cost(count * width * 16, count * width * 10),
        name="norm",
    )(me, own, *flat, gains)


def cot_kernel(size, local_len, tile, me_ref, len_ref, own, *refs):
    pairs = refs[: 2 * (size - 1)]
    rows_out, sum_out = refs[2 * (size - 1) :]
    part = own.shape[1]
    me, ctx = me_ref[0], me_ref[1]
    step = pl.program_id(0)
    start = step * tile
    seq = start // local_len
    length = len_ref[seq]
    position = ctx * local_len + lax.rem(start, local_len)
    position = position + lax.broadcasted_iota(jnp.int32, (tile, 1), 0)
    keep = position < length

    @pl.when(step == 0)
    def _():
        sum_out[...] = jnp.zeros_like(sum_out)

    for s in range(size):
        if s == 0:
            piece = own[...].astype(F32)
        else:
            piece = pairs[2 * s - 2][...].astype(F32) + pairs[2 * s - 1][...].astype(F32)
        piece = jnp.where(keep, piece, 0.0)
        at = lax.rem(me - s + size, size)
        cols = pl.ds(pl.multiple_of(at * part, part), part)
        rows_out[:, cols] = piece.astype(BF16)
        sum_out[0:1, cols] += jnp.sum(piece, axis=0, keepdims=True)


def cot_call(places, lengths, own, pairs, local_len, tile=256):
    count, part = own.shape
    size = len(pairs) + 1
    width = part * size
    flat = [p for pair in pairs for p in pair]
    block = pl.BlockSpec((tile, part), lambda i, *_: (i, 0))
    return pl.pallas_call(
        functools.partial(cot_kernel, size, local_len, tile),
        grid_spec=pltpu.PrefetchScalarGridSpec(
            num_scalar_prefetch=2,
            grid=(count // tile,),
            in_specs=[block] * (1 + len(flat)),
            out_specs=[
                pl.BlockSpec((tile, width), lambda i, *_: (i, 0)),
                pl.BlockSpec((8, width), lambda i, *_: (0, 0)),
            ],
        ),
        out_shape=[
            jax.ShapeDtypeStruct((count, width), BF16),
            jax.ShapeDtypeStruct((8, width), F32),
        ],
        compiler_params=params("arbitrary"),
        cost_estimate=cost(count * width * 4, count * width * 6),
        name="cotangent_rows",
    )(places, lengths, own, *flat)


def flat_rows(ref):
    value = ref[...]
    return value.reshape(value.shape[0] * value.shape[1], value.shape[2])


def joined_kernel(seqs, rows_ref, weight_ref, bias_ref, table_ref, query_ref, pair_ref):
    kind = lax.rem(pl.program_id(0), 3)
    out = dot(rows_ref[...], flat_rows(weight_ref), NN) + bias_ref[0:1, :]
    local_len = out.shape[0] // seqs

    def turned():
        front = out[:, :128]
        up = pltpu.roll(front, 128 - ROTARY // 2, 1)
        down = pltpu.roll(front, ROTARY // 2, 1)
        table = table_ref[...]
        if seqs > 1:
            table = jnp.concatenate([table] * seqs, axis=0)
        front = front * table[:, :128] + up * table[:, 128:256] + down * table[:, 256:]
        return jnp.concatenate([front, out[:, 128:]], axis=1)

    @pl.when(kind == 0)
    def _():
        query_ref[...] = (turned().astype(BF16).astype(F32) * HEAD ** (-0.5)).astype(BF16)

    @pl.when(kind == 1)
    def _():
        value = turned().astype(BF16)
        for s in range(seqs):
            pair_ref[s] = value[s * local_len : (s + 1) * local_len, :]

    @pl.when(kind == 2)
    def _():
        value = out.astype(BF16)
        for s in range(seqs):
            pair_ref[s] = value[s * local_len : (s + 1) * local_len, :]


def joined_call(rows, pack, bias, table, seqs, heads):
    count, width = rows.shape
    shards = pack.shape[0]
    local_len = count // seqs
    return pl.pallas_call(
        functools.partial(joined_kernel, seqs),
        grid=(3 * heads,),
        in_specs=[
            pl.BlockSpec((count, width), lambda j: (0, 0)),
            pl.BlockSpec((shards, width // shards, HEAD), lambda j: (0, 0, j)),
            pl.BlockSpec((8, HEAD), lambda j: (0, j)),
            pl.BlockSpec(table.shape, lambda j: (0, 0)),
        ],
        out_specs=[
            pl.BlockSpec((count, HEAD), lambda j: (0, j // 3)),
        ]
        + [
            pl.BlockSpec(
                (seqs, local_len, HEAD), lambda j: (0, 0, 2 * (j // 3) + (j % 3) // 2)
            )
        ],
        out_shape=[
            jax.ShapeDtypeStruct((count, heads * HEAD), BF16),
            jax.ShapeDtypeStruct((seqs, local_len, 2 * heads * HEAD), BF16),
        ],
        compiler_params=params("arbitrary"),
        cost_estimate=cost(6 * heads * HEAD * count * width, 2 * (count + 3 * heads * HEAD) * width),
        name="joined",
    )(rows, pack, jnp.broadcast_to(bias.reshape(1, -1), (8, bias.size)), table)


def visit(slot, local_len, half, block, place, length):
    first_key = block * local_len
    last_query = place * local_len + (half + 1) * (local_len // 2) - 1
    return (block >= 0) & (first_key <= last_query) & (first_key < length)


def masked(scores, first_key, first_query, length, axis_key):
    shape = scores.shape
    key = first_key + lax.broadcasted_iota(jnp.int32, shape, axis_key)
    query = first_query + lax.broadcasted_iota(jnp.int32, shape, 1 - axis_key)
    return (key <= query) & (key < length)


SLOTS = 4


def slot_refs(own_ref, below_ref, both_ref):
    return [own_ref, below_ref, both_ref.at[0], both_ref.at[1]]


def forward_kernel(slots, local_len, seq, info, lens, query_ref, pair_ref, *refs):
    context_ref, lse_ref, top, total, acc = refs
    length = lens[seq]
    place = info[slots]
    top[...] = jnp.full_like(top, -1e30)
    total[...] = jnp.zeros_like(total)
    acc[...] = jnp.zeros_like(acc)
    query = query_ref[...]
    for slot in range(slots):
        block = info[slot]
        first_key = block * local_len

        @pl.when((block >= 0) & (block <= place) & (first_key < length))
        def _():
            keys = pair_ref[block, :, :HEAD]
            vals = pair_ref[block, :, HEAD:]
            scores = dot(query, keys, NT)
            ok = masked(scores, first_key, place * local_len, length, 1)
            scores = jnp.where(ok, scores, -1e30)
            best = jnp.maximum(top[...], jnp.max(scores, axis=1, keepdims=True))
            scale = jnp.exp(top[...] - best)
            weights = jnp.exp(scores - best[:, :1])
            weights = jnp.where(ok, weights, 0.0)
            total[...] = total[...] * scale + jnp.sum(weights, axis=1, keepdims=True)
            acc[...] = acc[...] * scale[:, :1] + dot(weights.astype(BF16), vals, NN)
            top[...] = best

    context_ref[...] = (acc[...] / total[:, :1]).astype(BF16)
    lse_ref[...] = top[...] + jnp.log(total[...])


def forward_call(info, lengths, query, pairs, seq, heads):
    local_len = pairs.shape[2]
    slots = SLOTS
    return pl.pallas_call(
        functools.partial(forward_kernel, slots, local_len, seq),
        grid_spec=pltpu.PrefetchScalarGridSpec(
            num_scalar_prefetch=2,
            grid=(heads,),
            in_specs=[pl.BlockSpec((local_len, HEAD), lambda h, *_: (seq, h))]
            + [pl.BlockSpec((slots, None, local_len, 2 * HEAD), lambda h, *_: (0, seq, 0, h))],
            out_specs=[
                pl.BlockSpec((local_len, HEAD), lambda h, *_: (0, h)),
                pl.BlockSpec((local_len, 128), lambda h, *_: (0, h)),
            ],
            scratch_shapes=[
                pltpu.VMEM((local_len, 128), F32),
                pltpu.VMEM((local_len, 128), F32),
                pltpu.VMEM((local_len, HEAD), F32),
            ],
        ),
        out_shape=[
            jax.ShapeDtypeStruct((local_len, heads * HEAD), BF16),
            jax.ShapeDtypeStruct((local_len, heads * 128), F32),
        ],
        compiler_params=params("arbitrary"),
        cost_estimate=cost(
            4 * local_len * heads * HEAD * local_len * slots,
            4 * local_len * heads * HEAD * slots,
        ),
        name="attention_forward",
    )(info, lengths, query, pairs)


def backward_kernel(
    slots, local_len, seq, info, lens, query_ref, context_ref, grad_ref, lse_ref, pair_ref, *refs
):
    query_out = refs[0]
    pair_outs = slot_refs(*refs[1:4])
    acc = refs[4]
    length = lens[seq]
    place = info[slots]
    query = query_ref[...]
    grad = grad_ref[...]
    lse = lse_ref[:, :1]
    shared = jnp.sum(grad.astype(F32) * context_ref[...].astype(F32), axis=1, keepdims=True)
    acc[...] = jnp.zeros_like(acc)
    for slot in range(slots):
        block = info[slot]
        first_key = block * local_len
        seen = (block >= 0) & (block <= place) & (first_key < length)

        @pl.when(seen)
        def _():
            keys = pair_ref[block, :, :HEAD]
            vals = pair_ref[block, :, HEAD:]
            scores = dot(query, keys, NT)
            ok = masked(scores, first_key, place * local_len, length, 1)
            probs = jnp.where(ok, jnp.exp(scores - lse), 0.0)
            prob_grad = dot(grad, vals, NT)
            score_grad = (probs * (prob_grad - shared)).astype(BF16)
            acc[...] += dot(score_grad, keys, NN)
            pair_outs[slot][:, :HEAD] = dot(score_grad, query, TN).astype(BF16)
            pair_outs[slot][:, HEAD:] = dot(probs.astype(BF16), grad, TN).astype(BF16)

        @pl.when(jnp.logical_not(seen))
        def _():
            pair_outs[slot][...] = jnp.zeros_like(pair_outs[slot])

    query_out[...] = (acc[...] * HEAD ** (-0.5)).astype(BF16)


def backward_call(info, lengths, query, context, grad, lse, pairs, seq, heads):
    local_len = pairs.shape[2]
    slots = SLOTS
    here = pl.BlockSpec((local_len, HEAD), lambda h, *_: (seq, h))
    one = pl.BlockSpec((local_len, HEAD), lambda h, *_: (0, h))
    two = [pl.BlockSpec((local_len, 2 * HEAD), lambda h, *_: (0, h))] * 2
    two = two + [pl.BlockSpec((2, local_len, 2 * HEAD), lambda h, *_: (0, 0, h))]
    return pl.pallas_call(
        functools.partial(backward_kernel, slots, local_len, seq),
        grid_spec=pltpu.PrefetchScalarGridSpec(
            num_scalar_prefetch=2,
            grid=(heads,),
            in_specs=[here, one, here, pl.BlockSpec((local_len, 128), lambda h, *_: (0, h))]
            + [pl.BlockSpec((slots, None, local_len, 2 * HEAD), lambda h, *_: (0, seq, 0, h))],
            out_specs=[one] + two,
            scratch_shapes=[pltpu.VMEM((local_len, HEAD), F32)],
        ),
        out_shape=[jax.ShapeDtypeStruct((local_len, heads * HEAD), BF16)]
        + [jax.ShapeDtypeStruct((local_len, 2 * heads * HEAD), BF16)] * 2
        + [jax.ShapeDtypeStruct((2, local_len, 2 * heads * HEAD), BF16)],
        compiler_params=params("arbitrary"),
        cost_estimate=cost(
            10 * local_len * heads * HEAD * local_len * slots,
            8 * local_len * heads * HEAD * slots,
        ),
        name="attention_backward",
    )(info, lengths, query, context, grad, lse, pairs)


def return_pairs(own, below, siblings, axis):
    taken = lax.ppermute(siblings, axis, [(0, 1), (1, 0), (2, 3), (3, 2)])
    lower = (below.astype(F32) + taken[1].astype(F32)).astype(BF16)
    above = lax.ppermute(lower, axis, [(2, 0), (3, 1)])
    return [own, taken, above], taken


def branch_kernel(parts, active_ref, *refs):
    context_refs, (outer_ref, output_ref, out_ref) = refs[:parts], refs[parts:]
    out = dot(active_ref[...], outer_ref[...], NT)
    context = jnp.concatenate([ref[...] for ref in context_refs], axis=0)
    out_ref[...] = (out + dot(context, flat_rows(output_ref), NT)).astype(BF16)


def branch_call(active, contexts, outer, pack, column, tile=512):
    count, hidden = active.shape
    width, inside = outer.shape[0], contexts[0].shape[1]
    rows = width // pack.shape[0]
    return pl.pallas_call(
        functools.partial(branch_kernel, len(contexts)),
        grid=(width // tile,),
        in_specs=[pl.BlockSpec((count, hidden), lambda j: (0, 0))]
        + [pl.BlockSpec(c.shape, lambda j: (0, 0)) for c in contexts]
        + [
            pl.BlockSpec((tile, hidden), lambda j: (j, 0)),
            pl.BlockSpec((tile // rows, rows, inside), lambda j: (j, 0, column)),
        ],
        out_specs=pl.BlockSpec((count, tile), lambda j: (0, j)),
        out_shape=jax.ShapeDtypeStruct((count, width), BF16),
        compiler_params=params("arbitrary"),
        cost_estimate=cost(2 * count * width * (hidden + inside), 2 * width * (hidden + inside)),
        name="branch",
    )(active, *contexts, outer, pack)


def upper_kernel(rows_ref, weight_ref, bias_ref, active_ref, slope_ref):
    weight = flat_rows(weight_ref)
    bias = bias_ref[0:1, :]
    count = rows_ref.shape[0]
    piece = count // 4
    for i in range(4):
        here = slice(i * piece, (i + 1) * piece)
        upper = dot(rows_ref[here, :], weight, NN) + bias
        phi = 0.5 * (1.0 + lax.erf(upper * 0.7071067811865476))
        slope = phi + upper * jnp.exp(-0.5 * upper * upper) * 0.3989422804014327
        active_ref[here, :] = (upper * phi).astype(BF16)
        slope_ref[here, :] = slope.astype(BF16)


def upper_call(rows, pack, bias, column, tile=512):
    count, width = rows.shape
    hidden = bias.size
    shards = pack.shape[0]
    out = pl.BlockSpec((count, tile), lambda j: (0, j))
    first = column // tile
    return pl.pallas_call(
        upper_kernel,
        grid=(hidden // tile,),
        in_specs=[
            pl.BlockSpec((count, width), lambda j: (0, 0)),
            pl.BlockSpec((shards, width // shards, tile), lambda j: (0, 0, first + j)),
            pl.BlockSpec((8, tile), lambda j: (0, j)),
        ],
        out_specs=[out, out],
        out_shape=[jax.ShapeDtypeStruct((count, hidden), BF16)] * 2,
        compiler_params=params("arbitrary"),
        cost_estimate=cost(2 * count * width * hidden, 2 * width * (count + hidden)),
        name="upper",
    )(rows, pack, jnp.broadcast_to(bias.reshape(1, -1), (8, hidden)))


def context_grad_kernel(rows_ref, weight_ref, out_ref):
    out_ref[...] = dot(rows_ref[...], flat_rows(weight_ref), NN).astype(BF16)


def context_grad_call(rows, pack, column, inside, tile=512):
    count, width = rows.shape
    return pl.pallas_call(
        context_grad_kernel,
        grid=(count // tile,),
        in_specs=[
            pl.BlockSpec((tile, width), lambda i: (i, 0)),
            pl.BlockSpec(
                (pack.shape[0], width // pack.shape[0], inside), lambda i: (0, 0, column)
            ),
        ],
        out_specs=pl.BlockSpec((tile, inside), lambda i: (i, 0)),
        out_shape=jax.ShapeDtypeStruct((count, inside), BF16),
        compiler_params=params("arbitrary"),
        cost_estimate=cost(2 * count * width * inside, 2 * width * (count + inside)),
        name="context_grad",
    )(rows, pack)


def column_sums(grad, normed, out_ref):
    count, tile = grad.shape
    out_ref[0:1, :] = jnp.sum(grad * normed, axis=0, keepdims=True)
    out_ref[1:2, :] = jnp.sum(grad, axis=0, keepdims=True)
    out_ref[2:8, :] = jnp.zeros((6, tile), F32)


def second_kernel(grad_ref, weight_ref, rows_ref, stat_ref, gain_ref, out_ref, sum_ref):
    grad = dot(grad_ref[...], flat_rows(weight_ref), NT)
    normed = (rows_ref[...].astype(F32) - stat_ref[:, 0:1]) * stat_ref[:, 1:2]
    column_sums(grad, normed, sum_ref)
    out_ref[...] = (grad * gain_ref[2:3, :]).astype(BF16)


def second_call(grad, pack, column, rows, stats, gains, tile=512):
    count, hidden = grad.shape
    width = rows.shape[1]
    deep = width // pack.shape[0]
    return pl.pallas_call(
        second_kernel,
        grid=(width // tile,),
        in_specs=[
            pl.BlockSpec((count, hidden), lambda j: (0, 0)),
            pl.BlockSpec((tile // deep, deep, hidden), lambda j: (j, 0, column)),
            pl.BlockSpec((count, tile), lambda j: (0, j)),
            pl.BlockSpec((count, 128), lambda j: (0, 0)),
            pl.BlockSpec((4, tile), lambda j: (0, j)),
        ],
        out_specs=[
            pl.BlockSpec((count, tile), lambda j: (0, j)),
            pl.BlockSpec((8, tile), lambda j: (0, j)),
        ],
        out_shape=[
            jax.ShapeDtypeStruct((count, width), BF16),
            jax.ShapeDtypeStruct((8, width), F32),
        ],
        compiler_params=params("arbitrary"),
        cost_estimate=cost(2 * count * width * hidden, 2 * (width * hidden + 3 * count * width)),
        name="second_in_grad",
    )(grad, pack, rows, stats, gains)


def joined_grad_kernel(heads, *refs):
    (table_ref, out_ref, sum_ref), refs = refs[-3:], refs[:-3]
    table = table_ref[...]
    local_len = table.shape[0]

    def back(value):
        front = value[:, :128]
        up = pltpu.roll(front, 128 - ROTARY // 2, 1)
        down = pltpu.roll(front, ROTARY // 2, 1)
        front = front * table[:, :128] - up * table[:, 128:256] - down * table[:, 256:]
        return jnp.concatenate([front, value[:, 128:]], axis=1)

    sum_ref[...] = jnp.zeros_like(sum_ref)
    for seq in range(len(refs) // 4):
        query_ref, own_ref, near_ref, far_ref = refs[4 * seq : 4 * seq + 4]
        here = slice(seq * local_len, (seq + 1) * local_len)
        for head in range(heads):
            at = 3 * HEAD * head
            pair = slice(2 * HEAD * head, 2 * HEAD * (head + 1))
            total = own_ref[:, pair].astype(F32) + near_ref[0, :, pair].astype(F32)
            total = total + far_ref[:, pair].astype(F32)
            query = query_ref[:, HEAD * head : HEAD * (head + 1)].astype(F32)
            parts = [back(query), back(total[:, :HEAD]), total[:, HEAD:]]
            for i, part in enumerate(parts):
                cols = slice(at + HEAD * i, at + HEAD * (i + 1))
                low = part.astype(BF16)
                out_ref[here, cols] = low
                sum_ref[0:1, cols] += jnp.sum(low.astype(F32), axis=0, keepdims=True)


def joined_grad_call(queries, sums, table, heads):
    seqs = len(queries)
    count = seqs * queries[0].shape[0]
    width = 3 * heads * HEAD
    flat = [a for query, three in zip(queries, sums) for a in (query, *three)]
    return pl.pallas_call(
        functools.partial(joined_grad_kernel, heads),
        out_shape=[
            jax.ShapeDtypeStruct((count, width), BF16),
            jax.ShapeDtypeStruct((8, width), F32),
        ],
        compiler_params=params(),
        cost_estimate=cost(10 * count * width, 10 * count * width),
        name="joined_grad",
    )(*flat, table)


EXTRA = 8


def first_kernel(ranks, order, grad_ref, weight_ref, rows_ref, stat_ref, gain_ref, second_ref, *refs):
    out_refs, (sum_ref, row_ref) = refs[:ranks], refs[ranks:]
    step = pl.program_id(0)
    grad = dot(grad_ref[...], flat_rows(weight_ref), NT)
    count, tile = grad.shape
    normed = (rows_ref[...].astype(F32) - stat_ref[:, 0:1]) * stat_ref[:, 1:2]
    column_sums(grad, normed, sum_ref)
    total = grad * gain_ref[0:1, :] + second_ref[...].astype(F32)
    low = total.astype(BF16)
    for k in range(ranks):

        @pl.when(step == k)
        def _():
            out_refs[k][:count, :] = low

    plain = jnp.sum(total, axis=1, keepdims=True)
    along = jnp.sum(total * normed, axis=1, keepdims=True)
    lane = lax.broadcasted_iota(jnp.int32, row_ref.shape, 1)
    both = jnp.where(lane == 0, plain, along)

    @pl.when(step == 0)
    def _():
        row_ref[...] = both

    @pl.when(step > 0)
    def _():
        row_ref[...] += both

    @pl.when(step == ranks - 1)
    def _():
        turned = row_ref[...].T
        lines = [turned[i : i + 1, j : j + tile] for i in (0, 1) for j in range(0, count, tile)]
        lines.append(jnp.zeros((EXTRA - len(lines), tile), F32))
        extra = jnp.concatenate(lines, axis=0).astype(BF16)
        for ref in out_refs:
            ref[count:, :] = extra


def first_call(order, grad, pack, rows, stats, gains, second, ranks):
    count, inside = grad.shape
    width = rows.shape[1]
    tile = width // ranks
    deep = width // pack.shape[0]
    return pl.pallas_call(
        functools.partial(first_kernel, ranks),
        grid_spec=pltpu.PrefetchScalarGridSpec(
            num_scalar_prefetch=1,
            grid=(ranks,),
            in_specs=[
                pl.BlockSpec((count, inside), lambda j, _: (0, 0)),
                pl.BlockSpec((tile // deep, deep, inside), lambda j, order: (order[j], 0, 0)),
                pl.BlockSpec((count, tile), lambda j, order: (0, order[j])),
                pl.BlockSpec((count, 128), lambda j, _: (0, 0)),
                pl.BlockSpec((4, tile), lambda j, order: (0, order[j])),
                pl.BlockSpec((count, tile), lambda j, order: (0, order[j])),
            ],
            out_specs=[pl.BlockSpec((count + EXTRA, tile), lambda j, _: (0, 0))] * ranks
            + [pl.BlockSpec((8, tile), lambda j, order: (0, order[j]))],
            scratch_shapes=[pltpu.VMEM((count, 128), F32)],
        ),
        out_shape=[jax.ShapeDtypeStruct((count + EXTRA, tile), BF16)] * ranks
        + [jax.ShapeDtypeStruct((8, width), F32)],
        compiler_params=params("arbitrary"),
        cost_estimate=cost(2 * count * width * inside, 2 * (width * inside + 4 * count * width)),
        name="first_in_grad",
    )(order, grad, pack, rows, stats, gains, second)


def flips(size, by):
    return [(i, i ^ by) for i in range(size)]


def paired(group):
    return lax.axis_size(group[0]) == 2 and lax.axis_size(group[1]) == 4


def member(group):
    return lax.axis_size(group[1]) * lax.axis_index(group[0]) + lax.axis_index(group[1])


def gather_small(vector, group):
    if not paired(group):
        return lax.all_gather(vector.reshape(1, 1, -1), group, axis=0, tiled=True)[:, 0]
    rows = jnp.zeros((8, vector.size), vector.dtype)
    rows = lax.dynamic_update_slice_in_dim(rows, vector.reshape(1, -1), member(group), 0)
    for by in (1, 2, 4):
        rows = rows + lax.ppermute(rows, group, flips(8, by))
    return rows


def weight_grad_kernel(sizes, outs, small, order, *refs):
    parts = len(sizes)
    lhs_refs, rhs_refs, refs = refs[: 4 * parts], refs[4 * parts : 5 * parts], refs[5 * parts :]
    small_ref = refs[0] if small else None
    add_ref = refs[small] if outs > 1 else None
    out_refs, turned = refs[-1 - outs : -1], refs[-1]
    rows = lhs_refs[0].shape[1]
    deep = rows + EXTRA * small
    step = pl.program_id(0)

    def put(k, value, start):
        height = value.shape[0]
        if outs == 1:
            out_refs[0][k * deep + start : k * deep + start + height, :] = value.astype(BF16)
        else:
            add = add_ref[k * deep + start : k * deep + start + height, :].astype(F32)
            out_refs[k][start : start + height, :] = (value + add).astype(BF16)

    first = 0
    for i, size in enumerate(sizes):
        lhs, rhs_ref = lhs_refs[4 * i : 4 * i + 4], rhs_refs[i]

        @pl.when(step == first)
        def _():
            for k in range(4):
                turned[k * rows : (k + 1) * rows, :] = lhs[k][...].T

        @pl.when((step >= first) & (step < first + size))
        def _():
            out = dot(turned[...], rhs_ref[...], NN)
            for k in range(4):
                put(k, out[k * rows : (k + 1) * rows, :], 0)

        first += size
    if small:
        for k in range(4):
            put(k, small_ref[order[k]], rows)


def weight_grad_call(order, pairs, add=None, small=None, tile=512):
    count, width = pairs[0][0].shape
    rows = width // 8
    sizes = [rhs.shape[1] // tile for _, rhs in pairs]
    total = sum(sizes) * tile
    outs = 1 if add is None else 4
    height = rows if small is None else rows + EXTRA
    deep = 4 * height if add is None else height
    firsts = [sum(sizes[:i]) for i in range(len(sizes))]

    def column(k):
        return pl.BlockSpec((count, rows), lambda j, order: (0, order[k]))

    def piece(first, size):
        return pl.BlockSpec(
            (count, tile), lambda j, _: (0, jnp.minimum(jnp.maximum(j - first, 0), size - 1))
        )

    out = pl.BlockSpec((deep, tile), lambda j, *_: (0, j))
    extra_specs, extra = [], []
    if small is not None:
        extra_specs.append(pl.BlockSpec((8, EXTRA, tile), lambda j, *_: (0, 0, j)))
        extra.append(small)
    if add is not None:
        extra_specs.append(pl.BlockSpec((4 * height, tile), lambda j, *_: (0, j)))
        extra.append(add)
    return pl.pallas_call(
        functools.partial(weight_grad_kernel, sizes, outs, int(small is not None)),
        grid_spec=pltpu.PrefetchScalarGridSpec(
            num_scalar_prefetch=1,
            grid=(sum(sizes),),
            in_specs=[column(k) for _ in pairs for k in range(4)]
            + [piece(f, n) for f, n in zip(firsts, sizes)]
            + extra_specs,
            out_specs=[out] * outs,
            scratch_shapes=[pltpu.VMEM((4 * rows, count), BF16)],
        ),
        out_shape=[jax.ShapeDtypeStruct((deep, total), BF16)] * outs,
        compiler_params=params("arbitrary"),
        cost_estimate=cost(
            8 * rows * count * total, 2 * (count * (4 * rows + total) + 8 * rows * total)
        ),
        name="weight_grad",
    )(
        order,
        *[lhs for lhs, _ in pairs for _ in range(4)],
        *[rhs for _, rhs in pairs],
        *extra,
    )


def product_kernel(sizes, *refs):
    parts = len(sizes)
    lhs_refs, rhs_refs = refs[:parts], refs[parts : 2 * parts]
    out_ref, turned = refs[2 * parts :]
    step = pl.program_id(0)
    first = 0
    for lhs_ref, rhs_ref, size in zip(lhs_refs, rhs_refs, sizes):

        @pl.when(step == first)
        def _():
            turned[...] = lhs_ref[...].T

        @pl.when((step >= first) & (step < first + size))
        def _():
            out_ref[...] = dot(turned[...], rhs_ref[...], NN).astype(BF16)

        first += size


def product_call(pairs, tile=512):
    count, width = pairs[0][0].shape
    sizes = [rhs.shape[1] // tile for _, rhs in pairs]
    total = sum(sizes) * tile
    firsts = [sum(sizes[:i]) for i in range(len(sizes))]

    def piece(first, size):
        return pl.BlockSpec(
            (count, tile), lambda j: (0, jnp.minimum(jnp.maximum(j - first, 0), size - 1))
        )

    return pl.pallas_call(
        functools.partial(product_kernel, sizes),
        grid=(sum(sizes),),
        in_specs=[pl.BlockSpec((count, width), lambda j: (0, 0)) for _ in pairs]
        + [piece(f, n) for f, n in zip(firsts, sizes)],
        out_specs=pl.BlockSpec((width, tile), lambda j: (0, j)),
        out_shape=jax.ShapeDtypeStruct((width, total), BF16),
        scratch_shapes=[pltpu.VMEM((width, count), BF16)],
        compiler_params=params("arbitrary"),
        cost_estimate=cost(2 * width * count * total, 2 * (count * (width + total) + width * total)),
        name="product",
    )(*[lhs for lhs, _ in pairs], *[rhs for _, rhs in pairs])


STEPS = (0, 2, 4, 6)


def weight_grad_given(pairs, group, small=None):
    if not paired(group):
        return None
    steps = jnp.array(STEPS, jnp.int32)
    (given,) = weight_grad_call((member(group) ^ 1) ^ steps, pairs, small=small)
    return given


def weight_grad_kept(pairs, given, group, small=None):
    if not paired(group):
        whole = jnp.concatenate([dot(lhs, rhs, TN).astype(BF16) for lhs, rhs in pairs], axis=1)
        return [lax.psum_scatter(whole, group, scatter_dimension=0, tiled=True)]
    taken = lax.ppermute(given, group, flips(8, 1))
    sums = weight_grad_call(
        member(group) ^ jnp.array(STEPS, jnp.int32), pairs, taken, small=small
    )
    return [sums[0]] + [
        lax.ppermute(part, group, flips(8, by)) for part, by in zip(sums[1:], STEPS[1:])
    ]


def total_of(terms):
    return functools.reduce(lambda a, b: a + b, [t.astype(F32) for t in terms])


def line_sum(value, axis):
    size = lax.axis_size(axis)
    terms = [value]
    for step in range(1, size):
        terms.append(lax.ppermute(value, axis, [(i, (i + step) % size) for i in range(size)]))
    return functools.reduce(lambda a, b: a + b, terms)


def body(
    tokens,
    lengths,
    cotangent,
    first_gain,
    first_shift,
    joined_weight,
    joined_bias,
    output_weight,
    output_bias,
    second_gain,
    second_shift,
    inner_weight,
    inner_bias,
    outer_weight,
    outer_bias,
):
    group = ("fsdp", "ctx")
    seqs, local_len, part = tokens.shape
    count = seqs * local_len
    ranks = lax.axis_size("tp")
    width = part * ranks
    shards = lax.axis_size("fsdp") * lax.axis_size("ctx")
    rows_part = width // shards
    heads = joined_weight.shape[1]
    hidden = inner_weight.shape[1]
    me, ctx = lax.axis_index("tp"), lax.axis_index("ctx")

    own_tokens, own_cot = tokens.reshape(count, part), cotangent.reshape(count, part)
    joined_width, inside = heads * 3 * HEAD, heads * HEAD
    vectors = [first_gain, first_shift, second_gain, second_shift, output_bias, outer_bias]
    flat = jnp.concatenate(vectors + [joined_bias.reshape(-1), inner_bias.reshape(-1)])
    small = gather_small(jnp.pad(flat, (0, -flat.size % 256)), group)
    shard = jnp.concatenate(
        [joined_weight.reshape(rows_part, -1), output_weight.reshape(rows_part, -1), inner_weight],
        axis=1,
    )
    token_pairs, _ = line_gather(own_tokens, "tp")
    cot_pairs, cot_steps = line_gather(after(own_cot, token_pairs), "tp")
    pack = lax.all_gather(shard, group, axis=0, tiled=False)

    small = small.astype(F32)
    whole = [small[:, i * rows_part : (i + 1) * rows_part].reshape(width) for i in range(6)]
    at = 6 * rows_part
    whole_joined_bias = (
        small[:, at : at + joined_bias.size]
        .reshape((shards,) + joined_bias.shape)
        .transpose(1, 0, 2)
        .reshape(-1)
    )
    at += joined_bias.size
    whole_inner_bias = (
        small[:, at : at + inner_bias.size]
        .reshape((shards,) + inner_bias.shape)
        .transpose(1, 0, 2)
        .reshape(-1)
    )
    gains = jnp.stack(whole[:4])

    places = jnp.stack([me, ctx]).astype(jnp.int32)
    first_in, second_in, rows, stats = norm_call(places[:1], own_tokens, token_pairs, gains)
    center, inverse = stats[:, 0:1], stats[:, 1:2]
    positions = ctx * local_len + jnp.arange(local_len, dtype=jnp.int32)
    half = ROTARY // 2
    frequency = 1.0 / 10000.0 ** (jnp.arange(half, dtype=F32) * 2.0 / ROTARY)
    angles = positions.astype(F32)[:, None] * frequency[None, :]
    cosine, sine = jnp.cos(angles), jnp.sin(angles)
    ones = jnp.ones((local_len, 128 - ROTARY), F32)
    nothing = jnp.zeros((local_len, half), F32)
    blank = jnp.zeros((local_len, 128 - ROTARY), F32)
    table = jnp.concatenate(
        [cosine, cosine, ones, -sine, nothing, blank, nothing, sine, blank], axis=1
    )
    query, pair = joined_call(after(first_in, cot_steps[0]), pack, whole_joined_bias, table, seqs, heads)
    pairs = lax.all_gather(pair, "ctx", axis=0, tiled=False)
    low, odd = ctx - 2, ctx + 1 - 2 * lax.rem(ctx, 2)
    info = jnp.stack([ctx, low, odd, jnp.where(low >= 0, odd - 2, -1), ctx]).astype(jnp.int32)
    active, slope = upper_call(
        after(second_in, query, cot_steps[1:]), pack, whole_inner_bias, joined_width + inside
    )
    outer = lax.all_gather(after(outer_weight, active, pairs), group, axis=0, tiled=True)
    contexts, lses = [], []
    ready = after(query, active)
    for seq in range(seqs):
        context, lse = forward_call(info, lengths, ready, pairs, seq, heads)
        ready = after(query, context)
        contexts.append(context)
        lses.append(lse)

    grad_rows, bias_sums = cot_call(places, after(lengths, context), own_cot, cot_pairs, local_len)
    bias_grad = bias_sums[0]
    context_grad = context_grad_call(grad_rows, pack, joined_width // inside, inside)
    queries, sums = [], []
    for seq in range(seqs):
        query_grad, *pair_grads = backward_call(
            info, lengths, ready, contexts[seq], context_grad, lses[seq], pairs, seq, heads
        )
        ready = after(query, query_grad)
        queries.append(query_grad)
        three, taken = return_pairs(*pair_grads, "ctx")
        ready = after(ready, taken)
        sums.append(three)
    branch = branch_call(
        after(active, query_grad, taken), contexts, outer, pack, joined_width // inside
    )
    summed = lax.psum_scatter(branch, "tp", scatter_dimension=1, tiled=True).astype(F32)
    own_start = me * part
    own_bias = lax.dynamic_slice_in_dim(whole[4] + whole[5], own_start, part)
    valid = (positions[None, :] < lengths[:, None]).astype(F32).reshape(count, 1)
    layer_out = (valid * (own_tokens.astype(F32) + summed + own_bias)).astype(BF16)

    grad_late = after(grad_rows, branch)
    upper_grad = (dot(grad_late, outer, NN) * slope.astype(F32)).astype(BF16)
    inner_bias_grad = jnp.sum(upper_grad, axis=0, dtype=F32)
    feed = product_call([(after(grad_late, upper_grad), active), (second_in, upper_grad)])
    feed_out = lax.psum_scatter(feed, group, scatter_dimension=0, tiled=True)
    second_scaled, second_sums = second_call(
        after(upper_grad, feed),
        pack,
        (joined_width + inside) // hidden,
        rows,
        stats,
        gains,
    )
    joined_grad, joined_sums = joined_grad_call(
        after(queries, second_scaled), sums, table, heads
    )
    joined_bias_grad = joined_sums[0]
    order = lax.rem(me + jnp.arange(ranks, dtype=jnp.int32), ranks)
    *scaled, first_sums = first_call(
        order, joined_grad, pack, rows, stats, gains, second_scaled, ranks
    )

    column = jnp.concatenate([first_sums[:2], second_sums[:2], bias_grad.reshape(1, -1)])
    by_shard = [
        column.reshape(5, shards, rows_part).transpose(1, 0, 2).reshape(shards, -1),
        joined_bias_grad.reshape(heads, shards, -1).transpose(1, 0, 2).reshape(shards, -1),
        inner_bias_grad.reshape(-1, shards, inner_bias.shape[1])
        .transpose(1, 0, 2)
        .reshape(shards, -1),
    ]
    small_grads = jnp.concatenate(by_shard, axis=1)
    size = joined_width + inside
    riders = None
    if paired(group):
        riders = jnp.pad(
            small_grads.astype(BF16)[:, None, :],
            ((0, 0), (0, EXTRA - 1), (0, size - small_grads.shape[1])),
        )
    context = jnp.concatenate(contexts, axis=0)
    head_pairs = [(after(first_in, scaled[0]), joined_grad), (grad_rows, context)]
    head_given = weight_grad_given(head_pairs, group, riders)
    head_pairs = [(after(first_in, head_given), joined_grad), (grad_rows, context)]
    head_terms = weight_grad_kept(head_pairs, head_given, group, riders)
    head_out, feed_out = total_of(head_terms), feed_out.astype(F32)
    if riders is None:
        small_out = lax.psum_scatter(small_grads, group, scatter_dimension=0, tiled=True)[0]
    else:
        small_out = head_out[rows_part]
    vector = line_sum(small_out[: 4 * rows_part].reshape(-1, 128), "tp").reshape(4, -1)
    at = 5 * rows_part
    joined_bias_out = small_out[at : at + joined_bias.size].reshape(joined_bias.shape)
    at += joined_bias.size
    inner_bias_out = small_out[at : at + inner_bias.size].reshape(inner_bias.shape)
    bias_out = small_out[4 * rows_part : 5 * rows_part]

    share = total_of(send_chunks(scaled, "tp"))
    lines = 2 * count // part
    means = share[count : count + lines].reshape(2, count) / width
    share = share[:count]
    own_normed = (own_tokens.astype(F32) - center) * inverse
    own_rows = lax.dynamic_slice_in_dim(grad_rows, own_start, part, 1).astype(F32)
    tokens_grad = own_rows + inverse * (
        share - means[0][:, None] - own_normed * means[1][:, None]
    )

    return (
        layer_out.reshape(tokens.shape),
        tokens_grad.reshape(tokens.shape),
        vector[0],
        vector[1],
        head_out[:rows_part, :joined_width].reshape(joined_weight.shape),
        joined_bias_out,
        head_out[:rows_part, joined_width:].reshape(output_weight.shape),
        bias_out,
        vector[2],
        vector[3],
        feed_out[:, hidden:],
        inner_bias_out,
        feed_out[:, :hidden],
        bias_out,
    )


def solution(mesh):
    both = ("fsdp", "ctx")
    return jax.shard_map(
        body,
        mesh=mesh,
        in_specs=(
            P("fsdp", "ctx", "tp"),
            P("fsdp"),
            P("fsdp", "ctx", "tp"),
            P(both),
            P(both),
            P(both, "tp", None),
            P("tp", both),
            P(both, "tp", None),
            P(both),
            P(both),
            P(both),
            P(both, "tp"),
            P("tp", both),
            P(both, "tp"),
            P(both),
        ),
        out_specs=(
            P("fsdp", "ctx", "tp"),
            P("fsdp", "ctx", "tp"),
            P(both),
            P(both),
            P(both, "tp", None),
            P("tp", both),
            P(both, "tp", None),
            P(both),
            P(both),
            P(both),
            P(both, "tp"),
            P("tp", both),
            P(both, "tp"),
            P(both),
        ),
        check_vma=False,
    )
```

time: 707 us -> 578 us (0.82)
  matrix products: 122 us -> 14.9 us
  Pallas kernels: 55.6 us -> 155 us
  waiting for transfers between devices: 299 us -> 201 us
  blocking collectives: 71.3 us -> 0 us
  local copies, waits for them, and re-layouts: 45.3 us -> 87.6 us
  starting transfers between devices: 51.1 us -> 69.5 us
  other arithmetic: 37.9 us -> 22.9 us
    reduce_scatter x6 -> x2, waiting for transfers between devices: 145 us -> 0.01 us  [the longest x1 0.01 us: body(): lax.psum_scatter(branch, 'tp', scatter_dimension=1, tiled=True).astype(F32)]
    dot_general x11 -> x1, matrix products: 122 us -> 14.9 us  [dot(): return lax.dot_general(a, b, dims, preferred_element_type=F32)]
    pallas_call x2 -> x13, Pallas kernels: 22.8 us -> 129 us  [the longest x1 24.5 us: product_call(): pl.pallas_call(functools.partial(product_kernel, sizes), grid=(sum(sizes)...]
    unnamed x97 -> x160, local copies, waits for them, and re-layouts: 17.5 us -> 67.4 us
    ppermute x5 -> x15, waiting for transfers between devices: 29.6 us -> 79.4 us  [the longest x3 52.8 us: send_chunks(): lax.ppermute(chunks[k], axis, [(i, (i + k) % size) for i in range(size)])]
    psum x2 -> x0, blocking collectives: 48.3 us -> none  [the longest x1 24.6 us: body(): small_sums = lax.psum(small_grads, group)]
    ppermute x1 -> x2, waiting for transfers between devices: 63.5 us -> 33.8 us  [return_pairs(): above = lax.ppermute(lower, axis, [(2, 0), (3, 1)])]
    unnamed x1 -> x0, blocking collectives: 23 us -> none
  transfers between devices with their start and end apart: 26 -> 34, of which waited for: 8 -> 18; matrix products, arithmetic and copies ran while one was open for 28% -> 9% of each run, Pallas kernels for 8% -> 23%
where the time goes in v2:
time: 578 us; the launch traced here: 567 us
  waiting for transfers between devices  201 us (35%)
  Pallas kernels  155 us (27%)
  local copies, waits for them, and re-layouts  87.6 us (15%)
  starting transfers between devices  69.5 us (12%)
  other arithmetic  22.9 us (4%)
  between operations  15.2 us (3%)
  matrix products  14.9 us (3%)
    ppermute x6, waiting for transfers between devices, line_gather(): b = lax.ppermute(b, axis, down)  82 us
    unnamed x160, local copies, waits for them, and re-layouts  67.4 us
    ppermute x3, waiting for transfers between devices, send_chunks(): lax.ppermute(chunks[k], axis, [(i, (i + k) % size) for i in range(size)])  52.8 us
    ppermute x2, waiting for transfers between devices, return_pairs(): above = lax.ppermute(lower, axis, [(2, 0), (3, 1)])  33.8 us
    ppermute x6, starting transfers between devices, line_gather(): a = lax.ppermute(a, axis, up)  33.7 us
    pallas_call x1, Pallas kernels, product_call(): pl.pallas_call(functools.partial(product_kernel, sizes), grid=(sum(sizes)...  24.5 us
    pallas_call x2, Pallas kernels, weight_grad_call(): pl.pallas_call(functools.partial(weight_grad_kernel, sizes, outs, int(sma...  18.9 us
    pallas_call x1, Pallas kernels, first_call(): pl.pallas_call(functools.partial(first_kernel, ranks), grid_spec=pltpu.Pr...  15 us
  transfers between devices with their start and end apart: 34, of which 18 were waited for; matrix products, arithmetic and copies ran while one was open for 9% of the time, Pallas kernels for 23%

profile of v2, /device:TPU:0, one launch (start us, length us, event | category | flops | bytes accessed | tf_op | source)
XLA Modules:
  0.0 566.9 jit_solution(6313433452123404393)
XLA Ops:
  13.6 5.6 collective-permute-start
  19.2 21.2 %collective-permute-done.1.refs_5_ = bf16[1024,512]{1,0:T(8,128)(2,1)S(1)} collective-permute-done((bf16[1024,512]{1,0:T(8,128)(2,1)S(1)}, bf16[1024,512]{1,0:T(8,128)(2,1)S(1)}, u32[]{:S(2)}, u32[]{:S(2)}) %collective-permute-start.1) | collective-permute-done | bytes 1048608 | tf_op jit(solution)/shard_map/ppermute | solution.py:49
  42.6 5.5 collective-permute-start.4
  49.1 17.7 %collective-permute-done.2.refs_3_ = bf16[1024,512]{1,0:T(8,128)(2,1)} collective-permute-done((bf16[1024,512]{1,0:T(8,128)(2,1)S(1)}, bf16[1024,512]{1,0:T(8,128)(2,1)}, u32[]{:S(2)}, u32[]{:S(2)}) %collective-permute-start.2) | collective-permute-done | bytes 1048608 | tf_op jit(solution)/shard_map/ppermute | solution.py:49
  68.8 5.5 collective-permute-start.5
  77.7 3.3 collective-permute-done.7
  82.5 10.0 %collective-permute-done.3.refs_1_ = bf16[1024,512]{1,0:T(8,128)(2,1)} collective-permute-done((bf16[1024,512]{1,0:T(8,128)(2,1)}, bf16[1024,512]{1,0:T(8,128)(2,1)}, u32[]{:S(2)}, u32[]{:S(2)}) %collective-permute-start.3) | collective-permute-done | bytes 1048608 | tf_op jit(solution)/shard_map/ppermute | solution.py:49
  95.7 6.0 %collective-permute-start.9 = (bf16[1024,512]{1,0:T(8,128)(2,1)S(1)}, bf16[1024,512]{1,0:T(8,128)(2,1)}, u32[]{:S(2)}, u32[]{:S(2)}) collective-permute-start(bf16[1024,512]{1,0:T(8,128)(2,1)S(1)} %bitcast.93), channel_id=1, source_target_pairs={{0,1},{1,2},{2,3},{4,5},{5,6},{6,7},{8,9},{9,10},{10,11},{12,13},{... | collective-permute-start | bytes 3145736 | tf_op jit(solution)/shard_map/ppermute | solution.py:48
  109.0 10.0 %norm.1 = (bf16[1024,2048]{1,0:T(8,128)(2,1)S(1)}, bf16[1024,2048]{1,0:T(8,128)(2,1)}, bf16[1024,2048]{1,0:T(8,128)(2,1)}, f32[1024,128]{1,0:T(8,128)S(1)}) custom-call(s32[1]{0:T(128)} %bitcast.1.me_ref, bf16[1024,512]{1,0:T(8,128)(2,1)S(1)} %bitcast.91, bf16[1024,512]{1,0:T(8,128)(2,1)S(1)} %copy-done.46, ...), custom_call_target="tpu_custom_call" | custom-call | flops 33554432 | bytes 20971520 | tf_op jit(solution)/shard_map/norm/pallas_call | solution.py:96
  123.4 11.0 %joined.1 = (bf16[1024,512]{1,0:T(8,128)(2,1)S(1)}, bf16[2,512,1024]{2,1,0:T(8,128)(2,1)S(1)}) custom-call(bf16[1024,2048]{1,0:T(8,128)(2,1)S(1)} %copy-done.4, bf16[8,256,4096]{2,1,0:T(8,128)(2,1)} %bitcast.95, f32[8,1536]{1,0:T(8,128)S(1)} %broadcast_in_dim.34.bias_ref, f32[512,384]{1,0:T(8,128)S(1)} %concatenate.35.table_ref.refs_8_), custom_call_target="tpu_custom_call" | custom-call | flops 6442450944 | bytes 10485760 | tf_op jit(solution)/shard_map/joined/pallas_call | solution.py:214
  137.1 5.5 collective-permute-start.11
  142.6 17.4 %collective-permute-done.12.refs_3_ = bf16[1024,512]{1,0:T(8,128)(2,1)} collective-permute-done((bf16[1024,512]{1,0:T(8,128)(2,1)}, bf16[1024,512]{1,0:T(8,128)(2,1)}, u32[]{:S(2)}, u32[]{:S(2)}) %collective-permute-start.12) | collective-permute-done | bytes 1048608 | tf_op jit(solution)/shard_map/ppermute | solution.py:49
  161.3 5.5 collective-permute-start.13
  167.6 15.7 %collective-permute-done.14.refs_1_ = bf16[1024,512]{1,0:T(8,128)(2,1)} collective-permute-done((bf16[1024,512]{1,0:T(8,128)(2,1)}, bf16[1024,512]{1,0:T(8,128)(2,1)}, u32[]{:S(2)}, u32[]{:S(2)}) %collective-permute-start.14) | collective-permute-done | bytes 1048608 | tf_op jit(solution)/shard_map/ppermute | solution.py:49
  186.7 14.7 %upper.1 = (bf16[1024,2048]{1,0:T(8,128)(2,1)S(1)}, bf16[1024,2048]{1,0:T(8,128)(2,1)S(1)}) custom-call(bf16[1024,2048]{1,0:T(8,128)(2,1)S(1)} %copy-done.57, bf16[8,256,4096]{2,1,0:T(8,128)(2,1)} %bitcast.96, f32[8,2048]{1,0:T(8,128)S(1)} %broadcast_in_dim.39.bias_ref), custom_call_target="tpu_custom_call" | custom-call | flops 8589934592 | bytes 12582912 | tf_op jit(solution)/shard_map/upper/pallas_call | solution.py:447
  206.0 3.4 copy-done.7
  209.3 4.3 attention_forward.2
  213.7 4.3 attention_forward.3
  218.0 5.3 cotangent_rows.1
  223.3 5.6 context_grad.1.grad_ref
  229.0 5.9 %attention_backward.2 = (bf16[512,512]{1,0:T(8,128)(2,1)S(1)}, bf16[512,1024]{1,0:T(8,128)(2,1)S(1)}, bf16[512,1024]{1,0:T(8,128)(2,1)S(1)}, bf16[2,512,1024]{2,1,0:T(8,128)(2,1)S(1)}) custom-call(s32[5]{0:T(128)S(1)} %stack.32.info, s32[2]{0:T(128)S(1)} %copy-done.56, bf16[1024,512]{1,0:T(8,128)(2,1)S(1)} %get-tuple-element.86.query_ref, ...), custom_call_target="tpu_custom_call" | custom-call | flops 5368709120 | bytes 8388608 | tf_op jit(solution)/shard_map/attention_backward/pallas_call | solution.py:370
  237.6 2.5 collective-permute-start.15
  240.1 3.8 collective-permute-done.15.refs_2_
  245.9 5.4 attention_backward.3
  256.5 3.9 collective-permute-done.16.refs_6_
  265.9 13.6 %branch.1 = bf16[1024,2048]{1,0:T(8,128)(2,1)S(1)} custom-call(bf16[1024,2048]{1,0:T(8,128)(2,1)S(1)} %copy-done.60, bf16[512,512]{1,0:T(8,128)(2,1)S(1)} %copy-done.52, bf16[512,512]{1,0:T(8,128)(2,1)S(1)} %copy-done.54, bf16[2048,2048]{1,0:T(8,128)(2,1)} %all-gather.6.cloned.1.call-done.refs_2_, bf16[8,256,4096]{2,1,0:T(8,128)(2,1)} %bitcast.98), custom_call_target="tpu_custom_call" | custom-call | flops 10737418240 | bytes 10485760 | tf_op jit(solution)/shard_map/branch/pallas_call | solution.py:410
  281.6 14.9 %fusion.20 = f32[1024,2048]{1,0:T(8,128)} fusion(bf16[1024,2048]{1,0:T(8,128)(2,1)} %copy-done, bf16[2048,2048]{1,0:T(8,128)(2,1)} %all-gather.6.cloned.1.call-done.refs_2_), kind=kOutput, calls=%fused_computation.70 | convolution fusion | flops 8589934592 | bytes 20971520 | tf_op jit(solution)/shard_map/dot_general | solution.py:22
  296.4 7.2 %fusion.18 = (bf16[2048]{0:T(1024)(128)(2,1)S(1)}, bf16[1024,2048]{1,0:T(8,128)(2,1)}) fusion(f32[1024,2048]{1,0:T(8,128)} %fusion.20, bf16[1024,2048]{1,0:T(8,128)(2,1)S(1)} %copy-done.18), kind=kLoop, calls=%fused_computation.68 | loop fusion | flops 8386560 | bytes 16781312 | tf_op jit(solution)/shard_map/reduce_sum | solution.py:951
  308.1 24.5 %product.1 = bf16[2048,4096]{1,0:T(8,128)(2,1)} custom-call(bf16[1024,2048]{1,0:T(8,128)(2,1)S(1)} %copy-done.1, bf16[1024,2048]{1,0:T(8,128)(2,1)S(1)} %copy-done.58, bf16[1024,2048]{1,0:T(8,128)(2,1)S(1)} %copy-done.61, bf16[1024,2048]{1,0:T(8,128)(2,1)} %get-tuple-element.96.refs_3_.grad_ref), custom_call_target="tpu_custom_call" | custom-call | flops 17179869184 | bytes 29360128 | tf_op jit(solution)/shard_map/product/pallas_call | solution.py:788
  332.6 2.7 fusion.9
  336.6 2.7 fusion.8
  347.1 12.6 %second_in_grad.1 = (bf16[1024,2048]{1,0:T(8,128)(2,1)S(1)}, f32[8,2048]{1,0:T(8,128)S(1)}) custom-call(bf16[1024,2048]{1,0:T(8,128)(2,1)S(1)} %copy-done.19, bf16[8,256,4096]{2,1,0:T(8,128)(2,1)} %bitcast.99, bf16[1024,2048]{1,0:T(8,128)(2,1)S(1)} %copy-done.15, f32[1024,128]{1,0:T(8,128)S(1)} %get-tuple-element.92.stat_ref, ...), custom_call_target="tpu_custom_call" | custom-call | flops 8589934592 | bytes 20971520 | tf_op jit(solution)/shard_map/second_in_grad/pallas_call | solution.py:504
  361.7 12.8 %collective-permute-done.17.refs_3_ = bf16[512,1024]{1,0:T(8,128)(2,1)S(1)} collective-permute-done((bf16[512,1024]{1,0:T(8,128)(2,1)}, bf16[512,1024]{1,0:T(8,128)(2,1)S(1)}, u32[]{:S(2)}, u32[]{:S(2)}) %collective-permute-start.17) | collective-permute-done | bytes 1048608 | tf_op jit(solution)/shard_map/ppermute | solution.py:395
  375.4 21.0 %collective-permute-done.18.refs_7_ = bf16[512,1024]{1,0:T(8,128)(2,1)S(1)} collective-permute-done((bf16[512,1024]{1,0:T(8,128)(2,1)}, bf16[512,1024]{1,0:T(8,128)(2,1)S(1)}, u32[]{:S(2)}, u32[]{:S(2)}) %collective-permute-start.18) | collective-permute-done | bytes 1048608 | tf_op jit(solution)/shard_map/ppermute | solution.py:395
  400.1 4.4 joined_grad.1
  407.9 15.0 %first_in_grad.1 = (bf16[1032,512]{1,0:T(8,128)(2,1)S(1)}, bf16[1032,512]{1,0:T(8,128)(2,1)}, bf16[1032,512]{1,0:T(8,128)(2,1)}, bf16[1032,512]{1,0:T(8,128)(2,1)}, f32[8,2048]{1,0:T(8,128)S(1)}) custom-call(s32[4]{0:T(128)S(1)} %compare_select_fusion.order, bf16[1024,1536]{1,0:T(8,128)(2,1)S(1)} %get-tuple-element.105.grad_ref.refs_8_, ...), custom_call_target="tpu_custom_call" | custom-call | flops 6442450944 | bytes 23068672 | tf_op jit(solution)/shard_map/first_in_grad/pallas_call | solution.py:621
  424.3 2.4 copy-done.2
  426.8 2.5 copy-done.5
  430.5 9.1 %weight_grad.2 = bf16[1056,2048]{1,0:T(8,128)(2,1)} custom-call(s32[4]{0:T(128)S(1)} %fusion.16.order, bf16[1024,2048]{1,0:T(8,128)(2,1)S(1)} %copy-done.5, bf16[1024,2048]{1,0:T(8,128)(2,1)S(1)} %copy-done.5, bf16[1024,2048]{1,0:T(8,128)(2,1)S(1)} %copy-done.5, bf16[1024,2048]{1,0:T(8,128)(2,1)S(1)} %copy-done.5, bf16[1024,2048]{1,0:T(8,128)(2,1)S(1)} %copy-done.2, ...), custom_call_target="tpu_custom_call" | custom-call | flops 4294967296 | bytes 14680064 | tf_op jit(solution)/shard_map/weight_grad/pallas_call | solution.py:733
  441.7 3.5 collective-permute-start.20
  451.7 9.8 %weight_grad.3 = (bf16[264,2048]{1,0:T(8,128)(2,1)S(1)}, bf16[264,2048]{1,0:T(8,128)(2,1)S(1)}, bf16[264,2048]{1,0:T(8,128)(2,1)S(1)}, bf16[264,2048]{1,0:T(8,128)(2,1)S(1)}) custom-call(s32[4]{0:T(128)S(1)} %fusion.17.order, bf16[1024,2048]{1,0:T(8,128)(2,1)S(1)} %copy-done.6, bf16[1024,2048]{1,0:T(8,128)(2,1)S(1)} %copy-done.6, ...), custom_call_target="tpu_custom_call" | custom-call | flops 4294967296 | bytes 14680064 | tf_op jit(solution)/shard_map/weight_grad/pallas_call | solution.py:733
  461.6 7.7 %collective-permute-done.19 = bf16[1032,512]{1,0:T(8,128)(2,1)} collective-permute-done((bf16[1032,512]{1,0:T(8,128)(2,1)}, bf16[1032,512]{1,0:T(8,128)(2,1)}, u32[]{:S(2)}, u32[]{:S(2)}) %collective-permute-start.19) | collective-permute-done | bytes 1056800 | tf_op jit(solution)/shard_map/ppermute | solution.py:59
  469.3 45.0 %collective-permute-done.20 = bf16[1032,512]{1,0:T(8,128)(2,1)} collective-permute-done((bf16[1032,512]{1,0:T(8,128)(2,1)}, bf16[1032,512]{1,0:T(8,128)(2,1)}, u32[]{:S(2)}, u32[]{:S(2)}) %collective-permute-start.20) | collective-permute-done | bytes 1056800 | tf_op jit(solution)/shard_map/ppermute | solution.py:59
  516.9 14.4 %collective-permute-done.25 = bf16[264,2048]{1,0:T(8,128)(2,1)S(1)} collective-permute-done((bf16[264,2048]{1,0:T(8,128)(2,1)S(1)}, bf16[264,2048]{1,0:T(8,128)(2,1)S(1)}, u32[]{:S(2)}, u32[]{:S(2)}) %collective-permute-start.25) | collective-permute-done | bytes 1081376 | tf_op jit(solution)/shard_map/ppermute | solution.py:822
  532.0 9.3 %collective-permute-start.28 = (f32[8,128]{1,0:T(8,128)S(1)}, f32[8,128]{1,0:T(8,128)S(1)}, u32[]{:S(2)}, u32[]{:S(2)}) collective-permute-start(f32[8,128]{1,0:T(8,128)S(1)} %bitcast.120), channel_id=1, source_target_pairs={{0,3},{1,0},{2,1},{3,2},{4,7},{5,4},{6,5},{7,6},{8,11},{9,8},{10,9... | collective-permute-start | bytes 12296 | tf_op jit(solution)/shard_map/ppermute | solution.py:834
  545.9 3.2 reshape.218
  551.8 3.5 fusion.7
  555.3 4.1 fusion.19
  (274 shorter events, 106.7 us)
Async XLA Ops:
  7.2 113.8 %all-gather.8.cloned.1.call-start = ((), (), s32[]{:S(2)}) async-start(), calls=%async_computation.5 | async-start | bytes 18874368 | tf_op jit(solution)/shard_map/all_gather | solution.py:877
  11.1 63.2 %copy-start.71 = (bf16[2,96]{1,0:T(2,128)(2,1)S(1)}, bf16[2,96]{1,0:T(2,128)(2,1)}, u32[]{:S(2)}) copy-start(bf16[2,96]{1,0:T(2,128)(2,1)} %param.23) | copy-start | bytes 1156
  11.1 63.3 %copy-start.64 = (bf16[64,4]{0,1:T(4,128)(2,1)S(1)}, bf16[64,4]{0,1:T(4,128)(2,1)}, u32[]{:S(2)}) copy-start(bf16[64,4]{0,1:T(4,128)(2,1)} %param.29) | copy-start | bytes 1540
  11.1 63.5 %copy-start.65 = (bf16[256]{0:T(256)(128)(2,1)S(1)}, bf16[256]{0:T(256)(128)(2,1)}, u32[]{:S(2)}) copy-start(bf16[256]{0:T(256)(128)(2,1)} %param.20) | copy-start | bytes 1540
  11.1 63.5 %copy-start.66 = (bf16[256]{0:T(256)(128)(2,1)S(1)}, bf16[256]{0:T(256)(128)(2,1)}, u32[]{:S(2)}) copy-start(bf16[256]{0:T(256)(128)(2,1)} %param.21) | copy-start | bytes 1540
  11.1 63.5 %copy-start.67 = (bf16[256]{0:T(256)(128)(2,1)S(1)}, bf16[256]{0:T(256)(128)(2,1)}, u32[]{:S(2)}) copy-start(bf16[256]{0:T(256)(128)(2,1)} %param.26) | copy-start | bytes 1540
  11.1 63.5 %copy-start.68 = (bf16[256]{0:T(256)(128)(2,1)S(1)}, bf16[256]{0:T(256)(128)(2,1)}, u32[]{:S(2)}) copy-start(bf16[256]{0:T(256)(128)(2,1)} %param.27) | copy-start | bytes 1540
  11.1 63.5 %copy-start.69 = (bf16[256]{0:T(256)(128)(2,1)S(1)}, bf16[256]{0:T(256)(128)(2,1)}, u32[]{:S(2)}) copy-start(bf16[256]{0:T(256)(128)(2,1)} %param.25) | copy-start | bytes 1540
  11.1 63.5 %copy-start.70 = (bf16[256]{0:T(256)(128)(2,1)S(1)}, bf16[256]{0:T(256)(128)(2,1)}, u32[]{:S(2)}) copy-start(bf16[256]{0:T(256)(128)(2,1)} %param.31) | copy-start | bytes 1540
  11.1 83.3 %copy-start.42 = (bf16[2,512,512]{2,1,0:T(8,128)(2,1)S(1)}, bf16[2,512,512]{2,1,0:T(8,128)(2,1)}, u32[]{:S(2)}) copy-start(bf16[2,512,512]{2,1,0:T(8,128)(2,1)} %param.19) | copy-start | bytes 3145732
  11.2 194.3 %all-gather.10.cloned.1.call-start = ((), (), s32[]{:S(2)}) async-start(), calls=%async_computation.6 | async-start | bytes 10485760 | tf_op jit(solution)/shard_map/all_gather | solution.py:912
  12.3 28.1 %collective-permute-start.1 = (bf16[1024,512]{1,0:T(8,128)(2,1)S(1)}, bf16[1024,512]{1,0:T(8,128)(2,1)S(1)}, u32[]{:S(2)}, u32[]{:S(2)}) collective-permute-start(bf16[1024,512]{1,0:T(8,128)(2,1)S(1)} %bitcast.89), channel_id=1, source_target_pairs={{1,0},{2,1},{3,2},{5,4},{6,5},{7,6},{9,8},{10,9},{11,10},{13,12},{... | collective-permute-start | bytes 3145736 | tf_op jit(solution)/shard_map/ppermute | solution.py:49
  13.6 29.0 %collective-permute-start = (bf16[1024,512]{1,0:T(8,128)(2,1)S(1)}, bf16[1024,512]{1,0:T(8,128)(2,1)S(1)}, u32[]{:S(2)}, u32[]{:S(2)}) collective-permute-start(bf16[1024,512]{1,0:T(8,128)(2,1)S(1)} %bitcast.90), channel_id=1, source_target_pairs={{0,1},{1,2},{2,3},{4,5},{5,6},{6,7},{8,9},{9,10},{10,11},{12,13},{... | collective-permute-start | bytes 3145736 | tf_op jit(solution)/shard_map/ppermute | solution.py:48
  40.4 26.4 %collective-permute-start.2 = (bf16[1024,512]{1,0:T(8,128)(2,1)S(1)}, bf16[1024,512]{1,0:T(8,128)(2,1)}, u32[]{:S(2)}, u32[]{:S(2)}) collective-permute-start(bf16[1024,512]{1,0:T(8,128)(2,1)S(1)} %collective-permute-done.1.refs_5_), channel_id=1, source_target_pairs={{1,0},{2,1},{3,2},{5,4},{6,5},{7,6},{9,8},{10,9},{11,10},{13,12},{... | collective-permute-start | bytes 3145736 | tf_op jit(solution)/shard_map/ppermute | solution.py:49
  42.6 26.2 %collective-permute-start.4 = (bf16[1024,512]{1,0:T(8,128)(2,1)S(1)}, bf16[1024,512]{1,0:T(8,128)(2,1)}, u32[]{:S(2)}, u32[]{:S(2)}) collective-permute-start(bf16[1024,512]{1,0:T(8,128)(2,1)S(1)} %collective-permute-done.refs_0_), channel_id=1, source_target_pairs={{0,1},{1,2},{2,3},{4,5},{5,6},{6,7},{8,9},{9,10},{10,11},{12,13},{... | collective-permute-start | bytes 3145736 | tf_op jit(solution)/shard_map/ppermute | solution.py:48
  66.8 25.7 %collective-permute-start.3 = (bf16[1024,512]{1,0:T(8,128)(2,1)}, bf16[1024,512]{1,0:T(8,128)(2,1)}, u32[]{:S(2)}, u32[]{:S(2)}) collective-permute-start(bf16[1024,512]{1,0:T(8,128)(2,1)} %collective-permute-done.2.refs_3_), channel_id=1, source_target_pairs={{1,0},{2,1},{3,2},{5,4},{6,5},{7,6},{9,8},{10,9},{11,10},{13,12},{... | collective-permute-start | bytes 3145736 | tf_op jit(solution)/shard_map/ppermute | solution.py:49
  68.8 25.6 %collective-permute-start.5 = (bf16[1024,512]{1,0:T(8,128)(2,1)}, bf16[1024,512]{1,0:T(8,128)(2,1)}, u32[]{:S(2)}, u32[]{:S(2)}) collective-permute-start(bf16[1024,512]{1,0:T(8,128)(2,1)} %collective-permute-done.4.refs_2_), channel_id=1, source_target_pairs={{0,1},{1,2},{2,3},{4,5},{5,6},{6,7},{8,9},{9,10},{10,11},{12,13},{... | collective-permute-start | bytes 3145736 | tf_op jit(solution)/shard_map/ppermute | solution.py:48
  74.9 1.3 collective-permute-start.6
  76.3 4.7 collective-permute-start.7
  81.1 25.1 %collective-permute-start.8 = (bf16[8,2048]{1,0:T(8,128)(2,1)S(1)}, bf16[8,2048]{1,0:T(8,128)(2,1)S(1)}, u32[]{:S(2)}, u32[]{:S(2)}) collective-permute-start(bf16[8,2048]{1,0:T(8,128)(2,1)S(1)} %add.113), channel_id=1, source_target_pairs={{0,16},{4,20},{8,24},{12,28},{16,0},{20,4},{24,8},{28,12},{1,17},{... | collective-permute-start | bytes 98312 | tf_op jit(solution)/shard_map/ppermute | solution.py:664
  94.4 26.6 %collective-permute-start.10 = (bf16[1024,512]{1,0:T(8,128)(2,1)S(1)}, bf16[1024,512]{1,0:T(8,128)(2,1)}, u32[]{:S(2)}, u32[]{:S(2)}) collective-permute-start(bf16[1024,512]{1,0:T(8,128)(2,1)S(1)} %bitcast.92), channel_id=1, source_target_pairs={{1,0},{2,1},{3,2},{5,4},{6,5},{7,6},{9,8},{10,9},{11,10},{13,12},{... | collective-permute-start | bytes 3145736 | tf_op jit(solution)/shard_map/ppermute | solution.py:49
  95.7 25.3 %collective-permute-start.9 = (bf16[1024,512]{1,0:T(8,128)(2,1)S(1)}, bf16[1024,512]{1,0:T(8,128)(2,1)}, u32[]{:S(2)}, u32[]{:S(2)}) collective-permute-start(bf16[1024,512]{1,0:T(8,128)(2,1)S(1)} %bitcast.93), channel_id=1, source_target_pairs={{0,1},{1,2},{2,3},{4,5},{5,6},{6,7},{8,9},{9,10},{10,11},{12,13},{... | collective-permute-start | bytes 3145736 | tf_op jit(solution)/shard_map/ppermute | solution.py:48
  121.0 221.7 %copy-start.11 = (f32[1024,128]{1,0:T(8,128)}, f32[1024,128]{1,0:T(8,128)S(1)}, u32[]{:S(2)}) copy-start(f32[1024,128]{1,0:T(8,128)S(1)} %get-tuple-element.92.stat_ref) | copy-start | bytes 1572868
  135.7 93.3 %copy-start.21 = (bf16[1024,512]{1,0:T(8,128)(2,1)}, bf16[1024,512]{1,0:T(8,128)(2,1)S(1)}, u32[]{:S(2)}) copy-start(bf16[1024,512]{1,0:T(8,128)(2,1)S(1)} %get-tuple-element.86.query_ref) | copy-start | bytes 3145732
  135.7 127.0 %all-gather.6.cloned.1.call-start = ((), (), s32[]{:S(2)}) async-start(), calls=%async_computation.2 | async-start | bytes 9437184 | tf_op jit(solution)/shard_map/all_gather | solution.py:918
  135.8 24.3 %collective-permute-start.12 = (bf16[1024,512]{1,0:T(8,128)(2,1)}, bf16[1024,512]{1,0:T(8,128)(2,1)}, u32[]{:S(2)}, u32[]{:S(2)}) collective-permute-start(bf16[1024,512]{1,0:T(8,128)(2,1)} %collective-permute-done.10.refs_5_), channel_id=1, source_target_pairs={{1,0},{2,1},{3,2},{5,4},{6,5},{7,6},{9,8},{10,9},{11,10},{13,12},{... | collective-permute-start | bytes 3145736 | tf_op jit(solution)/shard_map/ppermute | solution.py:49
  137.1 24.2 %collective-permute-start.11 = (bf16[1024,512]{1,0:T(8,128)(2,1)}, bf16[1024,512]{1,0:T(8,128)(2,1)}, u32[]{:S(2)}, u32[]{:S(2)}) collective-permute-start(bf16[1024,512]{1,0:T(8,128)(2,1)} %collective-permute-done.9.refs_0_), channel_id=1, source_target_pairs={{0,1},{1,2},{2,3},{4,5},{5,6},{6,7},{8,9},{9,10},{10,11},{12,13},{... | collective-permute-start | bytes 3145736 | tf_op jit(solution)/shard_map/ppermute | solution.py:48
  160.0 23.3 %collective-permute-start.14 = (bf16[1024,512]{1,0:T(8,128)(2,1)}, bf16[1024,512]{1,0:T(8,128)(2,1)}, u32[]{:S(2)}, u32[]{:S(2)}) collective-permute-start(bf16[1024,512]{1,0:T(8,128)(2,1)} %collective-permute-done.12.refs_3_), channel_id=1, source_target_pairs={{1,0},{2,1},{3,2},{5,4},{6,5},{7,6},{9,8},{10,9},{11,10},{13,12},{... | collective-permute-start | bytes 3145736 | tf_op jit(solution)/shard_map/ppermute | solution.py:49
  161.3 23.2 %collective-permute-start.13 = (bf16[1024,512]{1,0:T(8,128)(2,1)}, bf16[1024,512]{1,0:T(8,128)(2,1)}, u32[]{:S(2)}, u32[]{:S(2)}) collective-permute-start(bf16[1024,512]{1,0:T(8,128)(2,1)} %collective-permute-done.11.refs_2_), channel_id=1, source_target_pairs={{0,1},{1,2},{2,3},{4,5},{5,6},{6,7},{8,9},{9,10},{10,11},{12,13},{... | collective-permute-start | bytes 3145736 | tf_op jit(solution)/shard_map/ppermute | solution.py:48
  205.5 346.3 %reduce-scatter.3.cloned.1.call-start = ((), (), s32[]{:S(2)}) async-start(), calls=%async_computation.3 | async-start | bytes 5242880 | tf_op jit(solution)/shard_map/reduce_scatter | solution.py:943
  237.6 6.3 %collective-permute-start.15 = (bf16[2,512,1024]{2,1,0:T(8,128)(2,1)S(1)}, bf16[2,512,1024]{2,1,0:T(8,128)(2,1)S(1)}, u32[]{:S(2)}, u32[]{:S(2)}) collective-permute-start(bf16[2,512,1024]{2,1,0:T(8,128)(2,1)S(1)} %get-tuple-element.85), channel_id=1, source_target_pairs={{0,4},{4,0},{8,12},{12,8},{1,5},{5,1},{9,13},{13,9},{2,6},{6,2},{1... | collective-permute-start | bytes 6291464 | tf_op jit(solution)/shard_map/ppermute | solution.py:393
  243.9 88.7 %copy-start.13 = (bf16[2,512,1024]{2,1,0:T(8,128)(2,1)}, bf16[2,512,1024]{2,1,0:T(8,128)(2,1)S(1)}, u32[]{:S(2)}) copy-start(bf16[2,512,1024]{2,1,0:T(8,128)(2,1)S(1)} %collective-permute-done.15.refs_2_) | copy-start | bytes 6291460
  254.1 6.3 %collective-permute-start.16 = (bf16[2,512,1024]{2,1,0:T(8,128)(2,1)S(1)}, bf16[2,512,1024]{2,1,0:T(8,128)(2,1)}, u32[]{:S(2)}, u32[]{:S(2)}) collective-permute-start(bf16[2,512,1024]{2,1,0:T(8,128)(2,1)S(1)} %get-tuple-element.89), channel_id=1, source_target_pairs={{0,4},{4,0},{8,12},{12,8},{1,5},{5,1},{9,13},{13,9},{2,6},{6,2},{1... | collective-permute-start | bytes 6291464 | tf_op jit(solution)/shard_map/ppermute | solution.py:393
  281.5 273.8 %reduce-scatter.5.cloned.1.call-start = ((), (), s32[]{:S(2)}) async-start(), calls=%async_computation.4 | async-start | bytes 18874368 | tf_op jit(solution)/shard_map/reduce_scatter | solution.py:953
  335.3 39.1 %collective-permute-start.17 = (bf16[512,1024]{1,0:T(8,128)(2,1)}, bf16[512,1024]{1,0:T(8,128)(2,1)S(1)}, u32[]{:S(2)}, u32[]{:S(2)}) collective-permute-start(bf16[512,1024]{1,0:T(8,128)(2,1)} %fusion.9), channel_id=1, source_target_pairs={{8,0},{12,4},{9,1},{13,5},{10,2},{14,6},{11,3},{15,7},{24,16},{28,... | collective-permute-start | bytes 3145736 | tf_op jit(solution)/shard_map/ppermute | solution.py:395
  339.3 57.1 %collective-permute-start.18 = (bf16[512,1024]{1,0:T(8,128)(2,1)}, bf16[512,1024]{1,0:T(8,128)(2,1)S(1)}, u32[]{:S(2)}, u32[]{:S(2)}) collective-permute-start(bf16[512,1024]{1,0:T(8,128)(2,1)} %fusion.8), channel_id=1, source_target_pairs={{8,0},{12,4},{9,1},{13,5},{10,2},{14,6},{11,3},{15,7},{24,16},{28,... | collective-permute-start | bytes 3145736 | tf_op jit(solution)/shard_map/ppermute | solution.py:395
  347.1 50.3 %copy-start.48 = (bf16[512,512]{1,0:T(8,128)(2,1)S(1)}, bf16[512,512]{1,0:T(8,128)(2,1)}, u32[]{:S(2)}) copy-start(bf16[512,512]{1,0:T(8,128)(2,1)} %copy-done.47) | copy-start | bytes 1572868
  439.5 8.6 %collective-permute-start.22 = (bf16[1056,2048]{1,0:T(8,128)(2,1)}, bf16[1056,2048]{1,0:T(8,128)(2,1)}, u32[]{:S(2)}, u32[]{:S(2)}) collective-permute-start(bf16[1056,2048]{1,0:T(8,128)(2,1)} %weight_grad.2), channel_id=1, source_target_pairs={{0,4},{4,0},{8,12},{12,8},{16,20},{20,16},{24,28},{28,24},{1,5},{5... | collective-permute-start | bytes 12976136 | tf_op jit(solution)/shard_map/ppermute | solution.py:817
  439.5 29.8 %collective-permute-start.19 = (bf16[1032,512]{1,0:T(8,128)(2,1)}, bf16[1032,512]{1,0:T(8,128)(2,1)}, u32[]{:S(2)}, u32[]{:S(2)}) collective-permute-start(bf16[1032,512]{1,0:T(8,128)(2,1)} %get-tuple-element.107), channel_id=1, source_target_pairs={{0,1},{1,2},{2,3},{3,0},{4,5},{5,6},{6,7},{7,4},{8,9},{9,10},{10,1... | collective-permute-start | bytes 3170312 | tf_op jit(solution)/shard_map/ppermute | solution.py:59
  441.7 72.7 %collective-permute-start.20 = (bf16[1032,512]{1,0:T(8,128)(2,1)}, bf16[1032,512]{1,0:T(8,128)(2,1)}, u32[]{:S(2)}, u32[]{:S(2)}) collective-permute-start(bf16[1032,512]{1,0:T(8,128)(2,1)} %get-tuple-element.108), channel_id=1, source_target_pairs={{0,2},{1,3},{2,0},{3,1},{4,6},{5,7},{6,4},{7,5},{8,10},{9,11},{10,... | collective-permute-start | bytes 3170312 | tf_op jit(solution)/shard_map/ppermute | solution.py:59
  445.3 69.1 %collective-permute-start.21 = (bf16[1032,512]{1,0:T(8,128)(2,1)}, bf16[1032,512]{1,0:T(8,128)(2,1)}, u32[]{:S(2)}, u32[]{:S(2)}) collective-permute-start(bf16[1032,512]{1,0:T(8,128)(2,1)} %get-tuple-element.109), channel_id=1, source_target_pairs={{0,3},{1,0},{2,1},{3,2},{4,7},{5,4},{6,5},{7,6},{8,11},{9,8},{10,9... | collective-permute-start | bytes 3170312 | tf_op jit(solution)/shard_map/ppermute | solution.py:59
  451.7 62.7 %copy-start.30 = (bf16[1032,512]{1,0:T(8,128)(2,1)S(1)}, bf16[1032,512]{1,0:T(8,128)(2,1)}, u32[]{:S(2)}) copy-start(bf16[1032,512]{1,0:T(8,128)(2,1)} %copy-done.29) | copy-start | bytes 3170308
  461.5 55.4 %collective-permute-start.23 = (bf16[264,2048]{1,0:T(8,128)(2,1)S(1)}, bf16[264,2048]{1,0:T(8,128)(2,1)S(1)}, u32[]{:S(2)}, u32[]{:S(2)}) collective-permute-start(bf16[264,2048]{1,0:T(8,128)(2,1)S(1)} %get-tuple-element.117), channel_id=1, source_target_pairs={{0,8},{4,12},{8,0},{12,4},{16,24},{20,28},{24,16},{28,20},{1,9},{5... | collective-permute-start | bytes 3244040 | tf_op jit(solution)/shard_map/ppermute | solution.py:822
  461.5 55.3 %collective-permute-start.24 = (bf16[264,2048]{1,0:T(8,128)(2,1)S(1)}, bf16[264,2048]{1,0:T(8,128)(2,1)S(1)}, u32[]{:S(2)}, u32[]{:S(2)}) collective-permute-start(bf16[264,2048]{1,0:T(8,128)(2,1)S(1)} %get-tuple-element.118), channel_id=1, source_target_pairs={{0,16},{4,20},{8,24},{12,28},{16,0},{20,4},{24,8},{28,12},{1,17},{... | collective-permute-start | bytes 3244040 | tf_op jit(solution)/shard_map/ppermute | solution.py:822
  469.3 61.9 %collective-permute-start.25 = (bf16[264,2048]{1,0:T(8,128)(2,1)S(1)}, bf16[264,2048]{1,0:T(8,128)(2,1)S(1)}, u32[]{:S(2)}, u32[]{:S(2)}) collective-permute-start(bf16[264,2048]{1,0:T(8,128)(2,1)S(1)} %get-tuple-element.119), channel_id=1, source_target_pairs={{0,24},{4,28},{8,16},{12,20},{16,8},{20,12},{24,0},{28,4},{1,25},{... | collective-permute-start | bytes 3244040 | tf_op jit(solution)/shard_map/ppermute | solution.py:822
  532.0 19.3 %collective-permute-start.28 = (f32[8,128]{1,0:T(8,128)S(1)}, f32[8,128]{1,0:T(8,128)S(1)}, u32[]{:S(2)}, u32[]{:S(2)}) collective-permute-start(f32[8,128]{1,0:T(8,128)S(1)} %bitcast.120), channel_id=1, source_target_pairs={{0,3},{1,0},{2,1},{3,2},{4,7},{5,4},{6,5},{7,6},{8,11},{9,8},{10,9... | collective-permute-start | bytes 12296 | tf_op jit(solution)/shard_map/ppermute | solution.py:834
  541.3 9.9 %collective-permute-start.27 = (f32[8,128]{1,0:T(8,128)S(1)}, f32[8,128]{1,0:T(8,128)S(1)}, u32[]{:S(2)}, u32[]{:S(2)}) collective-permute-start(f32[8,128]{1,0:T(8,128)S(1)} %bitcast.121), channel_id=1, source_target_pairs={{0,2},{1,3},{2,0},{3,1},{4,6},{5,7},{6,4},{7,5},{8,10},{9,11},{10,... | collective-permute-start | bytes 12296 | tf_op jit(solution)/shard_map/ppermute | solution.py:834
  542.2 9.0 %collective-permute-start.26 = (f32[8,128]{1,0:T(8,128)S(1)}, f32[8,128]{1,0:T(8,128)S(1)}, u32[]{:S(2)}, u32[]{:S(2)}) collective-permute-start(f32[8,128]{1,0:T(8,128)S(1)} %bitcast.122), channel_id=1, source_target_pairs={{0,1},{1,2},{2,3},{3,0},{4,5},{5,6},{6,7},{7,4},{8,9},{9,10},{10,1... | collective-permute-start | bytes 12296 | tf_op jit(solution)/shard_map/ppermute | solution.py:834
  (58 other events, 468.7 us)
Sparse Core Ops, SparseCore 0:
  11.3 93.2 all-gather.7
  135.8 60.4 all-gather.9
  205.6 57.0 all-gather.5
  281.6 91.1 reduce-scatter.2
  376.6 157.4 reduce-scatter.4

commit v3 on v2

--- a/solution.py
+++ b/solution.py
@@ -11,8 +11,10 @@
 ROTARY = 64
 F32 = jnp.float32
 BF16 = jnp.bfloat16
-VMEM_LIMIT = 40 << 20
-SHARE = 1
+VMEM_LIMIT = 56 << 20
+HEADS_WEIGHT = 1.0
+FEED_WEIGHT = 1.0
+LAST_WEIGHT = 1.0
 NN = (((1,), (0,)), ((), ()))
 NT = (((1,), (1,)), ((), ()))
 TN = (((0,), (0,)), ((), ()))
@@ -32,25 +34,29 @@
     )
 
 
-def cost(flops, moved, transcendentals=0):
+def cost(flops, moved, weight=1.0):
     return pl.CostEstimate(
-        flops=flops // SHARE, bytes_accessed=moved // SHARE, transcendentals=0
-    )
-
-
-def line_gather(piece, axis):
+        flops=int(flops * weight), bytes_accessed=int(moved * weight), transcendentals=0
+    )
+
+
+def line_gather(piece, axis, first=None, gate=None):
     size = lax.axis_size(axis)
     up = [(i, i + 1) for i in range(size - 1)]
     down = [(i + 1, i) for i in range(size - 1)]
     right, left = [], []
     a = b = piece
-    for _ in range(size - 1):
-        a = lax.ppermute(a, axis, up)
-        b = lax.ppermute(b, axis, down)
+    for step in range(size - 1):
+        if step == 2 and gate is not None:
+            a, b = after((a, b), gate)
+        if step == 0 and first is not None:
+            a, b = first
+        else:
+            a = lax.ppermute(a, axis, up)
+            b = lax.ppermute(b, axis, down)
         right.append(a)
         left.append(b)
-    pairs = [(right[s - 1], left[size - s - 1]) for s in range(1, size)]
-    return pairs, list(zip(right, left))
+    return [(right[s - 1], left[size - s - 1]) for s in range(1, size)]
 
 
 def send_chunks(chunks, axis):
@@ -238,19 +244,6 @@
     )(rows, pack, jnp.broadcast_to(bias.reshape(1, -1), (8, bias.size)), table)
 
 
-def visit(slot, local_len, half, block, place, length):
-    first_key = block * local_len
-    last_query = place * local_len + (half + 1) * (local_len // 2) - 1
-    return (block >= 0) & (first_key <= last_query) & (first_key < length)
-
-
-def masked(scores, first_key, first_query, length, axis_key):
-    shape = scores.shape
-    key = first_key + lax.broadcasted_iota(jnp.int32, shape, axis_key)
-    query = first_query + lax.broadcasted_iota(jnp.int32, shape, 1 - axis_key)
-    return (key <= query) & (key < length)
-
-
 SLOTS = 4
 
 
@@ -258,133 +251,170 @@
     return [own_ref, below_ref, both_ref.at[0], both_ref.at[1]]
 
 
-def forward_kernel(slots, local_len, seq, info, lens, query_ref, pair_ref, *refs):
-    context_ref, lse_ref, top, total, acc = refs
+def masked(scores, slot, first_key, first_query, length):
+    keys = first_key + lax.broadcasted_iota(jnp.int32, (1, scores.shape[1]), 1)
+    ok = keys < length
+    if slot == 0:
+        queries = first_query + lax.broadcasted_iota(jnp.int32, (scores.shape[0], 1), 0)
+        ok = ok & (keys <= queries)
+    return jnp.where(ok, scores, -1e30)
+
+
+def forward_kernel(heads, seq, info, lens, query_ref, pair_ref, context_ref, lse_ref, *scratch):
+    local_len = query_ref.shape[0]
     length = lens[seq]
-    place = info[slots]
-    top[...] = jnp.full_like(top, -1e30)
-    total[...] = jnp.zeros_like(total)
-    acc[...] = jnp.zeros_like(acc)
-    query = query_ref[...]
-    for slot in range(slots):
+    place = info[SLOTS]
+    top, total, acc = scratch[:heads], scratch[heads : 2 * heads], scratch[2 * heads :]
+    for slot in range(SLOTS):
         block = info[slot]
         first_key = block * local_len
 
         @pl.when((block >= 0) & (block <= place) & (first_key < length))
         def _():
-            keys = pair_ref[block, :, :HEAD]
-            vals = pair_ref[block, :, HEAD:]
-            scores = dot(query, keys, NT)
-            ok = masked(scores, first_key, place * local_len, length, 1)
-            scores = jnp.where(ok, scores, -1e30)
-            best = jnp.maximum(top[...], jnp.max(scores, axis=1, keepdims=True))
-            scale = jnp.exp(top[...] - best)
-            weights = jnp.exp(scores - best[:, :1])
-            weights = jnp.where(ok, weights, 0.0)
-            total[...] = total[...] * scale + jnp.sum(weights, axis=1, keepdims=True)
-            acc[...] = acc[...] * scale[:, :1] + dot(weights.astype(BF16), vals, NN)
-            top[...] = best
-
-    context_ref[...] = (acc[...] / total[:, :1]).astype(BF16)
-    lse_ref[...] = top[...] + jnp.log(total[...])
+            for head in range(heads):
+                at = 2 * HEAD * head
+                query = query_ref[:, HEAD * head : HEAD * (head + 1)]
+                keys = pair_ref[block, :, at : at + HEAD]
+                vals = pair_ref[block, :, at + HEAD : at + 2 * HEAD]
+                scores = dot(query, keys, NT)
+                scores = masked(scores, slot, first_key, place * local_len, length)
+                best = jnp.max(scores, axis=1, keepdims=True)
+                if slot > 0:
+                    best = jnp.maximum(best, top[head][...])
+                weights = jnp.exp(scores - best)
+                summed = jnp.sum(weights, axis=1, keepdims=True)
+                mixed = dot(weights.astype(BF16), vals, NN)
+                if slot > 0:
+                    scale = jnp.exp(top[head][...] - best)
+                    summed = summed + total[head][...] * scale
+                    mixed = mixed + acc[head][...] * scale
+                top[head][...] = best
+                total[head][...] = summed
+                acc[head][...] = mixed
+
+        if slot == 0:
+
+            @pl.when(first_key >= length)
+            def _():
+                for head in range(heads):
+                    top[head][...] = jnp.full_like(top[head], -1e30)
+                    total[head][...] = jnp.zeros_like(total[head])
+                    acc[head][...] = jnp.zeros_like(acc[head])
+
+    for head in range(heads):
+        cols = slice(HEAD * head, HEAD * (head + 1))
+        context_ref[:, cols] = (acc[head][...] / total[head][...]).astype(BF16)
+        lse = top[head][...] + jnp.log(total[head][...])
+        lse_ref[:, 128 * head : 128 * (head + 1)] = jnp.broadcast_to(lse, (local_len, 128))
 
 
 def forward_call(info, lengths, query, pairs, seq, heads):
     local_len = pairs.shape[2]
-    slots = SLOTS
-    return pl.pallas_call(
-        functools.partial(forward_kernel, slots, local_len, seq),
+    return pl.pallas_call(
+        functools.partial(forward_kernel, heads, seq),
         grid_spec=pltpu.PrefetchScalarGridSpec(
             num_scalar_prefetch=2,
-            grid=(heads,),
-            in_specs=[pl.BlockSpec((local_len, HEAD), lambda h, *_: (seq, h))]
-            + [pl.BlockSpec((slots, None, local_len, 2 * HEAD), lambda h, *_: (0, seq, 0, h))],
+            grid=(1,),
+            in_specs=[
+                pl.BlockSpec((local_len, heads * HEAD), lambda i, *_: (seq, 0)),
+                pl.BlockSpec(
+                    (SLOTS, None, local_len, 2 * heads * HEAD), lambda i, *_: (0, seq, 0, 0)
+                ),
+            ],
             out_specs=[
-                pl.BlockSpec((local_len, HEAD), lambda h, *_: (0, h)),
-                pl.BlockSpec((local_len, 128), lambda h, *_: (0, h)),
+                pl.BlockSpec((local_len, heads * HEAD), lambda i, *_: (0, 0)),
+                pl.BlockSpec((local_len, heads * 128), lambda i, *_: (0, 0)),
             ],
-            scratch_shapes=[
-                pltpu.VMEM((local_len, 128), F32),
-                pltpu.VMEM((local_len, 128), F32),
-                pltpu.VMEM((local_len, HEAD), F32),
-            ],
+            scratch_shapes=[pltpu.VMEM((local_len, 1), F32)] * (2 * heads)
+            + [pltpu.VMEM((local_len, HEAD), F32)] * heads,
         ),
         out_shape=[
             jax.ShapeDtypeStruct((local_len, heads * HEAD), BF16),
             jax.ShapeDtypeStruct((local_len, heads * 128), F32),
         ],
         compiler_params=params("arbitrary"),
-        cost_estimate=cost(
-            4 * local_len * heads * HEAD * local_len * slots,
-            4 * local_len * heads * HEAD * slots,
-        ),
+        cost_estimate=cost(4 * local_len * heads * HEAD * local_len * SLOTS,
+            4 * local_len * heads * HEAD * SLOTS, HEADS_WEIGHT),
         name="attention_forward",
     )(info, lengths, query, pairs)
 
 
 def backward_kernel(
-    slots, local_len, seq, info, lens, query_ref, context_ref, grad_ref, lse_ref, pair_ref, *refs
+    heads, seq, info, lens, query_ref, context_ref, grad_ref, lse_ref, pair_ref, query_out, *refs
 ):
-    query_out = refs[0]
-    pair_outs = slot_refs(*refs[1:4])
-    acc = refs[4]
+    local_len = query_ref.shape[0]
+    pair_outs = slot_refs(*refs[:3])
+    accs = refs[3:]
     length = lens[seq]
-    place = info[slots]
-    query = query_ref[...]
-    grad = grad_ref[...]
-    lse = lse_ref[:, :1]
-    shared = jnp.sum(grad.astype(F32) * context_ref[...].astype(F32), axis=1, keepdims=True)
-    acc[...] = jnp.zeros_like(acc)
-    for slot in range(slots):
+    place = info[SLOTS]
+    for slot in range(SLOTS):
         block = info[slot]
         first_key = block * local_len
         seen = (block >= 0) & (block <= place) & (first_key < length)
 
         @pl.when(seen)
         def _():
-            keys = pair_ref[block, :, :HEAD]
-            vals = pair_ref[block, :, HEAD:]
-            scores = dot(query, keys, NT)
-            ok = masked(scores, first_key, place * local_len, length, 1)
-            probs = jnp.where(ok, jnp.exp(scores - lse), 0.0)
-            prob_grad = dot(grad, vals, NT)
-            score_grad = (probs * (prob_grad - shared)).astype(BF16)
-            acc[...] += dot(score_grad, keys, NN)
-            pair_outs[slot][:, :HEAD] = dot(score_grad, query, TN).astype(BF16)
-            pair_outs[slot][:, HEAD:] = dot(probs.astype(BF16), grad, TN).astype(BF16)
+            for head in range(heads):
+                at = 2 * HEAD * head
+                cols = slice(HEAD * head, HEAD * (head + 1))
+                query, grad = query_ref[:, cols], grad_ref[:, cols]
+                keys = pair_ref[block, :, at : at + HEAD]
+                vals = pair_ref[block, :, at + HEAD : at + 2 * HEAD]
+                shared = grad.astype(F32) * context_ref[:, cols].astype(F32)
+                shared = jnp.sum(shared, axis=1, keepdims=True)
+                scores = dot(query, keys, NT)
+                scores = masked(scores, slot, first_key, place * local_len, length)
+                probs = jnp.exp(scores - lse_ref[:, 128 * head : 128 * head + 1])
+                score_grad = (probs * (dot(grad, vals, NT) - shared)).astype(BF16)
+                pair_outs[slot][:, at : at + HEAD] = dot(score_grad, query, TN).astype(BF16)
+                pair_outs[slot][:, at + HEAD : at + 2 * HEAD] = dot(
+                    probs.astype(BF16), grad, TN
+                ).astype(BF16)
+                mixed = dot(score_grad, keys, NN)
+                accs[head][...] = mixed if slot == 0 else accs[head][...] + mixed
 
         @pl.when(jnp.logical_not(seen))
         def _():
             pair_outs[slot][...] = jnp.zeros_like(pair_outs[slot])
-
-    query_out[...] = (acc[...] * HEAD ** (-0.5)).astype(BF16)
+            if slot == 0:
+                for head in range(heads):
+                    accs[head][...] = jnp.zeros_like(accs[head])
+
+    for head in range(heads):
+        query_out[:, HEAD * head : HEAD * (head + 1)] = (
+            accs[head][...] * HEAD ** (-0.5)
+        ).astype(BF16)
 
 
 def backward_call(info, lengths, query, context, grad, lse, pairs, seq, heads):
     local_len = pairs.shape[2]
-    slots = SLOTS
-    here = pl.BlockSpec((local_len, HEAD), lambda h, *_: (seq, h))
-    one = pl.BlockSpec((local_len, HEAD), lambda h, *_: (0, h))
-    two = [pl.BlockSpec((local_len, 2 * HEAD), lambda h, *_: (0, h))] * 2
-    two = two + [pl.BlockSpec((2, local_len, 2 * HEAD), lambda h, *_: (0, 0, h))]
-    return pl.pallas_call(
-        functools.partial(backward_kernel, slots, local_len, seq),
+    here = pl.BlockSpec((local_len, heads * HEAD), lambda i, *_: (seq, 0))
+    one = pl.BlockSpec((local_len, heads * HEAD), lambda i, *_: (0, 0))
+    two = [pl.BlockSpec((local_len, 2 * heads * HEAD), lambda i, *_: (0, 0))] * 2
+    two = two + [pl.BlockSpec((2, local_len, 2 * heads * HEAD), lambda i, *_: (0, 0, 0))]
+    return pl.pallas_call(
+        functools.partial(backward_kernel, heads, seq),
         grid_spec=pltpu.PrefetchScalarGridSpec(
             num_scalar_prefetch=2,
-            grid=(heads,),
-            in_specs=[here, one, here, pl.BlockSpec((local_len, 128), lambda h, *_: (0, h))]
-            + [pl.BlockSpec((slots, None, local_len, 2 * HEAD), lambda h, *_: (0, seq, 0, h))],
+            grid=(1,),
+            in_specs=[
+                here,
+                one,
+                here,
+                pl.BlockSpec((local_len, heads * 128), lambda i, *_: (0, 0)),
+                pl.BlockSpec(
+                    (SLOTS, None, local_len, 2 * heads * HEAD), lambda i, *_: (0, seq, 0, 0)
+                ),
+            ],
             out_specs=[one] + two,
-            scratch_shapes=[pltpu.VMEM((local_len, HEAD), F32)],
+            scratch_shapes=[pltpu.VMEM((local_len, HEAD), F32)] * heads,
         ),
         out_shape=[jax.ShapeDtypeStruct((local_len, heads * HEAD), BF16)]
         + [jax.ShapeDtypeStruct((local_len, 2 * heads * HEAD), BF16)] * 2
         + [jax.ShapeDtypeStruct((2, local_len, 2 * heads * HEAD), BF16)],
         compiler_params=params("arbitrary"),
-        cost_estimate=cost(
-            10 * local_len * heads * HEAD * local_len * slots,
-            8 * local_len * heads * HEAD * slots,
-        ),
+        cost_estimate=cost(10 * local_len * heads * HEAD * local_len * SLOTS,
+            8 * local_len * heads * HEAD * SLOTS, HEADS_WEIGHT),
         name="attention_backward",
     )(info, lengths, query, context, grad, lse, pairs)
 
@@ -419,7 +449,7 @@
         out_specs=pl.BlockSpec((count, tile), lambda j: (0, j)),
         out_shape=jax.ShapeDtypeStruct((count, width), BF16),
         compiler_params=params("arbitrary"),
-        cost_estimate=cost(2 * count * width * (hidden + inside), 2 * width * (hidden + inside)),
+        cost_estimate=cost(2 * count * width * (hidden + inside), 2 * width * (hidden + inside), HEADS_WEIGHT),
         name="branch",
     )(active, *contexts, outer, pack)
 
@@ -460,6 +490,38 @@
     )(rows, pack, jnp.broadcast_to(bias.reshape(1, -1), (8, hidden)))
 
 
+def upper_grad_kernel(rows_ref, weight_ref, slope_ref, out_ref, sum_ref):
+    grad = dot(rows_ref[...], weight_ref[...], NN) * slope_ref[...].astype(F32)
+    low = grad.astype(BF16)
+    out_ref[...] = low
+    sum_ref[...] = jnp.broadcast_to(
+        jnp.sum(low.astype(F32), axis=0, keepdims=True), sum_ref.shape
+    )
+
+
+def upper_grad_call(rows, weight, slope, tile=512):
+    count, width = rows.shape
+    hidden = weight.shape[1]
+    out = pl.BlockSpec((count, tile), lambda j: (0, j))
+    return pl.pallas_call(
+        upper_grad_kernel,
+        grid=(hidden // tile,),
+        in_specs=[
+            pl.BlockSpec((count, width), lambda j: (0, 0)),
+            pl.BlockSpec((width, tile), lambda j: (0, j)),
+            out,
+        ],
+        out_specs=[out, pl.BlockSpec((8, tile), lambda j: (0, j))],
+        out_shape=[
+            jax.ShapeDtypeStruct((count, hidden), BF16),
+            jax.ShapeDtypeStruct((8, hidden), F32),
+        ],
+        compiler_params=params("arbitrary"),
+        cost_estimate=cost(2 * count * width * hidden, 2 * width * (2 * count + hidden), FEED_WEIGHT),
+        name="upper_grad",
+    )(rows, weight, slope)
+
+
 def context_grad_kernel(rows_ref, weight_ref, out_ref):
     out_ref[...] = dot(rows_ref[...], flat_rows(weight_ref), NN).astype(BF16)
 
@@ -478,7 +540,7 @@
         out_specs=pl.BlockSpec((tile, inside), lambda i: (i, 0)),
         out_shape=jax.ShapeDtypeStruct((count, inside), BF16),
         compiler_params=params("arbitrary"),
-        cost_estimate=cost(2 * count * width * inside, 2 * width * (count + inside)),
+        cost_estimate=cost(2 * count * width * inside, 2 * width * (count + inside), HEADS_WEIGHT),
         name="context_grad",
     )(rows, pack)
 
@@ -520,7 +582,7 @@
             jax.ShapeDtypeStruct((8, width), F32),
         ],
         compiler_params=params("arbitrary"),
-        cost_estimate=cost(2 * count * width * hidden, 2 * (width * hidden + 3 * count * width)),
+        cost_estimate=cost(2 * count * width * hidden, 2 * (width * hidden + 3 * count * width), LAST_WEIGHT),
         name="second_in_grad",
     )(grad, pack, rows, stats, gains)
 
@@ -567,7 +629,7 @@
             jax.ShapeDtypeStruct((8, width), F32),
         ],
         compiler_params=params(),
-        cost_estimate=cost(10 * count * width, 10 * count * width),
+        cost_estimate=cost(10 * count * width, 10 * count * width, LAST_WEIGHT),
         name="joined_grad",
     )(*flat, table)
 
@@ -638,7 +700,7 @@
         out_shape=[jax.ShapeDtypeStruct((count + EXTRA, tile), BF16)] * ranks
         + [jax.ShapeDtypeStruct((8, width), F32)],
         compiler_params=params("arbitrary"),
-        cost_estimate=cost(2 * count * width * inside, 2 * (width * inside + 4 * count * width)),
+        cost_estimate=cost(2 * count * width * inside, 2 * (width * inside + 4 * count * width), LAST_WEIGHT),
         name="first_in_grad",
     )(order, grad, pack, rows, stats, gains, second)
 
@@ -743,9 +805,7 @@
         ),
         out_shape=[jax.ShapeDtypeStruct((deep, total), BF16)] * outs,
         compiler_params=params("arbitrary"),
-        cost_estimate=cost(
-            8 * rows * count * total, 2 * (count * (4 * rows + total) + 8 * rows * total)
-        ),
+        cost_estimate=cost(8 * rows * count * total, 2 * (count * (4 * rows + total) + 8 * rows * total), LAST_WEIGHT),
         name="weight_grad",
     )(
         order,
@@ -794,7 +854,7 @@
         out_shape=jax.ShapeDtypeStruct((width, total), BF16),
         scratch_shapes=[pltpu.VMEM((width, count), BF16)],
         compiler_params=params("arbitrary"),
-        cost_estimate=cost(2 * width * count * total, 2 * (count * (width + total) + width * total)),
+        cost_estimate=cost(2 * width * count * total, 2 * (count * (width + total) + width * total), FEED_WEIGHT),
         name="product",
     )(*[lhs for lhs, _ in pairs], *[rhs for _, rhs in pairs])
 
@@ -869,12 +929,16 @@
     flat = jnp.concatenate(vectors + [joined_bias.reshape(-1), inner_bias.reshape(-1)])
     small = gather_small(jnp.pad(flat, (0, -flat.size % 256)), group)
     shard = jnp.concatenate(
-        [joined_weight.reshape(rows_part, -1), output_weight.reshape(rows_part, -1), inner_weight],
-        axis=1,
-    )
-    token_pairs, _ = line_gather(own_tokens, "tp")
-    cot_pairs, cot_steps = line_gather(after(own_cot, token_pairs), "tp")
+        [joined_weight.reshape(rows_part, -1), output_weight.reshape(rows_part, -1)], axis=1
+    )
+    token_pairs = line_gather(own_tokens, "tp")
+    cot_start = after(own_cot, token_pairs)
+    cot_first = (
+        lax.ppermute(cot_start, "tp", [(i, i + 1) for i in range(ranks - 1)]),
+        lax.ppermute(cot_start, "tp", [(i + 1, i) for i in range(ranks - 1)]),
+    )
     pack = lax.all_gather(shard, group, axis=0, tiled=False)
+    inner = lax.all_gather(inner_weight, group, axis=0, tiled=False)
 
     small = small.astype(F32)
     whole = [small[:, i * rows_part : (i + 1) * rows_part].reshape(width) for i in range(6)]
@@ -908,25 +972,24 @@
     table = jnp.concatenate(
         [cosine, cosine, ones, -sine, nothing, blank, nothing, sine, blank], axis=1
     )
-    query, pair = joined_call(after(first_in, cot_steps[0]), pack, whole_joined_bias, table, seqs, heads)
+    query, pair = joined_call(after(first_in, cot_first), pack, whole_joined_bias, table, seqs, heads)
     pairs = lax.all_gather(pair, "ctx", axis=0, tiled=False)
     low, odd = ctx - 2, ctx + 1 - 2 * lax.rem(ctx, 2)
     info = jnp.stack([ctx, low, odd, jnp.where(low >= 0, odd - 2, -1), ctx]).astype(jnp.int32)
-    active, slope = upper_call(
-        after(second_in, query, cot_steps[1:]), pack, whole_inner_bias, joined_width + inside
-    )
-    outer = lax.all_gather(after(outer_weight, active, pairs), group, axis=0, tiled=True)
+    active, slope = upper_call(after(second_in, query), inner, whole_inner_bias, 0)
+    cot_pairs = line_gather(cot_start, "tp", cot_first, active)
+    grad_rows, bias_sums = cot_call(places, after(lengths, active), own_cot, cot_pairs, local_len)
+    bias_grad = bias_sums[0]
+    outer = lax.all_gather(after(outer_weight, grad_rows, pairs), group, axis=0, tiled=True)
     contexts, lses = [], []
-    ready = after(query, active)
+    ready = after(query, grad_rows)
     for seq in range(seqs):
         context, lse = forward_call(info, lengths, ready, pairs, seq, heads)
         ready = after(query, context)
         contexts.append(context)
         lses.append(lse)
 
-    grad_rows, bias_sums = cot_call(places, after(lengths, context), own_cot, cot_pairs, local_len)
-    bias_grad = bias_sums[0]
-    context_grad = context_grad_call(grad_rows, pack, joined_width // inside, inside)
+    context_grad = context_grad_call(after(grad_rows, ready), pack, joined_width // inside, inside)
     queries, sums = [], []
     for seq in range(seqs):
         query_grad, *pair_grads = backward_call(
@@ -946,15 +1009,15 @@
     valid = (positions[None, :] < lengths[:, None]).astype(F32).reshape(count, 1)
     layer_out = (valid * (own_tokens.astype(F32) + summed + own_bias)).astype(BF16)
 
-    grad_late = after(grad_rows, branch)
-    upper_grad = (dot(grad_late, outer, NN) * slope.astype(F32)).astype(BF16)
-    inner_bias_grad = jnp.sum(upper_grad, axis=0, dtype=F32)
-    feed = product_call([(after(grad_late, upper_grad), active), (second_in, upper_grad)])
-    feed_out = lax.psum_scatter(feed, group, scatter_dimension=0, tiled=True)
+    outer_whole = product_call([(after(grad_rows, branch), active)])
+    outer_out = lax.psum_scatter(outer_whole, group, scatter_dimension=0, tiled=True)
+    grad_late = after(grad_rows, outer_whole)
+    upper_grad, upper_sums = upper_grad_call(grad_late, outer, slope)
+    inner_bias_grad = upper_sums[0]
     second_scaled, second_sums = second_call(
-        after(upper_grad, feed),
-        pack,
-        (joined_width + inside) // hidden,
+        upper_grad,
+        inner,
+        0,
         rows,
         stats,
         gains,
@@ -967,6 +1030,9 @@
     *scaled, first_sums = first_call(
         order, joined_grad, pack, rows, stats, gains, second_scaled, ranks
     )
+
+    inner_whole = product_call([(after(second_in, scaled[0]), upper_grad)])
+    inner_out = lax.psum_scatter(inner_whole, group, scatter_dimension=0, tiled=True)
 
     column = jnp.concatenate([first_sums[:2], second_sums[:2], bias_grad.reshape(1, -1)])
     by_shard = [
@@ -985,11 +1051,22 @@
             ((0, 0), (0, EXTRA - 1), (0, size - small_grads.shape[1])),
         )
     context = jnp.concatenate(contexts, axis=0)
-    head_pairs = [(after(first_in, scaled[0]), joined_grad), (grad_rows, context)]
+    head_pairs = [(after(first_in, inner_whole), joined_grad), (grad_rows, context)]
     head_given = weight_grad_given(head_pairs, group, riders)
     head_pairs = [(after(first_in, head_given), joined_grad), (grad_rows, context)]
     head_terms = weight_grad_kept(head_pairs, head_given, group, riders)
-    head_out, feed_out = total_of(head_terms), feed_out.astype(F32)
+    share = total_of(send_chunks(scaled, "tp"))
+    lines = 2 * count // part
+    means = share[count : count + lines].reshape(2, count) / width
+    share = share[:count]
+    own_normed = (own_tokens.astype(F32) - center) * inverse
+    own_rows = lax.dynamic_slice_in_dim(grad_rows, own_start, part, 1).astype(F32)
+    tokens_grad = own_rows + inverse * (
+        share - means[0][:, None] - own_normed * means[1][:, None]
+    )
+
+    head_terms = [head_terms[0]] + [after(t, tokens_grad) for t in head_terms[1:]]
+    head_out = total_of(head_terms)
     if riders is None:
         small_out = lax.psum_scatter(small_grads, group, scatter_dimension=0, tiled=True)[0]
     else:
@@ -1000,16 +1077,6 @@
     at += joined_bias.size
     inner_bias_out = small_out[at : at + inner_bias.size].reshape(inner_bias.shape)
     bias_out = small_out[4 * rows_part : 5 * rows_part]
-
-    share = total_of(send_chunks(scaled, "tp"))
-    lines = 2 * count // part
-    means = share[count : count + lines].reshape(2, count) / width
-    share = share[:count]
-    own_normed = (own_tokens.astype(F32) - center) * inverse
-    own_rows = lax.dynamic_slice_in_dim(grad_rows, own_start, part, 1).astype(F32)
-    tokens_grad = own_rows + inverse * (
-        share - means[0][:, None] - own_normed * means[1][:, None]
-    )
 
     return (
         layer_out.reshape(tokens.shape),
@@ -1022,9 +1089,9 @@
         bias_out,
         vector[2],
         vector[3],
-        feed_out[:, hidden:],
+        inner_out.astype(F32),
         inner_bias_out,
-        feed_out[:, :hidden],
+        outer_out.astype(F32),
         bias_out,
     )
 

time: 578 us -> 540 us (0.934)
  local copies, waits for them, and re-layouts: 87.6 us -> 22.9 us
  Pallas kernels: 155 us -> 210 us
  waiting for transfers between devices: 201 us -> 160 us
  starting transfers between devices: 69.5 us -> 101 us
  matrix products: 14.9 us -> 0 us
    unnamed x160 -> x80, local copies, waits for them, and re-layouts: 67.4 us -> 6.33 us
    pallas_call x4 -> x5, Pallas kernels: 20 us -> 44.9 us  [the longest x2 16.8 us: backward_call(): pl.pallas_call(functools.partial(backward_kernel, heads, seq), grid_spec=...]
    ppermute x3, starting transfers between devices: 10.3 us -> 27.4 us  [line_sum(): lax.ppermute(value, axis, [(i, (i + step) % size) for i in range(size)])]
    ppermute x3, starting transfers between devices: 0.14 us -> 15.1 us  [weight_grad_kept(): lax.ppermute(part, group, flips(8, by))]
    dot_general x1 -> x0, matrix products: 14.9 us -> none  [dot(): return lax.dot_general(a, b, dims, preferred_element_type=F32)]
    ppermute x2, waiting for transfers between devices: 33.8 us -> 19.1 us  [return_pairs(): above = lax.ppermute(lower, axis, [(2, 0), (3, 1)])]
    ppermute x3, waiting for transfers between devices: 52.8 us -> 38.3 us  [send_chunks(): lax.ppermute(chunks[k], axis, [(i, (i + k) % size) for i in range(size)])]
    ppermute x6 -> x5, waiting for transfers between devices: 82 us -> 69.1 us  [line_gather(): b = lax.ppermute(b, axis, down)]
  transfers between devices with their start and end apart: 34 -> 36, of which waited for: 18 -> 21; matrix products, arithmetic and copies ran while one was open for 9% -> 7% of each run, Pallas kernels for 23% -> 37%
where the time goes in v3:
time: 540 us; the launch traced here: 530 us
  Pallas kernels  210 us (39%)
  waiting for transfers between devices  160 us (30%)
  starting transfers between devices  101 us (19%)
  local copies, waits for them, and re-layouts  22.9 us (4%)
  other arithmetic  21.5 us (4%)
  between operations  15.1 us (3%)
    ppermute x5, waiting for transfers between devices, line_gather(): b = lax.ppermute(b, axis, down)  69.1 us
    ppermute x3, waiting for transfers between devices, send_chunks(): lax.ppermute(chunks[k], axis, [(i, (i + k) % size) for i in range(size)])  38.3 us
    pallas_call x2, Pallas kernels, product_call(): pl.pallas_call(functools.partial(product_kernel, sizes), grid=(sum(sizes)...  30.2 us
    ppermute x3, starting transfers between devices, line_sum(): lax.ppermute(value, axis, [(i, (i + step) % size) for i in range(size)])  27.4 us
    ppermute x5, starting transfers between devices, line_gather(): a = lax.ppermute(a, axis, up)  25.9 us
    pallas_call x2, Pallas kernels, weight_grad_call(): pl.pallas_call(functools.partial(weight_grad_kernel, sizes, outs, int(sma...  23.7 us
    ppermute x2, waiting for transfers between devices, return_pairs(): above = lax.ppermute(lower, axis, [(2, 0), (3, 1)])  19.1 us
    pallas_call x1, Pallas kernels, upper_call(): pl.pallas_call(upper_kernel, grid=(hidden // tile,), in_specs=[pl.BlockSp...  17.5 us
  transfers between devices with their start and end apart: 36, of which 21 were waited for; matrix products, arithmetic and copies ran while one was open for 7% of the time, Pallas kernels for 37%

profile of v3, /device:TPU:0, one launch (start us, length us, event | category | flops | bytes accessed | tf_op | source)
XLA Modules:
  0.0 529.7 jit_solution(8412471901852528390)
XLA Ops:
  12.8 5.6 %collective-permute-start = (bf16[1024,512]{1,0:T(8,128)(2,1)S(1)}, bf16[1024,512]{1,0:T(8,128)(2,1)S(1)}, u32[]{:S(2)}, u32[]{:S(2)}) collective-permute-start(bf16[1024,512]{1,0:T(8,128)(2,1)S(1)} %bitcast.94), channel_id=1, source_target_pairs={{0,1},{1,2},{2,3},{4,5},{5,6},{6,7},{8,9},{9,10},{10,11},{12,13},{... | collective-permute-start | bytes 3145736 | tf_op jit(solution)/shard_map/ppermute | solution.py:55
  18.4 21.2 %collective-permute-done.1.refs_5_ = bf16[1024,512]{1,0:T(8,128)(2,1)S(1)} collective-permute-done((bf16[1024,512]{1,0:T(8,128)(2,1)S(1)}, bf16[1024,512]{1,0:T(8,128)(2,1)S(1)}, u32[]{:S(2)}, u32[]{:S(2)}) %collective-permute-start.1) | collective-permute-done | bytes 1048608 | tf_op jit(solution)/shard_map/ppermute | solution.py:56
  40.9 4.6 collective-permute-start.4
  45.5 20.4 %collective-permute-done.2.refs_3_ = bf16[1024,512]{1,0:T(8,128)(2,1)} collective-permute-done((bf16[1024,512]{1,0:T(8,128)(2,1)S(1)}, bf16[1024,512]{1,0:T(8,128)(2,1)}, u32[]{:S(2)}, u32[]{:S(2)}) %collective-permute-start.2) | collective-permute-done | bytes 1048608 | tf_op jit(solution)/shard_map/ppermute | solution.py:56
  67.2 5.6 %collective-permute-start.5 = (bf16[1024,512]{1,0:T(8,128)(2,1)S(1)}, bf16[1024,512]{1,0:T(8,128)(2,1)}, u32[]{:S(2)}, u32[]{:S(2)}) collective-permute-start(bf16[1024,512]{1,0:T(8,128)(2,1)S(1)} %collective-permute-done.4.refs_2_), channel_id=1, source_target_pairs={{0,1},{1,2},{2,3},{4,5},{5,6},{6,7},{8,9},{9,10},{10,11},{12,13},{... | collective-permute-start | bytes 3145736 | tf_op jit(solution)/shard_map/ppermute | solution.py:55
  76.2 2.6 collective-permute-done.7
  80.2 11.3 %collective-permute-done.3.refs_1_ = bf16[1024,512]{1,0:T(8,128)(2,1)} collective-permute-done((bf16[1024,512]{1,0:T(8,128)(2,1)}, bf16[1024,512]{1,0:T(8,128)(2,1)}, u32[]{:S(2)}, u32[]{:S(2)}) %collective-permute-start.3) | collective-permute-done | bytes 1048608 | tf_op jit(solution)/shard_map/ppermute | solution.py:56
  93.7 6.2 %collective-permute-start.9 = (bf16[1024,512]{1,0:T(8,128)(2,1)S(1)}, bf16[1024,512]{1,0:T(8,128)(2,1)}, u32[]{:S(2)}, u32[]{:S(2)}) collective-permute-start(bf16[1024,512]{1,0:T(8,128)(2,1)S(1)} %bitcast.100), channel_id=1, source_target_pairs={{0,1},{1,2},{2,3},{4,5},{5,6},{6,7},{8,9},{9,10},{10,11},{12,13},{... | collective-permute-start | bytes 3145736 | tf_op jit(solution)/shard_map/ppermute | solution.py:937
  103.4 11.7 %norm.1 = (bf16[1024,2048]{1,0:T(8,128)(2,1)}, bf16[1024,2048]{1,0:T(8,128)(2,1)}, bf16[1024,2048]{1,0:T(8,128)(2,1)}, f32[1024,128]{1,0:T(8,128)}) custom-call(s32[1]{0:T(128)} %bitcast.1.me_ref, bf16[1024,512]{1,0:T(8,128)(2,1)} %bitcast.92, bf16[1024,512]{1,0:T(8,128)(2,1)} %copy-done.18, bf16[1024,512]{1,0:T(8,128)(2,1)} %collective-permute-done.3.refs_1_, ...), custom_call_target="tpu_custom_call" | custom-call | flops 33554432 | bytes 20971520 | tf_op jit(solution)/shard_map/norm/pallas_call | solution.py:102
  119.2 13.3 %joined.1 = (bf16[1024,512]{1,0:T(8,128)(2,1)}, bf16[2,512,1024]{2,1,0:T(8,128)(2,1)}) custom-call(bf16[1024,2048]{1,0:T(8,128)(2,1)} %get-tuple-element.128.rows_ref.refs_0_.refs_1_.refs_2_.refs_3_, bf16[8,256,2048]{2,1,0:T(8,128)(2,1)} %bitcast.88, f32[8,1536]{1,0:T(8,128)} %broadcast_in_dim.34.bias_ref, f32[512,384]{1,0:T(8,128)} %concatenate.35.table_ref.refs_8_), custom_call_target="tpu_custom_call" | custom-call | flops 6442450944 | bytes 10485760 | tf_op jit(solution)/shard_map/joined/pallas_call | solution.py:220
  133.9 5.2 collective-permute-start.11
  140.5 17.5 %upper.1 = (bf16[1024,2048]{1,0:T(8,128)(2,1)}, bf16[1024,2048]{1,0:T(8,128)(2,1)}) custom-call(bf16[1024,2048]{1,0:T(8,128)(2,1)} %get-tuple-element.121.rows_ref.refs_0_, bf16[8,256,2048]{2,1,0:T(8,128)(2,1)} %bitcast.125, f32[8,2048]{1,0:T(8,128)} %broadcast_in_dim.39.bias_ref), custom_call_target="tpu_custom_call" | custom-call | flops 8589934592 | bytes 12582912 | tf_op jit(solution)/shard_map/upper/pallas_call | solution.py:477
  159.5 5.0 collective-permute-start.14
  165.1 16.2 %collective-permute-done.13.refs_1_ = bf16[1024,512]{1,0:T(8,128)(2,1)S(1)} collective-permute-done((bf16[1024,512]{1,0:T(8,128)(2,1)S(1)}, bf16[1024,512]{1,0:T(8,128)(2,1)S(1)}, u32[]{:S(2)}, u32[]{:S(2)}) %collective-permute-start.13) | collective-permute-done | bytes 1048608 | tf_op jit(solution)/shard_map/ppermute | solution.py:56
  183.5 7.2 %cotangent_rows.1 = (bf16[1024,2048]{1,0:T(8,128)(2,1)}, f32[8,2048]{1,0:T(8,128)}) custom-call(s32[2]{0:T(128)} %pad_add_fusion.me_ref, s32[2]{0:T(128)} %lens.7, bf16[1024,512]{1,0:T(8,128)(2,1)} %bitcast.98, bf16[1024,512]{1,0:T(8,128)(2,1)} %collective-permute-done.9.refs_0_, bf16[1024,512]{1,0:T(8,128)(2,1)} %copy-done.15, ...), custom_call_target="tpu_custom_call" | custom-call | flops 8388608 | bytes 12582912 | tf_op jit(solution)/shard_map/cotangent_rows/pallas_call | solution.py:158
  190.6 3.2 all-gather.14.cloned.1.call-done
  194.5 5.7 %attention_forward.2 = (bf16[512,512]{1,0:T(8,128)(2,1)}, f32[512,256]{1,0:T(8,128)}) custom-call(s32[5]{0:T(128)} %stack.32.info, s32[2]{0:T(128)} %lens.7, bf16[1024,512]{1,0:T(8,128)(2,1)} %get-tuple-element.97.query_ref, bf16[4,2,512,1024]{3,2,1,0:T(8,128)(2,1)} %bitcast.84), custom_call_target="tpu_custom_call" | custom-call | flops 2147483648 | bytes 4194304 | tf_op jit(solution)/shard_map/attention_forward/pallas_call | solution.py:313
  200.2 8.5 %attention_forward.3 = (bf16[512,512]{1,0:T(8,128)(2,1)}, f32[512,256]{1,0:T(8,128)}) custom-call(s32[5]{0:T(128)} %stack.32.info, s32[2]{0:T(128)} %lens.7, bf16[1024,512]{1,0:T(8,128)(2,1)} %get-tuple-element.97.query_ref, bf16[4,2,512,1024]{3,2,1,0:T(8,128)(2,1)} %bitcast.85), custom_call_target="tpu_custom_call" | custom-call | flops 2147483648 | bytes 4194304 | tf_op jit(solution)/shard_map/attention_forward/pallas_call | solution.py:313
  208.6 5.5 %context_grad.1.grad_ref = bf16[1024,512]{1,0:T(8,128)(2,1)} custom-call(bf16[1024,2048]{1,0:T(8,128)(2,1)} %get-tuple-element.105.rows_ref.refs_0_.refs_4_.refs_5_.refs_6_.refs_7_, bf16[8,256,2048]{2,1,0:T(8,128)(2,1)} %bitcast.89), custom_call_target="tpu_custom_call" | custom-call | flops 2147483648 | bytes 6291456 | tf_op jit(solution)/shard_map/context_grad/pallas_call | solution.py:531
  214.2 8.2 %attention_backward.2 = (bf16[512,512]{1,0:T(8,128)(2,1)}, bf16[512,1024]{1,0:T(8,128)(2,1)}, bf16[512,1024]{1,0:T(8,128)(2,1)}, bf16[2,512,1024]{2,1,0:T(8,128)(2,1)}) custom-call(s32[5]{0:T(128)} %stack.32.info, s32[2]{0:T(128)} %lens.7, bf16[1024,512]{1,0:T(8,128)(2,1)} %get-tuple-element.97.query_ref, ...), custom_call_target="tpu_custom_call" | custom-call | flops 5368709120 | bytes 8388608 | tf_op jit(solution)/shard_map/attention_backward/pallas_call | solution.py:395
  222.4 4.4 collective-permute-start.15
  226.8 4.0 collective-permute-done.15.refs_2_
  230.8 8.6 %attention_backward.3 = (bf16[512,512]{1,0:T(8,128)(2,1)}, bf16[512,1024]{1,0:T(8,128)(2,1)}, bf16[512,1024]{1,0:T(8,128)(2,1)}, bf16[2,512,1024]{2,1,0:T(8,128)(2,1)}) custom-call(s32[5]{0:T(128)} %stack.32.info, s32[2]{0:T(128)} %lens.7, bf16[1024,512]{1,0:T(8,128)(2,1)} %get-tuple-element.97.query_ref, ...), custom_call_target="tpu_custom_call" | custom-call | flops 5368709120 | bytes 8388608 | tf_op jit(solution)/shard_map/attention_backward/pallas_call | solution.py:395
  239.4 2.5 collective-permute-start.16
  241.9 4.1 collective-permute-done.16.refs_6_
  246.0 4.0 all-gather.8.cloned.1.call-done.refs_2_.weight_ref
  250.0 16.0 %branch.1 = bf16[1024,2048]{1,0:T(8,128)(2,1)} custom-call(bf16[1024,2048]{1,0:T(8,128)(2,1)} %get-tuple-element.101.active_ref.refs_1_, bf16[512,512]{1,0:T(8,128)(2,1)} %get-tuple-element.88.context_ref.refs_0_, bf16[512,512]{1,0:T(8,128)(2,1)} %get-tuple-element.90.context_ref.refs_1_, bf16[2048,2048]{1,0:T(8,128)(2,1)} %all-gather.8.cloned.1.call-done.refs_2_.weight_ref, ...), custom_call_target="tpu_custom_call" | custom-call | flops 10737418240 | bytes 10485760 | tf_op jit(solution)/shard_map/branch/pallas_call | solution.py:440
  266.1 14.7 %product.2 = bf16[2048,2048]{1,0:T(8,128)(2,1)} custom-call(bf16[1024,2048]{1,0:T(8,128)(2,1)} %get-tuple-element.105.rows_ref.refs_0_.refs_4_.refs_5_.refs_6_.refs_7_, bf16[1024,2048]{1,0:T(8,128)(2,1)} %get-tuple-element.101.active_ref.refs_1_), custom_call_target="tpu_custom_call" | custom-call | flops 8589934592 | bytes 16777216 | tf_op jit(solution)/shard_map/product/pallas_call | solution.py:848
  287.1 13.9 %upper_grad.1 = (bf16[1024,2048]{1,0:T(8,128)(2,1)}, f32[8,2048]{1,0:T(8,128)}) custom-call(bf16[1024,2048]{1,0:T(8,128)(2,1)} %get-tuple-element.105.rows_ref.refs_0_.refs_4_.refs_5_.refs_6_.refs_7_, bf16[2048,2048]{1,0:T(8,128)(2,1)} %all-gather.8.cloned.1.call-done.refs_2_.weight_ref, bf16[1024,2048]{1,0:T(8,128)(2,1)} %get-tuple-element.106.slope_ref), custom_call_target="tpu_custom_call" | custom-call | flops 8589934592 | bytes 16777216 | tf_op jit(solution)/shard_map/upper_grad/pallas_call | solution.py:506
  301.0 15.0 %second_in_grad.1 = (bf16[1024,2048]{1,0:T(8,128)(2,1)}, f32[8,2048]{1,0:T(8,128)}) custom-call(bf16[1024,2048]{1,0:T(8,128)(2,1)} %get-tuple-element.107.grad_ref.refs_1_, bf16[8,256,2048]{2,1,0:T(8,128)(2,1)} %bitcast.126, bf16[1024,2048]{1,0:T(8,128)(2,1)} %get-tuple-element.108.rows_ref, f32[1024,128]{1,0:T(8,128)} %get-tuple-element.103.stat_ref, ...), custom_call_target="tpu_custom_call" | custom-call | flops 8589934592 | bytes 20971520 | tf_op jit(solution)/shard_map/second_in_grad/pallas_call | solution.py:566
  316.0 19.1 %collective-permute-done.18.refs_7_ = bf16[512,1024]{1,0:T(8,128)(2,1)S(1)} collective-permute-done((bf16[512,1024]{1,0:T(8,128)(2,1)S(1)}, bf16[512,1024]{1,0:T(8,128)(2,1)S(1)}, u32[]{:S(2)}, u32[]{:S(2)}) %collective-permute-start.18) | collective-permute-done | bytes 1048608 | tf_op jit(solution)/shard_map/ppermute | solution.py:425
  336.1 7.9 %joined_grad.1 = (bf16[1024,1536]{1,0:T(8,128)(2,1)}, f32[8,1536]{1,0:T(8,128)}) custom-call(bf16[512,512]{1,0:T(8,128)(2,1)} %get-tuple-element.110.refs_0_, bf16[512,1024]{1,0:T(8,128)(2,1)} %get-tuple-element.111.refs_1_, bf16[2,512,1024]{2,1,0:T(8,128)(2,1)} %copy-done.1, bf16[512,1024]{1,0:T(8,128)(2,1)} %copy-done.10, ...), custom_call_target="tpu_custom_call" | custom-call | flops 15728640 | bytes 15728640 | tf_op jit(solution)/shard_map/joined_grad/pallas_call | solution.py:625
  344.0 17.2 %first_in_grad.1 = (bf16[1032,512]{1,0:T(8,128)(2,1)}, bf16[1032,512]{1,0:T(8,128)(2,1)}, bf16[1032,512]{1,0:T(8,128)(2,1)}, bf16[1032,512]{1,0:T(8,128)(2,1)}, f32[8,2048]{1,0:T(8,128)}) custom-call(s32[4]{0:T(128)} %compare_select_fusion.order, bf16[1024,1536]{1,0:T(8,128)(2,1)} %get-tuple-element.116.grad_ref.refs_8_, bf16[8,256,2048]{2,1,0:T(8,128)(2,1)} %bitcast.91, ...), custom_call_target="tpu_custom_call" | custom-call | flops 6442450944 | bytes 23068672 | tf_op jit(solution)/shard_map/first_in_grad/pallas_call | solution.py:683
  361.2 15.5 %product.3 = bf16[2048,2048]{1,0:T(8,128)(2,1)} custom-call(bf16[1024,2048]{1,0:T(8,128)(2,1)} %get-tuple-element.121.rows_ref.refs_0_, bf16[1024,2048]{1,0:T(8,128)(2,1)} %get-tuple-element.107.grad_ref.refs_1_), custom_call_target="tpu_custom_call" | custom-call | flops 8589934592 | bytes 16777216 | tf_op jit(solution)/shard_map/product/pallas_call | solution.py:848
  383.7 11.5 %weight_grad.2 = bf16[1056,2048]{1,0:T(8,128)(2,1)} custom-call(s32[4]{0:T(128)} %fusion.17.order, bf16[1024,2048]{1,0:T(8,128)(2,1)} %get-tuple-element.128.rows_ref.refs_0_.refs_1_.refs_2_.refs_3_, bf16[1024,2048]{1,0:T(8,128)(2,1)} %get-tuple-element.128.rows_ref.refs_0_.refs_1_.refs_2_.refs_3_, ...), custom_call_target="tpu_custom_call" | custom-call | flops 4294967296 | bytes 14680064 | tf_op jit(solution)/shard_map/weight_grad/pallas_call | solution.py:795
  396.6 2.4 collective-permute-start.20
  402.9 12.2 %weight_grad.3 = (bf16[264,2048]{1,0:T(8,128)(2,1)}, bf16[264,2048]{1,0:T(8,128)(2,1)}, bf16[264,2048]{1,0:T(8,128)(2,1)}, bf16[264,2048]{1,0:T(8,128)(2,1)}) custom-call(s32[4]{0:T(128)} %fusion.18.order, bf16[1024,2048]{1,0:T(8,128)(2,1)} %get-tuple-element.128.rows_ref.refs_0_.refs_1_.refs_2_.refs_3_, ...), custom_call_target="tpu_custom_call" | custom-call | flops 4294967296 | bytes 14680064 | tf_op jit(solution)/shard_map/weight_grad/pallas_call | solution.py:795
  415.1 8.1 %collective-permute-start.24 = (bf16[264,2048]{1,0:T(8,128)(2,1)}, bf16[264,2048]{1,0:T(8,128)(2,1)}, u32[]{:S(2)}, u32[]{:S(2)}) collective-permute-start(bf16[264,2048]{1,0:T(8,128)(2,1)} %get-tuple-element.132), channel_id=1, source_target_pairs={{0,16},{4,20},{8,24},{12,28},{16,0},{20,4},{24,8},{28,12},{1,17},{... | collective-permute-start | bytes 3244040 | tf_op jit(solution)/shard_map/ppermute | solution.py:882
  423.6 6.9 %collective-permute-start.25 = (bf16[264,2048]{1,0:T(8,128)(2,1)}, bf16[264,2048]{1,0:T(8,128)(2,1)}, u32[]{:S(2)}, u32[]{:S(2)}) collective-permute-start(bf16[264,2048]{1,0:T(8,128)(2,1)} %get-tuple-element.134), channel_id=1, source_target_pairs={{0,24},{4,28},{8,16},{12,20},{16,8},{20,12},{24,0},{28,4},{1,25},{... | collective-permute-start | bytes 3244040 | tf_op jit(solution)/shard_map/ppermute | solution.py:882
  430.4 38.1 %collective-permute-done.20 = bf16[1032,512]{1,0:T(8,128)(2,1)} collective-permute-done((bf16[1032,512]{1,0:T(8,128)(2,1)}, bf16[1032,512]{1,0:T(8,128)(2,1)}, u32[]{:S(2)}, u32[]{:S(2)}) %collective-permute-start.20) | collective-permute-done | bytes 1056800 | tf_op jit(solution)/shard_map/ppermute | solution.py:65
  468.5 2.4 convert_add_fusion.2
  471.0 3.6 fusion.7
  474.6 5.7 %collective-permute-done.25 = bf16[264,2048]{1,0:T(8,128)(2,1)} collective-permute-done((bf16[264,2048]{1,0:T(8,128)(2,1)}, bf16[264,2048]{1,0:T(8,128)(2,1)}, u32[]{:S(2)}, u32[]{:S(2)}) %collective-permute-start.25) | collective-permute-done | bytes 1081376 | tf_op jit(solution)/shard_map/ppermute | solution.py:882
  480.3 2.8 convert_add_fusion.1
  483.1 18.1 %collective-permute-start.28 = (f32[8,128]{1,0:T(8,128)S(1)}, f32[8,128]{1,0:T(8,128)S(1)}, u32[]{:S(2)}, u32[]{:S(2)}) collective-permute-start(f32[8,128]{1,0:T(8,128)S(1)} %bitcast.117), channel_id=1, source_target_pairs={{0,3},{1,0},{2,1},{3,2},{4,7},{5,4},{6,5},{7,6},{8,11},{9,8},{10,9... | collective-permute-start | bytes 12296 | tf_op jit(solution)/shard_map/ppermute | solution.py:894
  501.2 7.8 %collective-permute-start.27 = (f32[8,128]{1,0:T(8,128)S(1)}, f32[8,128]{1,0:T(8,128)S(1)}, u32[]{:S(2)}, u32[]{:S(2)}) collective-permute-start(f32[8,128]{1,0:T(8,128)S(1)} %bitcast.118), channel_id=1, source_target_pairs={{0,2},{1,3},{2,0},{3,1},{4,6},{5,7},{6,4},{7,5},{8,10},{9,11},{10,... | collective-permute-start | bytes 12296 | tf_op jit(solution)/shard_map/ppermute | solution.py:894
  516.1 2.8 convert_element_type.124
  519.3 2.8 convert_element_type.123
  (202 shorter events, 58.1 us)
Async XLA Ops:
  7.2 111.4 %all-gather.10.cloned.1.call-start = ((), (), s32[]{:S(2)}) async-start(), calls=%async_computation.7 | async-start | bytes 9437184 | tf_op jit(solution)/shard_map/all_gather | solution.py:940
  9.4 63.3 %copy-start.31 = (bf16[2,96]{1,0:T(2,128)(2,1)S(1)}, bf16[2,96]{1,0:T(2,128)(2,1)}, u32[]{:S(2)}) copy-start(bf16[2,96]{1,0:T(2,128)(2,1)} %param.23) | copy-start | bytes 1156
  9.5 63.4 %copy-start.24 = (bf16[64,4]{0,1:T(4,128)(2,1)S(1)}, bf16[64,4]{0,1:T(4,128)(2,1)}, u32[]{:S(2)}) copy-start(bf16[64,4]{0,1:T(4,128)(2,1)} %param.29) | copy-start | bytes 1540
  9.5 63.6 %copy-start.25 = (bf16[256]{0:T(256)(128)(2,1)S(1)}, bf16[256]{0:T(256)(128)(2,1)}, u32[]{:S(2)}) copy-start(bf16[256]{0:T(256)(128)(2,1)} %param.20) | copy-start | bytes 1540
  9.5 63.6 %copy-start.26 = (bf16[256]{0:T(256)(128)(2,1)S(1)}, bf16[256]{0:T(256)(128)(2,1)}, u32[]{:S(2)}) copy-start(bf16[256]{0:T(256)(128)(2,1)} %param.21) | copy-start | bytes 1540
  9.5 63.6 %copy-start.27 = (bf16[256]{0:T(256)(128)(2,1)S(1)}, bf16[256]{0:T(256)(128)(2,1)}, u32[]{:S(2)}) copy-start(bf16[256]{0:T(256)(128)(2,1)} %param.26) | copy-start | bytes 1540
  9.5 63.6 %copy-start.28 = (bf16[256]{0:T(256)(128)(2,1)S(1)}, bf16[256]{0:T(256)(128)(2,1)}, u32[]{:S(2)}) copy-start(bf16[256]{0:T(256)(128)(2,1)} %param.27) | copy-start | bytes 1540
  9.5 63.6 %copy-start.29 = (bf16[256]{0:T(256)(128)(2,1)S(1)}, bf16[256]{0:T(256)(128)(2,1)}, u32[]{:S(2)}) copy-start(bf16[256]{0:T(256)(128)(2,1)} %param.25) | copy-start | bytes 1540
  9.5 63.6 %copy-start.30 = (bf16[256]{0:T(256)(128)(2,1)S(1)}, bf16[256]{0:T(256)(128)(2,1)}, u32[]{:S(2)}) copy-start(bf16[256]{0:T(256)(128)(2,1)} %param.31) | copy-start | bytes 1540
  9.5 82.9 %copy-start.12 = (bf16[2,512,512]{2,1,0:T(8,128)(2,1)S(1)}, bf16[2,512,512]{2,1,0:T(8,128)(2,1)}, u32[]{:S(2)}) copy-start(bf16[2,512,512]{2,1,0:T(8,128)(2,1)} %param.19) | copy-start | bytes 3145732
  10.7 129.2 %all-gather.12.cloned.1.call-start = ((), (), s32[]{:S(2)}) async-start(), calls=%async_computation.8 | async-start | bytes 9437184 | tf_op jit(solution)/shard_map/all_gather | solution.py:941
  11.4 182.4 %all-gather.14.cloned.1.call-start = ((), (), s32[]{:S(2)}) async-start(), calls=%async_computation.9 | async-start | bytes 10485760 | tf_op jit(solution)/shard_map/all_gather | solution.py:976
  11.5 28.1 %collective-permute-start.1 = (bf16[1024,512]{1,0:T(8,128)(2,1)S(1)}, bf16[1024,512]{1,0:T(8,128)(2,1)S(1)}, u32[]{:S(2)}, u32[]{:S(2)}) collective-permute-start(bf16[1024,512]{1,0:T(8,128)(2,1)S(1)} %bitcast.93), channel_id=1, source_target_pairs={{1,0},{2,1},{3,2},{5,4},{6,5},{7,6},{9,8},{10,9},{11,10},{13,12},{... | collective-permute-start | bytes 3145736 | tf_op jit(solution)/shard_map/ppermute | solution.py:56
  12.8 28.1 %collective-permute-start = (bf16[1024,512]{1,0:T(8,128)(2,1)S(1)}, bf16[1024,512]{1,0:T(8,128)(2,1)S(1)}, u32[]{:S(2)}, u32[]{:S(2)}) collective-permute-start(bf16[1024,512]{1,0:T(8,128)(2,1)S(1)} %bitcast.94), channel_id=1, source_target_pairs={{0,1},{1,2},{2,3},{4,5},{5,6},{6,7},{8,9},{9,10},{10,11},{12,13},{... | collective-permute-start | bytes 3145736 | tf_op jit(solution)/shard_map/ppermute | solution.py:55
  39.6 26.3 %collective-permute-start.2 = (bf16[1024,512]{1,0:T(8,128)(2,1)S(1)}, bf16[1024,512]{1,0:T(8,128)(2,1)}, u32[]{:S(2)}, u32[]{:S(2)}) collective-permute-start(bf16[1024,512]{1,0:T(8,128)(2,1)S(1)} %collective-permute-done.1.refs_5_), channel_id=1, source_target_pairs={{1,0},{2,1},{3,2},{5,4},{6,5},{7,6},{9,8},{10,9},{11,10},{13,12},{... | collective-permute-start | bytes 3145736 | tf_op jit(solution)/shard_map/ppermute | solution.py:56
  40.9 26.3 %collective-permute-start.4 = (bf16[1024,512]{1,0:T(8,128)(2,1)S(1)}, bf16[1024,512]{1,0:T(8,128)(2,1)S(1)}, u32[]{:S(2)}, u32[]{:S(2)}) collective-permute-start(bf16[1024,512]{1,0:T(8,128)(2,1)S(1)} %collective-permute-done.refs_0_), channel_id=1, source_target_pairs={{0,1},{1,2},{2,3},{4,5},{5,6},{6,7},{8,9},{9,10},{10,11},{12,13},{... | collective-permute-start | bytes 3145736 | tf_op jit(solution)/shard_map/ppermute | solution.py:55
  65.9 25.6 %collective-permute-start.3 = (bf16[1024,512]{1,0:T(8,128)(2,1)}, bf16[1024,512]{1,0:T(8,128)(2,1)}, u32[]{:S(2)}, u32[]{:S(2)}) collective-permute-start(bf16[1024,512]{1,0:T(8,128)(2,1)} %collective-permute-done.2.refs_3_), channel_id=1, source_target_pairs={{1,0},{2,1},{3,2},{5,4},{6,5},{7,6},{9,8},{10,9},{11,10},{13,12},{... | collective-permute-start | bytes 3145736 | tf_op jit(solution)/shard_map/ppermute | solution.py:56
  67.2 25.2 %collective-permute-start.5 = (bf16[1024,512]{1,0:T(8,128)(2,1)S(1)}, bf16[1024,512]{1,0:T(8,128)(2,1)}, u32[]{:S(2)}, u32[]{:S(2)}) collective-permute-start(bf16[1024,512]{1,0:T(8,128)(2,1)S(1)} %collective-permute-done.4.refs_2_), channel_id=1, source_target_pairs={{0,1},{1,2},{2,3},{4,5},{5,6},{6,7},{8,9},{9,10},{10,11},{12,13},{... | collective-permute-start | bytes 3145736 | tf_op jit(solution)/shard_map/ppermute | solution.py:55
  73.4 1.3 collective-permute-start.6
  74.8 4.0 collective-permute-start.7
  78.8 23.6 %collective-permute-start.8 = (bf16[8,2048]{1,0:T(8,128)(2,1)S(1)}, bf16[8,2048]{1,0:T(8,128)(2,1)S(1)}, u32[]{:S(2)}, u32[]{:S(2)}) collective-permute-start(bf16[8,2048]{1,0:T(8,128)(2,1)S(1)} %add.115), channel_id=1, source_target_pairs={{0,16},{4,20},{8,24},{12,28},{16,0},{20,4},{24,8},{28,12},{1,17},{... | collective-permute-start | bytes 98312 | tf_op jit(solution)/shard_map/ppermute | solution.py:726
  92.4 25.1 %collective-permute-start.10 = (bf16[1024,512]{1,0:T(8,128)(2,1)S(1)}, bf16[1024,512]{1,0:T(8,128)(2,1)}, u32[]{:S(2)}, u32[]{:S(2)}) collective-permute-start(bf16[1024,512]{1,0:T(8,128)(2,1)S(1)} %bitcast.99), channel_id=1, source_target_pairs={{1,0},{2,1},{3,2},{5,4},{6,5},{7,6},{9,8},{10,9},{11,10},{13,12},{... | collective-permute-start | bytes 3145736 | tf_op jit(solution)/shard_map/ppermute | solution.py:938
  93.7 24.9 %collective-permute-start.9 = (bf16[1024,512]{1,0:T(8,128)(2,1)S(1)}, bf16[1024,512]{1,0:T(8,128)(2,1)}, u32[]{:S(2)}, u32[]{:S(2)}) collective-permute-start(bf16[1024,512]{1,0:T(8,128)(2,1)S(1)} %bitcast.100), channel_id=1, source_target_pairs={{0,1},{1,2},{2,3},{4,5},{5,6},{6,7},{8,9},{9,10},{10,11},{12,13},{... | collective-permute-start | bytes 3145736 | tf_op jit(solution)/shard_map/ppermute | solution.py:937
  132.5 117.5 %all-gather.8.cloned.1.call-start = ((), (), s32[]{:S(2)}) async-start(), calls=%async_computation.3 | async-start | bytes 9437184 | tf_op jit(solution)/shard_map/all_gather | solution.py:983
  132.6 25.4 %collective-permute-start.12 = (bf16[1024,512]{1,0:T(8,128)(2,1)}, bf16[1024,512]{1,0:T(8,128)(2,1)S(1)}, u32[]{:S(2)}, u32[]{:S(2)}) collective-permute-start(bf16[1024,512]{1,0:T(8,128)(2,1)} %collective-permute-done.10.refs_5_), channel_id=1, source_target_pairs={{1,0},{2,1},{3,2},{5,4},{6,5},{7,6},{9,8},{10,9},{11,10},{13,12},{... | collective-permute-start | bytes 3145736 | tf_op jit(solution)/shard_map/ppermute | solution.py:56
  133.9 24.3 %collective-permute-start.11 = (bf16[1024,512]{1,0:T(8,128)(2,1)}, bf16[1024,512]{1,0:T(8,128)(2,1)S(1)}, u32[]{:S(2)}, u32[]{:S(2)}) collective-permute-start(bf16[1024,512]{1,0:T(8,128)(2,1)} %collective-permute-done.9.refs_0_), channel_id=1, source_target_pairs={{0,1},{1,2},{2,3},{4,5},{5,6},{6,7},{8,9},{9,10},{10,11},{12,13},{... | collective-permute-start | bytes 3145736 | tf_op jit(solution)/shard_map/ppermute | solution.py:55
  158.2 23.1 %collective-permute-start.13 = (bf16[1024,512]{1,0:T(8,128)(2,1)S(1)}, bf16[1024,512]{1,0:T(8,128)(2,1)S(1)}, u32[]{:S(2)}, u32[]{:S(2)}) collective-permute-start(bf16[1024,512]{1,0:T(8,128)(2,1)S(1)} %collective-permute-done.12.refs_3_), channel_id=1, source_target_pairs={{1,0},{2,1},{3,2},{5,4},{6,5},{7,6},{9,8},{10,9},{11,10},{13,12},{... | collective-permute-start | bytes 3145736 | tf_op jit(solution)/shard_map/ppermute | solution.py:56
  159.5 23.0 %collective-permute-start.14 = (bf16[1024,512]{1,0:T(8,128)(2,1)S(1)}, bf16[1024,512]{1,0:T(8,128)(2,1)S(1)}, u32[]{:S(2)}, u32[]{:S(2)}) collective-permute-start(bf16[1024,512]{1,0:T(8,128)(2,1)S(1)} %collective-permute-done.11.refs_2_), channel_id=1, source_target_pairs={{0,1},{1,2},{2,3},{4,5},{5,6},{6,7},{8,9},{9,10},{10,11},{12,13},{... | collective-permute-start | bytes 3145736 | tf_op jit(solution)/shard_map/ppermute | solution.py:55
  193.8 277.1 %reduce-scatter.4.cloned.1.call-start = ((), (), s32[]{:S(2)}) async-start(), calls=%async_computation.4 | async-start | bytes 5242880 | tf_op jit(solution)/shard_map/reduce_scatter | solution.py:1006
  222.4 8.4 %collective-permute-start.15 = (bf16[2,512,1024]{2,1,0:T(8,128)(2,1)}, bf16[2,512,1024]{2,1,0:T(8,128)(2,1)S(1)}, u32[]{:S(2)}, u32[]{:S(2)}) collective-permute-start(bf16[2,512,1024]{2,1,0:T(8,128)(2,1)} %get-tuple-element.96), channel_id=1, source_target_pairs={{0,4},{4,0},{8,12},{12,8},{1,5},{5,1},{9,13},{13,9},{2,6},{6,2},{1... | collective-permute-start | bytes 6291464 | tf_op jit(solution)/shard_map/ppermute | solution.py:423
  230.8 50.6 %copy-start.1 = (bf16[2,512,1024]{2,1,0:T(8,128)(2,1)}, bf16[2,512,1024]{2,1,0:T(8,128)(2,1)S(1)}, u32[]{:S(2)}) copy-start(bf16[2,512,1024]{2,1,0:T(8,128)(2,1)S(1)} %collective-permute-done.15.refs_2_) | copy-start | bytes 6291460
  239.4 6.6 %collective-permute-start.16 = (bf16[2,512,1024]{2,1,0:T(8,128)(2,1)}, bf16[2,512,1024]{2,1,0:T(8,128)(2,1)}, u32[]{:S(2)}, u32[]{:S(2)}) collective-permute-start(bf16[2,512,1024]{2,1,0:T(8,128)(2,1)} %get-tuple-element.100), channel_id=1, source_target_pairs={{0,4},{4,0},{8,12},{12,8},{1,5},{5,1},{9,13},{13,9},{2,6},{6,2},{1... | collective-permute-start | bytes 6291464 | tf_op jit(solution)/shard_map/ppermute | solution.py:423
  266.0 250.1 %reduce-scatter.8.cloned.1.call-start = ((), (), s32[]{:S(2)}) async-start(), calls=%async_computation.6 | async-start | bytes 9437184 | tf_op jit(solution)/shard_map/reduce_scatter | solution.py:1013
  280.8 238.5 %reduce-scatter.6.cloned.1.call-start = ((), (), s32[]{:S(2)}) async-start(), calls=%async_computation.5 | async-start | bytes 9437184 | tf_op jit(solution)/shard_map/reduce_scatter | solution.py:1035
  282.4 33.5 %collective-permute-start.17 = (bf16[512,1024]{1,0:T(8,128)(2,1)S(1)}, bf16[512,1024]{1,0:T(8,128)(2,1)S(1)}, u32[]{:S(2)}, u32[]{:S(2)}) collective-permute-start(bf16[512,1024]{1,0:T(8,128)(2,1)S(1)} %fusion.9), channel_id=1, source_target_pairs={{8,0},{12,4},{9,1},{13,5},{10,2},{14,6},{11,3},{15,7},{24,16},{28,... | collective-permute-start | bytes 3145736 | tf_op jit(solution)/shard_map/ppermute | solution.py:425
  285.4 49.7 %collective-permute-start.18 = (bf16[512,1024]{1,0:T(8,128)(2,1)S(1)}, bf16[512,1024]{1,0:T(8,128)(2,1)S(1)}, u32[]{:S(2)}, u32[]{:S(2)}) collective-permute-start(bf16[512,1024]{1,0:T(8,128)(2,1)S(1)} %fusion.8), channel_id=1, source_target_pairs={{8,0},{12,4},{9,1},{13,5},{10,2},{14,6},{11,3},{15,7},{24,16},{28,... | collective-permute-start | bytes 3145736 | tf_op jit(solution)/shard_map/ppermute | solution.py:425
  395.2 7.7 %collective-permute-start.22 = (bf16[1056,2048]{1,0:T(8,128)(2,1)}, bf16[1056,2048]{1,0:T(8,128)(2,1)}, u32[]{:S(2)}, u32[]{:S(2)}) collective-permute-start(bf16[1056,2048]{1,0:T(8,128)(2,1)} %weight_grad.2), channel_id=1, source_target_pairs={{0,4},{4,0},{8,12},{12,8},{16,20},{20,16},{24,28},{28,24},{1,5},{5... | collective-permute-start | bytes 12976136 | tf_op jit(solution)/shard_map/ppermute | solution.py:877
  395.2 28.3 %collective-permute-start.19 = (bf16[1032,512]{1,0:T(8,128)(2,1)}, bf16[1032,512]{1,0:T(8,128)(2,1)S(1)}, u32[]{:S(2)}, u32[]{:S(2)}) collective-permute-start(bf16[1032,512]{1,0:T(8,128)(2,1)} %get-tuple-element.118), channel_id=1, source_target_pairs={{0,1},{1,2},{2,3},{3,0},{4,5},{5,6},{6,7},{7,4},{8,9},{9,10},{10,1... | collective-permute-start | bytes 3170312 | tf_op jit(solution)/shard_map/ppermute | solution.py:65
  396.6 71.9 %collective-permute-start.20 = (bf16[1032,512]{1,0:T(8,128)(2,1)}, bf16[1032,512]{1,0:T(8,128)(2,1)}, u32[]{:S(2)}, u32[]{:S(2)}) collective-permute-start(bf16[1032,512]{1,0:T(8,128)(2,1)} %get-tuple-element.119), channel_id=1, source_target_pairs={{0,2},{1,3},{2,0},{3,1},{4,6},{5,7},{6,4},{7,5},{8,10},{9,11},{10,... | collective-permute-start | bytes 3170312 | tf_op jit(solution)/shard_map/ppermute | solution.py:65
  399.1 69.4 %collective-permute-start.21 = (bf16[1032,512]{1,0:T(8,128)(2,1)}, bf16[1032,512]{1,0:T(8,128)(2,1)}, u32[]{:S(2)}, u32[]{:S(2)}) collective-permute-start(bf16[1032,512]{1,0:T(8,128)(2,1)} %get-tuple-element.120), channel_id=1, source_target_pairs={{0,3},{1,0},{2,1},{3,2},{4,7},{5,4},{6,5},{7,6},{8,11},{9,8},{10,9... | collective-permute-start | bytes 3170312 | tf_op jit(solution)/shard_map/ppermute | solution.py:65
  401.6 66.9 %copy-start.6 = (bf16[1032,512]{1,0:T(8,128)(2,1)S(1)}, bf16[1032,512]{1,0:T(8,128)(2,1)}, u32[]{:S(2)}) copy-start(bf16[1032,512]{1,0:T(8,128)(2,1)} %get-tuple-element.117) | copy-start | bytes 3170308
  415.1 59.5 %collective-permute-start.23 = (bf16[264,2048]{1,0:T(8,128)(2,1)}, bf16[264,2048]{1,0:T(8,128)(2,1)}, u32[]{:S(2)}, u32[]{:S(2)}) collective-permute-start(bf16[264,2048]{1,0:T(8,128)(2,1)} %get-tuple-element.130), channel_id=1, source_target_pairs={{0,8},{4,12},{8,0},{12,4},{16,24},{20,28},{24,16},{28,20},{1,9},{5... | collective-permute-start | bytes 3244040 | tf_op jit(solution)/shard_map/ppermute | solution.py:882
  415.1 59.4 %collective-permute-start.24 = (bf16[264,2048]{1,0:T(8,128)(2,1)}, bf16[264,2048]{1,0:T(8,128)(2,1)}, u32[]{:S(2)}, u32[]{:S(2)}) collective-permute-start(bf16[264,2048]{1,0:T(8,128)(2,1)} %get-tuple-element.132), channel_id=1, source_target_pairs={{0,16},{4,20},{8,24},{12,28},{16,0},{20,4},{24,8},{28,12},{1,17},{... | collective-permute-start | bytes 3244040 | tf_op jit(solution)/shard_map/ppermute | solution.py:882
  423.6 47.4 %copy-start.3 = (bf16[2,512,512]{2,1,0:T(8,128)(2,1)S(1)}, bf16[2,512,512]{2,1,0:T(8,128)(2,1)}, u32[]{:S(2)}) copy-start(bf16[2,512,512]{2,1,0:T(8,128)(2,1)} %param.17) | copy-start | bytes 3145732
  423.6 56.7 %collective-permute-start.25 = (bf16[264,2048]{1,0:T(8,128)(2,1)}, bf16[264,2048]{1,0:T(8,128)(2,1)}, u32[]{:S(2)}, u32[]{:S(2)}) collective-permute-start(bf16[264,2048]{1,0:T(8,128)(2,1)} %get-tuple-element.134), channel_id=1, source_target_pairs={{0,24},{4,28},{8,16},{12,20},{16,8},{20,12},{24,0},{28,4},{1,25},{... | collective-permute-start | bytes 3244040 | tf_op jit(solution)/shard_map/ppermute | solution.py:882
  483.1 32.4 %collective-permute-start.28 = (f32[8,128]{1,0:T(8,128)S(1)}, f32[8,128]{1,0:T(8,128)S(1)}, u32[]{:S(2)}, u32[]{:S(2)}) collective-permute-start(f32[8,128]{1,0:T(8,128)S(1)} %bitcast.117), channel_id=1, source_target_pairs={{0,3},{1,0},{2,1},{3,2},{4,7},{5,4},{6,5},{7,6},{8,11},{9,8},{10,9... | collective-permute-start | bytes 12296 | tf_op jit(solution)/shard_map/ppermute | solution.py:894
  501.2 14.3 %collective-permute-start.27 = (f32[8,128]{1,0:T(8,128)S(1)}, f32[8,128]{1,0:T(8,128)S(1)}, u32[]{:S(2)}, u32[]{:S(2)}) collective-permute-start(f32[8,128]{1,0:T(8,128)S(1)} %bitcast.118), channel_id=1, source_target_pairs={{0,2},{1,3},{2,0},{3,1},{4,6},{5,7},{6,4},{7,5},{8,10},{9,11},{10,... | collective-permute-start | bytes 12296 | tf_op jit(solution)/shard_map/ppermute | solution.py:894
  509.0 6.5 %collective-permute-start.26 = (f32[8,128]{1,0:T(8,128)S(1)}, f32[8,128]{1,0:T(8,128)S(1)}, u32[]{:S(2)}, u32[]{:S(2)}) collective-permute-start(f32[8,128]{1,0:T(8,128)S(1)} %bitcast.119), channel_id=1, source_target_pairs={{0,1},{1,2},{2,3},{3,0},{4,5},{5,6},{6,7},{7,4},{8,9},{9,10},{10,1... | collective-permute-start | bytes 12296 | tf_op jit(solution)/shard_map/ppermute | solution.py:894
  (20 other events, 244.6 us)
Sparse Core Ops, SparseCore 0:
  10.8 57.0 all-gather.9
  69.8 54.7 all-gather.11
  132.7 61.1 all-gather.13
  195.6 54.4 all-gather.7
  266.2 87.0 reduce-scatter.3
  357.0 80.8 reduce-scatter.7
  441.4 77.9 reduce-scatter.5

commit v4 on v3

--- a/solution.py
+++ b/solution.py
@@ -998,7 +998,6 @@
         ready = after(query, query_grad)
         queries.append(query_grad)
         three, taken = return_pairs(*pair_grads, "ctx")
-        ready = after(ready, taken)
         sums.append(three)
     branch = branch_call(
         after(active, query_grad, taken), contexts, outer, pack, joined_width // inside
@@ -1030,9 +1029,6 @@
     *scaled, first_sums = first_call(
         order, joined_grad, pack, rows, stats, gains, second_scaled, ranks
     )
-
-    inner_whole = product_call([(after(second_in, scaled[0]), upper_grad)])
-    inner_out = lax.psum_scatter(inner_whole, group, scatter_dimension=0, tiled=True)
 
     column = jnp.concatenate([first_sums[:2], second_sums[:2], bias_grad.reshape(1, -1)])
     by_shard = [
@@ -1051,9 +1047,11 @@
             ((0, 0), (0, EXTRA - 1), (0, size - small_grads.shape[1])),
         )
     context = jnp.concatenate(contexts, axis=0)
-    head_pairs = [(after(first_in, inner_whole), joined_grad), (grad_rows, context)]
+    head_pairs = [(after(first_in, scaled[0]), joined_grad), (grad_rows, context)]
     head_given = weight_grad_given(head_pairs, group, riders)
-    head_pairs = [(after(first_in, head_given), joined_grad), (grad_rows, context)]
+    inner_whole = product_call([(after(second_in, head_given), upper_grad)])
+    inner_out = lax.psum_scatter(inner_whole, group, scatter_dimension=0, tiled=True)
+    head_pairs = [(after(first_in, head_given, inner_whole), joined_grad), (grad_rows, context)]
     head_terms = weight_grad_kept(head_pairs, head_given, group, riders)
     share = total_of(send_chunks(scaled, "tp"))
     lines = 2 * count // part

time: 540 us -> 534 us (0.989)
  starting transfers between devices: 101 us -> 89.9 us
  transfers between devices with their start and end apart: 36 -> 36, of which waited for: 21 -> 20; matrix products, arithmetic and copies ran while one was open for 7% -> 7% of each run, Pallas kernels for 37% -> 37%
where the time goes in v4:
time: 534 us; the launch traced here: 524 us
  Pallas kernels  211 us (40%)
  waiting for transfers between devices  161 us (30%)
  starting transfers between devices  89.9 us (17%)
  local copies, waits for them, and re-layouts  26.5 us (5%)
  other arithmetic  21.4 us (4%)
  between operations  15.1 us (3%)
    ppermute x5, waiting for transfers between devices, line_gather(): b = lax.ppermute(b, axis, down)  69.1 us
    ppermute x3, waiting for transfers between devices, send_chunks(): lax.ppermute(chunks[k], axis, [(i, (i + k) % size) for i in range(size)])  42.4 us
    pallas_call x2, Pallas kernels, product_call(): pl.pallas_call(functools.partial(product_kernel, sizes), grid=(sum(sizes)...  29.6 us
    ppermute x5, starting transfers between devices, line_gather(): a = lax.ppermute(a, axis, up)  25.9 us
    pallas_call x2, Pallas kernels, weight_grad_call(): pl.pallas_call(functools.partial(weight_grad_kernel, sizes, outs, int(sma...  24.2 us
    ppermute x3, starting transfers between devices, line_sum(): lax.ppermute(value, axis, [(i, (i + step) % size) for i in range(size)])  22.2 us
    pallas_call x2, Pallas kernels, backward_call(): pl.pallas_call(functools.partial(backward_kernel, heads, seq), grid_spec=...  17.7 us
    pallas_call x1, Pallas kernels, upper_call(): pl.pallas_call(upper_kernel, grid=(hidden // tile,), in_specs=[pl.BlockSp...  17.5 us
  transfers between devices with their start and end apart: 36, of which 20 were waited for; matrix products, arithmetic and copies ran while one was open for 7% of the time, Pallas kernels for 37%

profile of v4, /device:TPU:0, one launch (start us, length us, event | category | flops | bytes accessed | tf_op | source)
XLA Modules:
  0.0 524.4 jit_solution(11467561345604904930)
XLA Ops:
  12.8 5.6 %collective-permute-start = (bf16[1024,512]{1,0:T(8,128)(2,1)S(1)}, bf16[1024,512]{1,0:T(8,128)(2,1)S(1)}, u32[]{:S(2)}, u32[]{:S(2)}) collective-permute-start(bf16[1024,512]{1,0:T(8,128)(2,1)S(1)} %bitcast.94), channel_id=1, source_target_pairs={{0,1},{1,2},{2,3},{4,5},{5,6},{6,7},{8,9},{9,10},{10,11},{12,13},{... | collective-permute-start | bytes 3145736 | tf_op jit(solution)/shard_map/ppermute | solution.py:55
  18.4 21.2 %collective-permute-done.1.refs_5_ = bf16[1024,512]{1,0:T(8,128)(2,1)S(1)} collective-permute-done((bf16[1024,512]{1,0:T(8,128)(2,1)S(1)}, bf16[1024,512]{1,0:T(8,128)(2,1)S(1)}, u32[]{:S(2)}, u32[]{:S(2)}) %collective-permute-start.1) | collective-permute-done | bytes 1048608 | tf_op jit(solution)/shard_map/ppermute | solution.py:56
  40.9 4.6 collective-permute-start.4
  45.5 20.4 %collective-permute-done.2.refs_3_ = bf16[1024,512]{1,0:T(8,128)(2,1)} collective-permute-done((bf16[1024,512]{1,0:T(8,128)(2,1)S(1)}, bf16[1024,512]{1,0:T(8,128)(2,1)}, u32[]{:S(2)}, u32[]{:S(2)}) %collective-permute-start.2) | collective-permute-done | bytes 1048608 | tf_op jit(solution)/shard_map/ppermute | solution.py:56
  67.2 5.6 %collective-permute-start.5 = (bf16[1024,512]{1,0:T(8,128)(2,1)S(1)}, bf16[1024,512]{1,0:T(8,128)(2,1)}, u32[]{:S(2)}, u32[]{:S(2)}) collective-permute-start(bf16[1024,512]{1,0:T(8,128)(2,1)S(1)} %collective-permute-done.4.refs_2_), channel_id=1, source_target_pairs={{0,1},{1,2},{2,3},{4,5},{5,6},{6,7},{8,9},{9,10},{10,11},{12,13},{... | collective-permute-start | bytes 3145736 | tf_op jit(solution)/shard_map/ppermute | solution.py:55
  76.2 2.6 collective-permute-done.7
  80.2 11.3 %collective-permute-done.3.refs_1_ = bf16[1024,512]{1,0:T(8,128)(2,1)} collective-permute-done((bf16[1024,512]{1,0:T(8,128)(2,1)}, bf16[1024,512]{1,0:T(8,128)(2,1)}, u32[]{:S(2)}, u32[]{:S(2)}) %collective-permute-start.3) | collective-permute-done | bytes 1048608 | tf_op jit(solution)/shard_map/ppermute | solution.py:56
  93.7 6.1 %collective-permute-start.9 = (bf16[1024,512]{1,0:T(8,128)(2,1)S(1)}, bf16[1024,512]{1,0:T(8,128)(2,1)}, u32[]{:S(2)}, u32[]{:S(2)}) collective-permute-start(bf16[1024,512]{1,0:T(8,128)(2,1)S(1)} %bitcast.100), channel_id=1, source_target_pairs={{0,1},{1,2},{2,3},{4,5},{5,6},{6,7},{8,9},{9,10},{10,11},{12,13},{... | collective-permute-start | bytes 3145736 | tf_op jit(solution)/shard_map/ppermute | solution.py:937
  103.4 11.7 %norm.1 = (bf16[1024,2048]{1,0:T(8,128)(2,1)}, bf16[1024,2048]{1,0:T(8,128)(2,1)}, bf16[1024,2048]{1,0:T(8,128)(2,1)}, f32[1024,128]{1,0:T(8,128)}) custom-call(s32[1]{0:T(128)} %bitcast.1.me_ref, bf16[1024,512]{1,0:T(8,128)(2,1)} %bitcast.92, bf16[1024,512]{1,0:T(8,128)(2,1)} %copy-done.19, bf16[1024,512]{1,0:T(8,128)(2,1)} %collective-permute-done.3.refs_1_, ...), custom_call_target="tpu_custom_call" | custom-call | flops 33554432 | bytes 20971520 | tf_op jit(solution)/shard_map/norm/pallas_call | solution.py:102
  115.1 2.4 collective-permute-done.10.refs_5_
  119.2 13.3 %joined.1 = (bf16[1024,512]{1,0:T(8,128)(2,1)}, bf16[2,512,1024]{2,1,0:T(8,128)(2,1)}) custom-call(bf16[1024,2048]{1,0:T(8,128)(2,1)} %get-tuple-element.126.rows_ref.refs_0_.refs_1_.refs_2_.refs_3_, bf16[8,256,2048]{2,1,0:T(8,128)(2,1)} %bitcast.88, f32[8,1536]{1,0:T(8,128)} %broadcast_in_dim.34.bias_ref, f32[512,384]{1,0:T(8,128)} %concatenate.35.table_ref.refs_8_), custom_call_target="tpu_custom_call" | custom-call | flops 6442450944 | bytes 10485760 | tf_op jit(solution)/shard_map/joined/pallas_call | solution.py:220
  133.9 5.2 collective-permute-start.11
  140.5 17.5 %upper.1 = (bf16[1024,2048]{1,0:T(8,128)(2,1)}, bf16[1024,2048]{1,0:T(8,128)(2,1)}) custom-call(bf16[1024,2048]{1,0:T(8,128)(2,1)} %get-tuple-element.125.rows_ref.refs_0_, bf16[8,256,2048]{2,1,0:T(8,128)(2,1)} %bitcast.125, f32[8,2048]{1,0:T(8,128)} %broadcast_in_dim.39.bias_ref), custom_call_target="tpu_custom_call" | custom-call | flops 8589934592 | bytes 12582912 | tf_op jit(solution)/shard_map/upper/pallas_call | solution.py:477
  159.5 5.0 collective-permute-start.14
  165.1 16.3 %collective-permute-done.13.refs_1_ = bf16[1024,512]{1,0:T(8,128)(2,1)S(1)} collective-permute-done((bf16[1024,512]{1,0:T(8,128)(2,1)S(1)}, bf16[1024,512]{1,0:T(8,128)(2,1)S(1)}, u32[]{:S(2)}, u32[]{:S(2)}) %collective-permute-start.13) | collective-permute-done | bytes 1048608 | tf_op jit(solution)/shard_map/ppermute | solution.py:56
  183.6 7.1 %cotangent_rows.1 = (bf16[1024,2048]{1,0:T(8,128)(2,1)}, f32[8,2048]{1,0:T(8,128)}) custom-call(s32[2]{0:T(128)} %pad_add_fusion.me_ref, s32[2]{0:T(128)} %lens.7, bf16[1024,512]{1,0:T(8,128)(2,1)} %bitcast.98, bf16[1024,512]{1,0:T(8,128)(2,1)} %collective-permute-done.9.refs_0_, bf16[1024,512]{1,0:T(8,128)(2,1)} %copy-done.16, ...), custom_call_target="tpu_custom_call" | custom-call | flops 8388608 | bytes 12582912 | tf_op jit(solution)/shard_map/cotangent_rows/pallas_call | solution.py:158
  190.7 3.1 all-gather.14.cloned.1.call-done
  194.5 5.7 %attention_forward.2 = (bf16[512,512]{1,0:T(8,128)(2,1)}, f32[512,256]{1,0:T(8,128)}) custom-call(s32[5]{0:T(128)} %stack.32.info, s32[2]{0:T(128)} %lens.7, bf16[1024,512]{1,0:T(8,128)(2,1)} %get-tuple-element.94.query_ref, bf16[4,2,512,1024]{3,2,1,0:T(8,128)(2,1)} %bitcast.84), custom_call_target="tpu_custom_call" | custom-call | flops 2147483648 | bytes 4194304 | tf_op jit(solution)/shard_map/attention_forward/pallas_call | solution.py:313
  200.2 8.4 %attention_forward.3 = (bf16[512,512]{1,0:T(8,128)(2,1)}, f32[512,256]{1,0:T(8,128)}) custom-call(s32[5]{0:T(128)} %stack.32.info, s32[2]{0:T(128)} %lens.7, bf16[1024,512]{1,0:T(8,128)(2,1)} %get-tuple-element.94.query_ref, bf16[4,2,512,1024]{3,2,1,0:T(8,128)(2,1)} %bitcast.85), custom_call_target="tpu_custom_call" | custom-call | flops 2147483648 | bytes 4194304 | tf_op jit(solution)/shard_map/attention_forward/pallas_call | solution.py:313
  208.6 5.5 %context_grad.1.grad_ref = bf16[1024,512]{1,0:T(8,128)(2,1)} custom-call(bf16[1024,2048]{1,0:T(8,128)(2,1)} %get-tuple-element.102.rows_ref.refs_0_.refs_4_.refs_5_.refs_6_.refs_7_, bf16[8,256,2048]{2,1,0:T(8,128)(2,1)} %bitcast.89), custom_call_target="tpu_custom_call" | custom-call | flops 2147483648 | bytes 6291456 | tf_op jit(solution)/shard_map/context_grad/pallas_call | solution.py:531
  214.1 8.2 %attention_backward.2 = (bf16[512,512]{1,0:T(8,128)(2,1)}, bf16[512,1024]{1,0:T(8,128)(2,1)}, bf16[512,1024]{1,0:T(8,128)(2,1)}, bf16[2,512,1024]{2,1,0:T(8,128)(2,1)}) custom-call(s32[5]{0:T(128)} %stack.32.info, s32[2]{0:T(128)} %lens.7, bf16[1024,512]{1,0:T(8,128)(2,1)} %get-tuple-element.94.query_ref, ...), custom_call_target="tpu_custom_call" | custom-call | flops 5368709120 | bytes 8388608 | tf_op jit(solution)/shard_map/attention_backward/pallas_call | solution.py:395
  222.4 9.4 %attention_backward.3 = (bf16[512,512]{1,0:T(8,128)(2,1)}, bf16[512,1024]{1,0:T(8,128)(2,1)}, bf16[512,1024]{1,0:T(8,128)(2,1)}, bf16[2,512,1024]{2,1,0:T(8,128)(2,1)}) custom-call(s32[5]{0:T(128)} %stack.32.info, s32[2]{0:T(128)} %lens.7, bf16[1024,512]{1,0:T(8,128)(2,1)} %get-tuple-element.94.query_ref, ...), custom_call_target="tpu_custom_call" | custom-call | flops 5368709120 | bytes 8388608 | tf_op jit(solution)/shard_map/attention_backward/pallas_call | solution.py:395
  231.8 5.6 %collective-permute-start.15 = (bf16[2,512,1024]{2,1,0:T(8,128)(2,1)}, bf16[2,512,1024]{2,1,0:T(8,128)(2,1)S(1)}, u32[]{:S(2)}, u32[]{:S(2)}) collective-permute-start(bf16[2,512,1024]{2,1,0:T(8,128)(2,1)} %get-tuple-element.97), channel_id=1, source_target_pairs={{0,4},{4,0},{8,12},{12,8},{1,5},{5,1},{9,13},{13,9},{2,6},{6,2},{1... | collective-permute-start | bytes 6291464 | tf_op jit(solution)/shard_map/ppermute | solution.py:423
  237.4 4.6 collective-permute-done.15.refs_6_
  242.0 8.1 %all-gather.8.cloned.1.call-done.refs_2_.weight_ref = bf16[2048,2048]{1,0:T(8,128)(2,1)} async-done(((bf16[256,2048]{1,0:T(8,128)(2,1)}), bf16[2048,2048]{1,0:T(8,128)(2,1)}) %all-gather.8.cloned.1.call-update) | async-done | bytes 8388624 | tf_op jit(solution)/shard_map/all_gather | solution.py:983
  250.1 16.0 %branch.1 = bf16[1024,2048]{1,0:T(8,128)(2,1)} custom-call(bf16[1024,2048]{1,0:T(8,128)(2,1)} %get-tuple-element.98.active_ref.refs_1_, bf16[512,512]{1,0:T(8,128)(2,1)} %get-tuple-element.87.context_ref.refs_0_, bf16[512,512]{1,0:T(8,128)(2,1)} %get-tuple-element.89.context_ref.refs_1_, bf16[2048,2048]{1,0:T(8,128)(2,1)} %all-gather.8.cloned.1.call-done.refs_2_.weight_ref, ...), custom_call_target="tpu_custom_call" | custom-call | flops 10737418240 | bytes 10485760 | tf_op jit(solution)/shard_map/branch/pallas_call | solution.py:440
  266.2 14.7 %product.2 = bf16[2048,2048]{1,0:T(8,128)(2,1)} custom-call(bf16[1024,2048]{1,0:T(8,128)(2,1)} %get-tuple-element.102.rows_ref.refs_0_.refs_4_.refs_5_.refs_6_.refs_7_, bf16[1024,2048]{1,0:T(8,128)(2,1)} %get-tuple-element.98.active_ref.refs_1_), custom_call_target="tpu_custom_call" | custom-call | flops 8589934592 | bytes 16777216 | tf_op jit(solution)/shard_map/product/pallas_call | solution.py:848
  290.5 13.9 %upper_grad.1 = (bf16[1024,2048]{1,0:T(8,128)(2,1)}, f32[8,2048]{1,0:T(8,128)}) custom-call(bf16[1024,2048]{1,0:T(8,128)(2,1)} %get-tuple-element.102.rows_ref.refs_0_.refs_4_.refs_5_.refs_6_.refs_7_, bf16[2048,2048]{1,0:T(8,128)(2,1)} %all-gather.8.cloned.1.call-done.refs_2_.weight_ref, bf16[1024,2048]{1,0:T(8,128)(2,1)} %get-tuple-element.103.slope_ref), custom_call_target="tpu_custom_call" | custom-call | flops 8589934592 | bytes 16777216 | tf_op jit(solution)/shard_map/upper_grad/pallas_call | solution.py:506
  304.5 15.0 %second_in_grad.1 = (bf16[1024,2048]{1,0:T(8,128)(2,1)}, f32[8,2048]{1,0:T(8,128)}) custom-call(bf16[1024,2048]{1,0:T(8,128)(2,1)} %get-tuple-element.104.grad_ref.refs_1_, bf16[8,256,2048]{2,1,0:T(8,128)(2,1)} %bitcast.126, bf16[1024,2048]{1,0:T(8,128)(2,1)} %get-tuple-element.105.rows_ref, f32[1024,128]{1,0:T(8,128)} %get-tuple-element.100.stat_ref, ...), custom_call_target="tpu_custom_call" | custom-call | flops 8589934592 | bytes 20971520 | tf_op jit(solution)/shard_map/second_in_grad/pallas_call | solution.py:566
  320.3 15.2 %collective-permute-done.17.refs_3_ = bf16[512,1024]{1,0:T(8,128)(2,1)S(1)} collective-permute-done((bf16[512,1024]{1,0:T(8,128)(2,1)S(1)}, bf16[512,1024]{1,0:T(8,128)(2,1)S(1)}, u32[]{:S(2)}, u32[]{:S(2)}) %collective-permute-start.17) | collective-permute-done | bytes 1048608 | tf_op jit(solution)/shard_map/ppermute | solution.py:425
  336.5 7.9 %joined_grad.1 = (bf16[1024,1536]{1,0:T(8,128)(2,1)}, f32[8,1536]{1,0:T(8,128)}) custom-call(bf16[512,512]{1,0:T(8,128)(2,1)} %get-tuple-element.107.refs_0_, bf16[512,1024]{1,0:T(8,128)(2,1)} %get-tuple-element.108.refs_1_, bf16[2,512,1024]{2,1,0:T(8,128)(2,1)} %collective-permute-done.16.refs_2_, bf16[512,1024]{1,0:T(8,128)(2,1)} %copy-done.12, ...), custom_call_target="tpu_custom_call" | custom-call | flops 15728640 | bytes 15728640 | tf_op jit(solution)/shard_map/joined_grad/pallas_call | solution.py:625
  345.4 17.4 %first_in_grad.1 = (bf16[1032,512]{1,0:T(8,128)(2,1)}, bf16[1032,512]{1,0:T(8,128)(2,1)}, bf16[1032,512]{1,0:T(8,128)(2,1)}, bf16[1032,512]{1,0:T(8,128)(2,1)}, f32[8,2048]{1,0:T(8,128)}) custom-call(s32[4]{0:T(128)} %compare_select_fusion.order, bf16[1024,1536]{1,0:T(8,128)(2,1)} %get-tuple-element.114.grad_ref.refs_8_, bf16[8,256,2048]{2,1,0:T(8,128)(2,1)} %bitcast.91, ...), custom_call_target="tpu_custom_call" | custom-call | flops 6442450944 | bytes 23068672 | tf_op jit(solution)/shard_map/first_in_grad/pallas_call | solution.py:683
  366.5 12.1 %weight_grad.2 = bf16[1056,2048]{1,0:T(8,128)(2,1)} custom-call(s32[4]{0:T(128)} %fusion.17.order, bf16[1024,2048]{1,0:T(8,128)(2,1)} %get-tuple-element.126.rows_ref.refs_0_.refs_1_.refs_2_.refs_3_, bf16[1024,2048]{1,0:T(8,128)(2,1)} %get-tuple-element.126.rows_ref.refs_0_.refs_1_.refs_2_.refs_3_, ...), custom_call_target="tpu_custom_call" | custom-call | flops 4294967296 | bytes 14680064 | tf_op jit(solution)/shard_map/weight_grad/pallas_call | solution.py:795
  378.6 14.9 %product.3 = bf16[2048,2048]{1,0:T(8,128)(2,1)} custom-call(bf16[1024,2048]{1,0:T(8,128)(2,1)} %get-tuple-element.125.rows_ref.refs_0_, bf16[1024,2048]{1,0:T(8,128)(2,1)} %get-tuple-element.104.grad_ref.refs_1_), custom_call_target="tpu_custom_call" | custom-call | flops 8589934592 | bytes 16777216 | tf_op jit(solution)/shard_map/product/pallas_call | solution.py:848
  395.4 2.4 collective-permute-start.20
  401.3 12.1 %weight_grad.3 = (bf16[264,2048]{1,0:T(8,128)(2,1)}, bf16[264,2048]{1,0:T(8,128)(2,1)}, bf16[264,2048]{1,0:T(8,128)(2,1)}, bf16[264,2048]{1,0:T(8,128)(2,1)}) custom-call(s32[4]{0:T(128)} %fusion.18.order, bf16[1024,2048]{1,0:T(8,128)(2,1)} %get-tuple-element.126.rows_ref.refs_0_.refs_1_.refs_2_.refs_3_, ...), custom_call_target="tpu_custom_call" | custom-call | flops 4294967296 | bytes 14680064 | tf_op jit(solution)/shard_map/weight_grad/pallas_call | solution.py:795
  413.5 5.5 %collective-permute-start.24 = (bf16[264,2048]{1,0:T(8,128)(2,1)}, bf16[264,2048]{1,0:T(8,128)(2,1)}, u32[]{:S(2)}, u32[]{:S(2)}) collective-permute-start(bf16[264,2048]{1,0:T(8,128)(2,1)} %get-tuple-element.130), channel_id=1, source_target_pairs={{0,16},{4,20},{8,24},{12,28},{16,0},{20,4},{24,8},{28,12},{1,17},{... | collective-permute-start | bytes 3244040 | tf_op jit(solution)/shard_map/ppermute | solution.py:882
  419.0 2.9 collective-permute-done.19
  423.0 4.4 collective-permute-start.25
  427.4 39.4 %collective-permute-done.20 = bf16[1032,512]{1,0:T(8,128)(2,1)S(1)} collective-permute-done((bf16[1032,512]{1,0:T(8,128)(2,1)}, bf16[1032,512]{1,0:T(8,128)(2,1)S(1)}, u32[]{:S(2)}, u32[]{:S(2)}) %collective-permute-start.20) | collective-permute-done | bytes 1056800 | tf_op jit(solution)/shard_map/ppermute | solution.py:65
  467.8 2.4 convert_add_fusion.2
  470.3 3.6 fusion.7
  473.9 5.2 collective-permute-done.25
  479.1 2.7 convert_add_fusion.1
  481.8 19.1 %collective-permute-start.28 = (f32[8,128]{1,0:T(8,128)S(1)}, f32[8,128]{1,0:T(8,128)S(1)}, u32[]{:S(2)}, u32[]{:S(2)}) collective-permute-start(f32[8,128]{1,0:T(8,128)S(1)} %bitcast.117), channel_id=1, source_target_pairs={{0,3},{1,0},{2,1},{3,2},{4,7},{5,4},{6,5},{7,6},{8,11},{9,8},{10,9... | collective-permute-start | bytes 12296 | tf_op jit(solution)/shard_map/ppermute | solution.py:894
  505.7 2.2 reshape.213
  509.6 2.8 convert_element_type.124
  514.0 2.8 convert_element_type.123
  (200 shorter events, 60.1 us)
Async XLA Ops:
  7.2 111.4 %all-gather.10.cloned.1.call-start = ((), (), s32[]{:S(2)}) async-start(), calls=%async_computation.7 | async-start | bytes 9437184 | tf_op jit(solution)/shard_map/all_gather | solution.py:940
  9.4 63.3 %copy-start.30 = (bf16[2,96]{1,0:T(2,128)(2,1)S(1)}, bf16[2,96]{1,0:T(2,128)(2,1)}, u32[]{:S(2)}) copy-start(bf16[2,96]{1,0:T(2,128)(2,1)} %param.23) | copy-start | bytes 1156
  9.5 63.4 %copy-start.23 = (bf16[64,4]{0,1:T(4,128)(2,1)S(1)}, bf16[64,4]{0,1:T(4,128)(2,1)}, u32[]{:S(2)}) copy-start(bf16[64,4]{0,1:T(4,128)(2,1)} %param.29) | copy-start | bytes 1540
  9.5 63.6 %copy-start.24 = (bf16[256]{0:T(256)(128)(2,1)S(1)}, bf16[256]{0:T(256)(128)(2,1)}, u32[]{:S(2)}) copy-start(bf16[256]{0:T(256)(128)(2,1)} %param.20) | copy-start | bytes 1540
  9.5 63.6 %copy-start.25 = (bf16[256]{0:T(256)(128)(2,1)S(1)}, bf16[256]{0:T(256)(128)(2,1)}, u32[]{:S(2)}) copy-start(bf16[256]{0:T(256)(128)(2,1)} %param.21) | copy-start | bytes 1540
  9.5 63.6 %copy-start.26 = (bf16[256]{0:T(256)(128)(2,1)S(1)}, bf16[256]{0:T(256)(128)(2,1)}, u32[]{:S(2)}) copy-start(bf16[256]{0:T(256)(128)(2,1)} %param.26) | copy-start | bytes 1540
  9.5 63.6 %copy-start.27 = (bf16[256]{0:T(256)(128)(2,1)S(1)}, bf16[256]{0:T(256)(128)(2,1)}, u32[]{:S(2)}) copy-start(bf16[256]{0:T(256)(128)(2,1)} %param.27) | copy-start | bytes 1540
  9.5 63.6 %copy-start.28 = (bf16[256]{0:T(256)(128)(2,1)S(1)}, bf16[256]{0:T(256)(128)(2,1)}, u32[]{:S(2)}) copy-start(bf16[256]{0:T(256)(128)(2,1)} %param.25) | copy-start | bytes 1540
  9.5 63.6 %copy-start.29 = (bf16[256]{0:T(256)(128)(2,1)S(1)}, bf16[256]{0:T(256)(128)(2,1)}, u32[]{:S(2)}) copy-start(bf16[256]{0:T(256)(128)(2,1)} %param.31) | copy-start | bytes 1540
  9.5 82.9 %copy-start.13 = (bf16[2,512,512]{2,1,0:T(8,128)(2,1)S(1)}, bf16[2,512,512]{2,1,0:T(8,128)(2,1)}, u32[]{:S(2)}) copy-start(bf16[2,512,512]{2,1,0:T(8,128)(2,1)} %param.19) | copy-start | bytes 3145732
  10.7 129.2 %all-gather.12.cloned.1.call-start = ((), (), s32[]{:S(2)}) async-start(), calls=%async_computation.8 | async-start | bytes 9437184 | tf_op jit(solution)/shard_map/all_gather | solution.py:941
  11.4 182.4 %all-gather.14.cloned.1.call-start = ((), (), s32[]{:S(2)}) async-start(), calls=%async_computation.9 | async-start | bytes 10485760 | tf_op jit(solution)/shard_map/all_gather | solution.py:976
  11.5 28.1 %collective-permute-start.1 = (bf16[1024,512]{1,0:T(8,128)(2,1)S(1)}, bf16[1024,512]{1,0:T(8,128)(2,1)S(1)}, u32[]{:S(2)}, u32[]{:S(2)}) collective-permute-start(bf16[1024,512]{1,0:T(8,128)(2,1)S(1)} %bitcast.93), channel_id=1, source_target_pairs={{1,0},{2,1},{3,2},{5,4},{6,5},{7,6},{9,8},{10,9},{11,10},{13,12},{... | collective-permute-start | bytes 3145736 | tf_op jit(solution)/shard_map/ppermute | solution.py:56
  12.8 28.1 %collective-permute-start = (bf16[1024,512]{1,0:T(8,128)(2,1)S(1)}, bf16[1024,512]{1,0:T(8,128)(2,1)S(1)}, u32[]{:S(2)}, u32[]{:S(2)}) collective-permute-start(bf16[1024,512]{1,0:T(8,128)(2,1)S(1)} %bitcast.94), channel_id=1, source_target_pairs={{0,1},{1,2},{2,3},{4,5},{5,6},{6,7},{8,9},{9,10},{10,11},{12,13},{... | collective-permute-start | bytes 3145736 | tf_op jit(solution)/shard_map/ppermute | solution.py:55
  39.6 26.3 %collective-permute-start.2 = (bf16[1024,512]{1,0:T(8,128)(2,1)S(1)}, bf16[1024,512]{1,0:T(8,128)(2,1)}, u32[]{:S(2)}, u32[]{:S(2)}) collective-permute-start(bf16[1024,512]{1,0:T(8,128)(2,1)S(1)} %collective-permute-done.1.refs_5_), channel_id=1, source_target_pairs={{1,0},{2,1},{3,2},{5,4},{6,5},{7,6},{9,8},{10,9},{11,10},{13,12},{... | collective-permute-start | bytes 3145736 | tf_op jit(solution)/shard_map/ppermute | solution.py:56
  40.9 26.3 %collective-permute-start.4 = (bf16[1024,512]{1,0:T(8,128)(2,1)S(1)}, bf16[1024,512]{1,0:T(8,128)(2,1)S(1)}, u32[]{:S(2)}, u32[]{:S(2)}) collective-permute-start(bf16[1024,512]{1,0:T(8,128)(2,1)S(1)} %collective-permute-done.refs_0_), channel_id=1, source_target_pairs={{0,1},{1,2},{2,3},{4,5},{5,6},{6,7},{8,9},{9,10},{10,11},{12,13},{... | collective-permute-start | bytes 3145736 | tf_op jit(solution)/shard_map/ppermute | solution.py:55
  65.9 25.6 %collective-permute-start.3 = (bf16[1024,512]{1,0:T(8,128)(2,1)}, bf16[1024,512]{1,0:T(8,128)(2,1)}, u32[]{:S(2)}, u32[]{:S(2)}) collective-permute-start(bf16[1024,512]{1,0:T(8,128)(2,1)} %collective-permute-done.2.refs_3_), channel_id=1, source_target_pairs={{1,0},{2,1},{3,2},{5,4},{6,5},{7,6},{9,8},{10,9},{11,10},{13,12},{... | collective-permute-start | bytes 3145736 | tf_op jit(solution)/shard_map/ppermute | solution.py:56
  67.2 25.2 %collective-permute-start.5 = (bf16[1024,512]{1,0:T(8,128)(2,1)S(1)}, bf16[1024,512]{1,0:T(8,128)(2,1)}, u32[]{:S(2)}, u32[]{:S(2)}) collective-permute-start(bf16[1024,512]{1,0:T(8,128)(2,1)S(1)} %collective-permute-done.4.refs_2_), channel_id=1, source_target_pairs={{0,1},{1,2},{2,3},{4,5},{5,6},{6,7},{8,9},{9,10},{10,11},{12,13},{... | collective-permute-start | bytes 3145736 | tf_op jit(solution)/shard_map/ppermute | solution.py:55
  73.4 1.3 collective-permute-start.6
  74.8 4.0 collective-permute-start.7
  78.8 23.6 %collective-permute-start.8 = (bf16[8,2048]{1,0:T(8,128)(2,1)S(1)}, bf16[8,2048]{1,0:T(8,128)(2,1)S(1)}, u32[]{:S(2)}, u32[]{:S(2)}) collective-permute-start(bf16[8,2048]{1,0:T(8,128)(2,1)S(1)} %add.115), channel_id=1, source_target_pairs={{0,16},{4,20},{8,24},{12,28},{16,0},{20,4},{24,8},{28,12},{1,17},{... | collective-permute-start | bytes 98312 | tf_op jit(solution)/shard_map/ppermute | solution.py:726
  92.4 25.1 %collective-permute-start.10 = (bf16[1024,512]{1,0:T(8,128)(2,1)S(1)}, bf16[1024,512]{1,0:T(8,128)(2,1)}, u32[]{:S(2)}, u32[]{:S(2)}) collective-permute-start(bf16[1024,512]{1,0:T(8,128)(2,1)S(1)} %bitcast.99), channel_id=1, source_target_pairs={{1,0},{2,1},{3,2},{5,4},{6,5},{7,6},{9,8},{10,9},{11,10},{13,12},{... | collective-permute-start | bytes 3145736 | tf_op jit(solution)/shard_map/ppermute | solution.py:938
  93.7 24.9 %collective-permute-start.9 = (bf16[1024,512]{1,0:T(8,128)(2,1)S(1)}, bf16[1024,512]{1,0:T(8,128)(2,1)}, u32[]{:S(2)}, u32[]{:S(2)}) collective-permute-start(bf16[1024,512]{1,0:T(8,128)(2,1)S(1)} %bitcast.100), channel_id=1, source_target_pairs={{0,1},{1,2},{2,3},{4,5},{5,6},{6,7},{8,9},{9,10},{10,11},{12,13},{... | collective-permute-start | bytes 3145736 | tf_op jit(solution)/shard_map/ppermute | solution.py:937
  132.5 117.5 %all-gather.8.cloned.1.call-start = ((), (), s32[]{:S(2)}) async-start(), calls=%async_computation.3 | async-start | bytes 9437184 | tf_op jit(solution)/shard_map/all_gather | solution.py:983
  132.6 25.4 %collective-permute-start.12 = (bf16[1024,512]{1,0:T(8,128)(2,1)}, bf16[1024,512]{1,0:T(8,128)(2,1)S(1)}, u32[]{:S(2)}, u32[]{:S(2)}) collective-permute-start(bf16[1024,512]{1,0:T(8,128)(2,1)} %collective-permute-done.10.refs_5_), channel_id=1, source_target_pairs={{1,0},{2,1},{3,2},{5,4},{6,5},{7,6},{9,8},{10,9},{11,10},{13,12},{... | collective-permute-start | bytes 3145736 | tf_op jit(solution)/shard_map/ppermute | solution.py:56
  133.9 24.3 %collective-permute-start.11 = (bf16[1024,512]{1,0:T(8,128)(2,1)}, bf16[1024,512]{1,0:T(8,128)(2,1)S(1)}, u32[]{:S(2)}, u32[]{:S(2)}) collective-permute-start(bf16[1024,512]{1,0:T(8,128)(2,1)} %collective-permute-done.9.refs_0_), channel_id=1, source_target_pairs={{0,1},{1,2},{2,3},{4,5},{5,6},{6,7},{8,9},{9,10},{10,11},{12,13},{... | collective-permute-start | bytes 3145736 | tf_op jit(solution)/shard_map/ppermute | solution.py:55
  158.2 23.1 %collective-permute-start.13 = (bf16[1024,512]{1,0:T(8,128)(2,1)S(1)}, bf16[1024,512]{1,0:T(8,128)(2,1)S(1)}, u32[]{:S(2)}, u32[]{:S(2)}) collective-permute-start(bf16[1024,512]{1,0:T(8,128)(2,1)S(1)} %collective-permute-done.12.refs_3_), channel_id=1, source_target_pairs={{1,0},{2,1},{3,2},{5,4},{6,5},{7,6},{9,8},{10,9},{11,10},{13,12},{... | collective-permute-start | bytes 3145736 | tf_op jit(solution)/shard_map/ppermute | solution.py:56
  159.5 23.0 %collective-permute-start.14 = (bf16[1024,512]{1,0:T(8,128)(2,1)S(1)}, bf16[1024,512]{1,0:T(8,128)(2,1)S(1)}, u32[]{:S(2)}, u32[]{:S(2)}) collective-permute-start(bf16[1024,512]{1,0:T(8,128)(2,1)S(1)} %collective-permute-done.11.refs_2_), channel_id=1, source_target_pairs={{0,1},{1,2},{2,3},{4,5},{5,6},{6,7},{8,9},{9,10},{10,11},{12,13},{... | collective-permute-start | bytes 3145736 | tf_op jit(solution)/shard_map/ppermute | solution.py:55
  193.8 276.4 %reduce-scatter.4.cloned.1.call-start = ((), (), s32[]{:S(2)}) async-start(), calls=%async_computation.4 | async-start | bytes 5242880 | tf_op jit(solution)/shard_map/reduce_scatter | solution.py:1005
  231.8 10.2 %collective-permute-start.15 = (bf16[2,512,1024]{2,1,0:T(8,128)(2,1)}, bf16[2,512,1024]{2,1,0:T(8,128)(2,1)S(1)}, u32[]{:S(2)}, u32[]{:S(2)}) collective-permute-start(bf16[2,512,1024]{2,1,0:T(8,128)(2,1)} %get-tuple-element.97), channel_id=1, source_target_pairs={{0,4},{4,0},{8,12},{12,8},{1,5},{5,1},{9,13},{13,9},{2,6},{6,2},{1... | collective-permute-start | bytes 6291464 | tf_op jit(solution)/shard_map/ppermute | solution.py:423
  242.0 43.5 %copy-start.1 = (bf16[2,512,1024]{2,1,0:T(8,128)(2,1)}, bf16[2,512,1024]{2,1,0:T(8,128)(2,1)S(1)}, u32[]{:S(2)}) copy-start(bf16[2,512,1024]{2,1,0:T(8,128)(2,1)S(1)} %collective-permute-done.15.refs_6_) | copy-start | bytes 6291460
  266.1 243.5 %reduce-scatter.8.cloned.1.call-start = ((), (), s32[]{:S(2)}) async-start(), calls=%async_computation.6 | async-start | bytes 9437184 | tf_op jit(solution)/shard_map/reduce_scatter | solution.py:1012
  280.9 233.1 %reduce-scatter.6.cloned.1.call-start = ((), (), s32[]{:S(2)}) async-start(), calls=%async_computation.5 | async-start | bytes 9437184 | tf_op jit(solution)/shard_map/reduce_scatter | solution.py:1053
  280.9 6.2 %collective-permute-start.16 = (bf16[2,512,1024]{2,1,0:T(8,128)(2,1)}, bf16[2,512,1024]{2,1,0:T(8,128)(2,1)}, u32[]{:S(2)}, u32[]{:S(2)}) collective-permute-start(bf16[2,512,1024]{2,1,0:T(8,128)(2,1)} %get-tuple-element.109), channel_id=1, source_target_pairs={{0,4},{4,0},{8,12},{12,8},{1,5},{5,1},{9,13},{13,9},{2,6},{6,2},{1... | collective-permute-start | bytes 6291464 | tf_op jit(solution)/shard_map/ppermute | solution.py:423
  285.8 34.4 %collective-permute-start.18 = (bf16[512,1024]{1,0:T(8,128)(2,1)S(1)}, bf16[512,1024]{1,0:T(8,128)(2,1)S(1)}, u32[]{:S(2)}, u32[]{:S(2)}) collective-permute-start(bf16[512,1024]{1,0:T(8,128)(2,1)S(1)} %fusion.8), channel_id=1, source_target_pairs={{8,0},{12,4},{9,1},{13,5},{10,2},{14,6},{11,3},{15,7},{24,16},{28,... | collective-permute-start | bytes 3145736 | tf_op jit(solution)/shard_map/ppermute | solution.py:425
  288.8 46.7 %collective-permute-start.17 = (bf16[512,1024]{1,0:T(8,128)(2,1)S(1)}, bf16[512,1024]{1,0:T(8,128)(2,1)S(1)}, u32[]{:S(2)}, u32[]{:S(2)}) collective-permute-start(bf16[512,1024]{1,0:T(8,128)(2,1)S(1)} %fusion.9), channel_id=1, source_target_pairs={{8,0},{12,4},{9,1},{13,5},{10,2},{14,6},{11,3},{15,7},{24,16},{28,... | collective-permute-start | bytes 3145736 | tf_op jit(solution)/shard_map/ppermute | solution.py:425
  393.5 7.8 %collective-permute-start.22 = (bf16[1056,2048]{1,0:T(8,128)(2,1)}, bf16[1056,2048]{1,0:T(8,128)(2,1)}, u32[]{:S(2)}, u32[]{:S(2)}) collective-permute-start(bf16[1056,2048]{1,0:T(8,128)(2,1)} %weight_grad.2), channel_id=1, source_target_pairs={{0,4},{4,0},{8,12},{12,8},{16,20},{20,16},{24,28},{28,24},{1,5},{5... | collective-permute-start | bytes 12976136 | tf_op jit(solution)/shard_map/ppermute | solution.py:877
  393.7 28.3 %collective-permute-start.19 = (bf16[1032,512]{1,0:T(8,128)(2,1)}, bf16[1032,512]{1,0:T(8,128)(2,1)S(1)}, u32[]{:S(2)}, u32[]{:S(2)}) collective-permute-start(bf16[1032,512]{1,0:T(8,128)(2,1)} %get-tuple-element.116), channel_id=1, source_target_pairs={{0,1},{1,2},{2,3},{3,0},{4,5},{5,6},{6,7},{7,4},{8,9},{9,10},{10,1... | collective-permute-start | bytes 3170312 | tf_op jit(solution)/shard_map/ppermute | solution.py:65
  395.4 71.4 %collective-permute-start.20 = (bf16[1032,512]{1,0:T(8,128)(2,1)}, bf16[1032,512]{1,0:T(8,128)(2,1)S(1)}, u32[]{:S(2)}, u32[]{:S(2)}) collective-permute-start(bf16[1032,512]{1,0:T(8,128)(2,1)} %get-tuple-element.117), channel_id=1, source_target_pairs={{0,2},{1,3},{2,0},{3,1},{4,6},{5,7},{6,4},{7,5},{8,10},{9,11},{10,... | collective-permute-start | bytes 3170312 | tf_op jit(solution)/shard_map/ppermute | solution.py:65
  397.9 70.0 %collective-permute-start.21 = (bf16[1032,512]{1,0:T(8,128)(2,1)}, bf16[1032,512]{1,0:T(8,128)(2,1)}, u32[]{:S(2)}, u32[]{:S(2)}) collective-permute-start(bf16[1032,512]{1,0:T(8,128)(2,1)} %get-tuple-element.118), channel_id=1, source_target_pairs={{0,3},{1,0},{2,1},{3,2},{4,7},{5,4},{6,5},{7,6},{8,11},{9,8},{10,9... | collective-permute-start | bytes 3170312 | tf_op jit(solution)/shard_map/ppermute | solution.py:65
  400.4 67.4 %copy-start.6 = (bf16[1032,512]{1,0:T(8,128)(2,1)S(1)}, bf16[1032,512]{1,0:T(8,128)(2,1)}, u32[]{:S(2)}) copy-start(bf16[1032,512]{1,0:T(8,128)(2,1)} %get-tuple-element.115) | copy-start | bytes 3170308
  413.4 60.5 %collective-permute-start.23 = (bf16[264,2048]{1,0:T(8,128)(2,1)}, bf16[264,2048]{1,0:T(8,128)(2,1)}, u32[]{:S(2)}, u32[]{:S(2)}) collective-permute-start(bf16[264,2048]{1,0:T(8,128)(2,1)} %get-tuple-element.128), channel_id=1, source_target_pairs={{0,8},{4,12},{8,0},{12,4},{16,24},{20,28},{24,16},{28,20},{1,9},{5... | collective-permute-start | bytes 3244040 | tf_op jit(solution)/shard_map/ppermute | solution.py:882
  413.5 60.4 %collective-permute-start.24 = (bf16[264,2048]{1,0:T(8,128)(2,1)}, bf16[264,2048]{1,0:T(8,128)(2,1)}, u32[]{:S(2)}, u32[]{:S(2)}) collective-permute-start(bf16[264,2048]{1,0:T(8,128)(2,1)} %get-tuple-element.130), channel_id=1, source_target_pairs={{0,16},{4,20},{8,24},{12,28},{16,0},{20,4},{24,8},{28,12},{1,17},{... | collective-permute-start | bytes 3244040 | tf_op jit(solution)/shard_map/ppermute | solution.py:882
  423.0 47.3 %copy-start.3 = (bf16[2,512,512]{2,1,0:T(8,128)(2,1)S(1)}, bf16[2,512,512]{2,1,0:T(8,128)(2,1)}, u32[]{:S(2)}) copy-start(bf16[2,512,512]{2,1,0:T(8,128)(2,1)} %param.17) | copy-start | bytes 3145732
  423.0 56.1 %collective-permute-start.25 = (bf16[264,2048]{1,0:T(8,128)(2,1)}, bf16[264,2048]{1,0:T(8,128)(2,1)}, u32[]{:S(2)}, u32[]{:S(2)}) collective-permute-start(bf16[264,2048]{1,0:T(8,128)(2,1)} %get-tuple-element.132), channel_id=1, source_target_pairs={{0,24},{4,28},{8,16},{12,20},{16,8},{20,12},{24,0},{28,4},{1,25},{... | collective-permute-start | bytes 3244040 | tf_op jit(solution)/shard_map/ppermute | solution.py:882
  481.8 27.2 %collective-permute-start.28 = (f32[8,128]{1,0:T(8,128)S(1)}, f32[8,128]{1,0:T(8,128)S(1)}, u32[]{:S(2)}, u32[]{:S(2)}) collective-permute-start(f32[8,128]{1,0:T(8,128)S(1)} %bitcast.117), channel_id=1, source_target_pairs={{0,3},{1,0},{2,1},{3,2},{4,7},{5,4},{6,5},{7,6},{8,11},{9,8},{10,9... | collective-permute-start | bytes 12296 | tf_op jit(solution)/shard_map/ppermute | solution.py:894
  500.8 8.1 %collective-permute-start.27 = (f32[8,128]{1,0:T(8,128)S(1)}, f32[8,128]{1,0:T(8,128)S(1)}, u32[]{:S(2)}, u32[]{:S(2)}) collective-permute-start(f32[8,128]{1,0:T(8,128)S(1)} %bitcast.118), channel_id=1, source_target_pairs={{0,2},{1,3},{2,0},{3,1},{4,6},{5,7},{6,4},{7,5},{8,10},{9,11},{10,... | collective-permute-start | bytes 12296 | tf_op jit(solution)/shard_map/ppermute | solution.py:894
  502.5 6.5 %collective-permute-start.26 = (f32[8,128]{1,0:T(8,128)S(1)}, f32[8,128]{1,0:T(8,128)S(1)}, u32[]{:S(2)}, u32[]{:S(2)}) collective-permute-start(f32[8,128]{1,0:T(8,128)S(1)} %bitcast.119), channel_id=1, source_target_pairs={{0,1},{1,2},{2,3},{3,0},{4,5},{5,6},{6,7},{7,4},{8,9},{9,10},{10,1... | collective-permute-start | bytes 12296 | tf_op jit(solution)/shard_map/ppermute | solution.py:894
  (19 other events, 175.0 us)
Sparse Core Ops, SparseCore 0:
  10.8 57.0 all-gather.9
  69.8 54.7 all-gather.11
  132.7 61.1 all-gather.13
  195.6 54.4 all-gather.7
  266.2 83.2 reduce-scatter.3
  353.3 78.7 reduce-scatter.7
  435.5 78.4 reduce-scatter.5

commit v5 on v4

--- a/solution.py
+++ b/solution.py
@@ -931,15 +931,6 @@
     shard = jnp.concatenate(
         [joined_weight.reshape(rows_part, -1), output_weight.reshape(rows_part, -1)], axis=1
     )
-    token_pairs = line_gather(own_tokens, "tp")
-    cot_start = after(own_cot, token_pairs)
-    cot_first = (
-        lax.ppermute(cot_start, "tp", [(i, i + 1) for i in range(ranks - 1)]),
-        lax.ppermute(cot_start, "tp", [(i + 1, i) for i in range(ranks - 1)]),
-    )
-    pack = lax.all_gather(shard, group, axis=0, tiled=False)
-    inner = lax.all_gather(inner_weight, group, axis=0, tiled=False)
-
     small = small.astype(F32)
     whole = [small[:, i * rows_part : (i + 1) * rows_part].reshape(width) for i in range(6)]
     at = 6 * rows_part
@@ -957,10 +948,6 @@
         .reshape(-1)
     )
     gains = jnp.stack(whole[:4])
-
-    places = jnp.stack([me, ctx]).astype(jnp.int32)
-    first_in, second_in, rows, stats = norm_call(places[:1], own_tokens, token_pairs, gains)
-    center, inverse = stats[:, 0:1], stats[:, 1:2]
     positions = ctx * local_len + jnp.arange(local_len, dtype=jnp.int32)
     half = ROTARY // 2
     frequency = 1.0 / 10000.0 ** (jnp.arange(half, dtype=F32) * 2.0 / ROTARY)
@@ -972,6 +959,19 @@
     table = jnp.concatenate(
         [cosine, cosine, ones, -sine, nothing, blank, nothing, sine, blank], axis=1
     )
+    early = (table, gains)
+    token_pairs = line_gather(own_tokens, "tp", None, early)
+    cot_start = after(own_cot, token_pairs)
+    cot_first = (
+        lax.ppermute(cot_start, "tp", [(i, i + 1) for i in range(ranks - 1)]),
+        lax.ppermute(cot_start, "tp", [(i + 1, i) for i in range(ranks - 1)]),
+    )
+    pack = lax.all_gather(shard, group, axis=0, tiled=False)
+    inner = lax.all_gather(inner_weight, group, axis=0, tiled=False)
+
+    places = jnp.stack([me, ctx]).astype(jnp.int32)
+    first_in, second_in, rows, stats = norm_call(places[:1], own_tokens, token_pairs, gains)
+    center, inverse = stats[:, 0:1], stats[:, 1:2]
     query, pair = joined_call(after(first_in, cot_first), pack, whole_joined_bias, table, seqs, heads)
     pairs = lax.all_gather(pair, "ctx", axis=0, tiled=False)
     low, odd = ctx - 2, ctx + 1 - 2 * lax.rem(ctx, 2)

time: 534 us -> 535 us (level)
  no operation moved by 1% of the time
where the time goes in v5:
time: 535 us; the launch traced here: 525 us
  Pallas kernels  211 us (39%)
  waiting for transfers between devices  158 us (30%)
  starting transfers between devices  92.7 us (17%)
  local copies, waits for them, and re-layouts  26.5 us (5%)
  other arithmetic  21.4 us (4%)
  between operations  15.1 us (3%)
    ppermute x5, waiting for transfers between devices, line_gather(): b = lax.ppermute(b, axis, down)  63.8 us
    ppermute x3, waiting for transfers between devices, send_chunks(): lax.ppermute(chunks[k], axis, [(i, (i + k) % size) for i in range(size)])  42.3 us
    pallas_call x2, Pallas kernels, product_call(): pl.pallas_call(functools.partial(product_kernel, sizes), grid=(sum(sizes)...  29.6 us
    ppermute x5, starting transfers between devices, line_gather(): a = lax.ppermute(a, axis, up)  27.5 us
    pallas_call x2, Pallas kernels, weight_grad_call(): pl.pallas_call(functools.partial(weight_grad_kernel, sizes, outs, int(sma...  24.2 us
    ppermute x3, starting transfers between devices, line_sum(): lax.ppermute(value, axis, [(i, (i + step) % size) for i in range(size)])  22.3 us
    pallas_call x2, Pallas kernels, backward_call(): pl.pallas_call(functools.partial(backward_kernel, heads, seq), grid_spec=...  17.6 us
    pallas_call x1, Pallas kernels, upper_call(): pl.pallas_call(upper_kernel, grid=(hidden // tile,), in_specs=[pl.BlockSp...  17.6 us
  transfers between devices with their start and end apart: 36, of which 20 were waited for; matrix products, arithmetic and copies ran while one was open for 7% of the time, Pallas kernels for 37%

profile of v5, /device:TPU:0, one launch (start us, length us, event | category | flops | bytes accessed | tf_op | source)
XLA Modules:
  0.0 525.4 jit_solution(252057929571801457)
XLA Ops:
  12.8 6.5 %collective-permute-start = (bf16[1024,512]{1,0:T(8,128)(2,1)S(1)}, bf16[1024,512]{1,0:T(8,128)(2,1)}, u32[]{:S(2)}, u32[]{:S(2)}) collective-permute-start(bf16[1024,512]{1,0:T(8,128)(2,1)S(1)} %bitcast.94), channel_id=1, source_target_pairs={{0,1},{1,2},{2,3},{4,5},{5,6},{6,7},{8,9},{9,10},{10,11},{12,13},{... | collective-permute-start | bytes 3145736 | tf_op jit(solution)/shard_map/ppermute | solution.py:55
  23.3 2.4 collective-permute-done.5
  27.9 11.8 %collective-permute-done.2.refs_5_ = bf16[1024,512]{1,0:T(8,128)(2,1)} collective-permute-done((bf16[1024,512]{1,0:T(8,128)(2,1)S(1)}, bf16[1024,512]{1,0:T(8,128)(2,1)}, u32[]{:S(2)}, u32[]{:S(2)}) %collective-permute-start.2) | collective-permute-done | bytes 1048608 | tf_op jit(solution)/shard_map/ppermute | solution.py:56
  41.0 5.6 %collective-permute-start.1 = (bf16[1024,512]{1,0:T(8,128)(2,1)}, bf16[1024,512]{1,0:T(8,128)(2,1)}, u32[]{:S(2)}, u32[]{:S(2)}) collective-permute-start(bf16[1024,512]{1,0:T(8,128)(2,1)} %collective-permute-done.refs_0_), channel_id=1, source_target_pairs={{0,1},{1,2},{2,3},{4,5},{5,6},{6,7},{8,9},{9,10},{10,11},{12,13},{... | collective-permute-start | bytes 3145736 | tf_op jit(solution)/shard_map/ppermute | solution.py:55
  49.9 16.3 %collective-permute-done.3.refs_3_ = bf16[1024,512]{1,0:T(8,128)(2,1)} collective-permute-done((bf16[1024,512]{1,0:T(8,128)(2,1)}, bf16[1024,512]{1,0:T(8,128)(2,1)}, u32[]{:S(2)}, u32[]{:S(2)}) %collective-permute-start.3) | collective-permute-done | bytes 1048608 | tf_op jit(solution)/shard_map/ppermute | solution.py:56
  68.7 5.1 collective-permute-start.8
  73.8 19.6 %collective-permute-done.7.refs_1_ = bf16[1024,512]{1,0:T(8,128)(2,1)S(1)} collective-permute-done((bf16[1024,512]{1,0:T(8,128)(2,1)}, bf16[1024,512]{1,0:T(8,128)(2,1)S(1)}, u32[]{:S(2)}, u32[]{:S(2)}) %collective-permute-start.7) | collective-permute-done | bytes 1048608 | tf_op jit(solution)/shard_map/ppermute | solution.py:56
  96.0 5.9 %collective-permute-start.9 = (bf16[1024,512]{1,0:T(8,128)(2,1)S(1)}, bf16[1024,512]{1,0:T(8,128)(2,1)}, u32[]{:S(2)}, u32[]{:S(2)}) collective-permute-start(bf16[1024,512]{1,0:T(8,128)(2,1)S(1)} %bitcast.100), channel_id=1, source_target_pairs={{0,1},{1,2},{2,3},{4,5},{5,6},{6,7},{8,9},{9,10},{10,11},{12,13},{... | collective-permute-start | bytes 3145736 | tf_op jit(solution)/shard_map/ppermute | solution.py:966
  102.1 12.1 %norm.1 = (bf16[1024,2048]{1,0:T(8,128)(2,1)}, bf16[1024,2048]{1,0:T(8,128)(2,1)}, bf16[1024,2048]{1,0:T(8,128)(2,1)}, f32[1024,128]{1,0:T(8,128)}) custom-call(s32[1]{0:T(128)} %bitcast.1.me_ref, bf16[1024,512]{1,0:T(8,128)(2,1)} %bitcast.92, bf16[1024,512]{1,0:T(8,128)(2,1)} %collective-permute-done.refs_0_, bf16[1024,512]{1,0:T(8,128)(2,1)} %copy-done.19, ...), custom_call_target="tpu_custom_call" | custom-call | flops 33554432 | bytes 20971520 | tf_op jit(solution)/shard_map/norm/pallas_call | solution.py:102
  114.2 5.3 %collective-permute-done.10.refs_5_ = bf16[1024,512]{1,0:T(8,128)(2,1)S(1)} collective-permute-done((bf16[1024,512]{1,0:T(8,128)(2,1)S(1)}, bf16[1024,512]{1,0:T(8,128)(2,1)S(1)}, u32[]{:S(2)}, u32[]{:S(2)}) %collective-permute-start.10) | collective-permute-done | bytes 1048608 | tf_op jit(solution)/shard_map/ppermute | solution.py:967
  121.3 13.3 %joined.1 = (bf16[1024,512]{1,0:T(8,128)(2,1)}, bf16[2,512,1024]{2,1,0:T(8,128)(2,1)}) custom-call(bf16[1024,2048]{1,0:T(8,128)(2,1)} %get-tuple-element.130.rows_ref.refs_0_.refs_1_.refs_2_.refs_3_, bf16[8,256,2048]{2,1,0:T(8,128)(2,1)} %bitcast.88, f32[8,1536]{1,0:T(8,128)} %broadcast_in_dim.37.bias_ref, f32[512,384]{1,0:T(8,128)} %concatenate.33.table_ref.refs_8_), custom_call_target="tpu_custom_call" | custom-call | flops 6442450944 | bytes 10485760 | tf_op jit(solution)/shard_map/joined/pallas_call | solution.py:220
  136.0 5.3 %collective-permute-start.11 = (bf16[1024,512]{1,0:T(8,128)(2,1)}, bf16[1024,512]{1,0:T(8,128)(2,1)S(1)}, u32[]{:S(2)}, u32[]{:S(2)}) collective-permute-start(bf16[1024,512]{1,0:T(8,128)(2,1)} %collective-permute-done.9.refs_0_), channel_id=1, source_target_pairs={{0,1},{1,2},{2,3},{4,5},{5,6},{6,7},{8,9},{9,10},{10,11},{12,13},{... | collective-permute-start | bytes 3145736 | tf_op jit(solution)/shard_map/ppermute | solution.py:55
  142.7 17.6 %upper.1 = (bf16[1024,2048]{1,0:T(8,128)(2,1)}, bf16[1024,2048]{1,0:T(8,128)(2,1)}) custom-call(bf16[1024,2048]{1,0:T(8,128)(2,1)} %get-tuple-element.129.rows_ref.refs_0_, bf16[8,256,2048]{2,1,0:T(8,128)(2,1)} %bitcast.125, f32[8,2048]{1,0:T(8,128)} %broadcast_in_dim.39.bias_ref), custom_call_target="tpu_custom_call" | custom-call | flops 8589934592 | bytes 12582912 | tf_op jit(solution)/shard_map/upper/pallas_call | solution.py:477
  161.6 5.0 collective-permute-start.14
  167.2 16.1 %collective-permute-done.13.refs_1_ = bf16[1024,512]{1,0:T(8,128)(2,1)S(1)} collective-permute-done((bf16[1024,512]{1,0:T(8,128)(2,1)S(1)}, bf16[1024,512]{1,0:T(8,128)(2,1)S(1)}, u32[]{:S(2)}, u32[]{:S(2)}) %collective-permute-start.13) | collective-permute-done | bytes 1048608 | tf_op jit(solution)/shard_map/ppermute | solution.py:56
  185.5 7.1 %cotangent_rows.1 = (bf16[1024,2048]{1,0:T(8,128)(2,1)}, f32[8,2048]{1,0:T(8,128)}) custom-call(s32[2]{0:T(128)} %pad_add_fusion.me_ref, s32[2]{0:T(128)} %lens.7, bf16[1024,512]{1,0:T(8,128)(2,1)} %bitcast.98, bf16[1024,512]{1,0:T(8,128)(2,1)} %collective-permute-done.9.refs_0_, bf16[1024,512]{1,0:T(8,128)(2,1)} %copy-done.17, ...), custom_call_target="tpu_custom_call" | custom-call | flops 8388608 | bytes 12582912 | tf_op jit(solution)/shard_map/cotangent_rows/pallas_call | solution.py:158
  192.7 2.1 all-gather.14.cloned.1.call-done
  195.5 5.7 %attention_forward.2 = (bf16[512,512]{1,0:T(8,128)(2,1)}, f32[512,256]{1,0:T(8,128)}) custom-call(s32[5]{0:T(128)} %stack.32.info, s32[2]{0:T(128)} %lens.7, bf16[1024,512]{1,0:T(8,128)(2,1)} %get-tuple-element.98.query_ref, bf16[4,2,512,1024]{3,2,1,0:T(8,128)(2,1)} %bitcast.84), custom_call_target="tpu_custom_call" | custom-call | flops 2147483648 | bytes 4194304 | tf_op jit(solution)/shard_map/attention_forward/pallas_call | solution.py:313
  201.2 8.4 %attention_forward.3 = (bf16[512,512]{1,0:T(8,128)(2,1)}, f32[512,256]{1,0:T(8,128)}) custom-call(s32[5]{0:T(128)} %stack.32.info, s32[2]{0:T(128)} %lens.7, bf16[1024,512]{1,0:T(8,128)(2,1)} %get-tuple-element.98.query_ref, bf16[4,2,512,1024]{3,2,1,0:T(8,128)(2,1)} %bitcast.85), custom_call_target="tpu_custom_call" | custom-call | flops 2147483648 | bytes 4194304 | tf_op jit(solution)/shard_map/attention_forward/pallas_call | solution.py:313
  209.6 5.5 %context_grad.1.grad_ref = bf16[1024,512]{1,0:T(8,128)(2,1)} custom-call(bf16[1024,2048]{1,0:T(8,128)(2,1)} %get-tuple-element.106.rows_ref.refs_0_.refs_4_.refs_5_.refs_6_.refs_7_, bf16[8,256,2048]{2,1,0:T(8,128)(2,1)} %bitcast.89), custom_call_target="tpu_custom_call" | custom-call | flops 2147483648 | bytes 6291456 | tf_op jit(solution)/shard_map/context_grad/pallas_call | solution.py:531
  215.1 8.2 %attention_backward.2 = (bf16[512,512]{1,0:T(8,128)(2,1)}, bf16[512,1024]{1,0:T(8,128)(2,1)}, bf16[512,1024]{1,0:T(8,128)(2,1)}, bf16[2,512,1024]{2,1,0:T(8,128)(2,1)}) custom-call(s32[5]{0:T(128)} %stack.32.info, s32[2]{0:T(128)} %lens.7, bf16[1024,512]{1,0:T(8,128)(2,1)} %get-tuple-element.98.query_ref, ...), custom_call_target="tpu_custom_call" | custom-call | flops 5368709120 | bytes 8388608 | tf_op jit(solution)/shard_map/attention_backward/pallas_call | solution.py:395
  223.4 9.4 %attention_backward.3 = (bf16[512,512]{1,0:T(8,128)(2,1)}, bf16[512,1024]{1,0:T(8,128)(2,1)}, bf16[512,1024]{1,0:T(8,128)(2,1)}, bf16[2,512,1024]{2,1,0:T(8,128)(2,1)}) custom-call(s32[5]{0:T(128)} %stack.32.info, s32[2]{0:T(128)} %lens.7, bf16[1024,512]{1,0:T(8,128)(2,1)} %get-tuple-element.98.query_ref, ...), custom_call_target="tpu_custom_call" | custom-call | flops 5368709120 | bytes 8388608 | tf_op jit(solution)/shard_map/attention_backward/pallas_call | solution.py:395
  232.7 5.7 %collective-permute-start.15 = (bf16[2,512,1024]{2,1,0:T(8,128)(2,1)}, bf16[2,512,1024]{2,1,0:T(8,128)(2,1)S(1)}, u32[]{:S(2)}, u32[]{:S(2)}) collective-permute-start(bf16[2,512,1024]{2,1,0:T(8,128)(2,1)} %get-tuple-element.101), channel_id=1, source_target_pairs={{0,4},{4,0},{8,12},{12,8},{1,5},{5,1},{9,13},{13,9},{2,6},{6,2},{1... | collective-permute-start | bytes 6291464 | tf_op jit(solution)/shard_map/ppermute | solution.py:423
  238.4 4.6 collective-permute-done.15.refs_6_
  242.9 8.1 %all-gather.8.cloned.1.call-done.refs_2_.weight_ref = bf16[2048,2048]{1,0:T(8,128)(2,1)} async-done(((bf16[256,2048]{1,0:T(8,128)(2,1)}), bf16[2048,2048]{1,0:T(8,128)(2,1)}) %all-gather.8.cloned.1.call-update) | async-done | bytes 8388624 | tf_op jit(solution)/shard_map/all_gather | solution.py:983
  251.0 16.0 %branch.1 = bf16[1024,2048]{1,0:T(8,128)(2,1)} custom-call(bf16[1024,2048]{1,0:T(8,128)(2,1)} %get-tuple-element.102.active_ref.refs_1_, bf16[512,512]{1,0:T(8,128)(2,1)} %get-tuple-element.91.context_ref.refs_0_, bf16[512,512]{1,0:T(8,128)(2,1)} %get-tuple-element.93.context_ref.refs_1_, bf16[2048,2048]{1,0:T(8,128)(2,1)} %all-gather.8.cloned.1.call-done.refs_2_.weight_ref, ...), custom_call_target="tpu_custom_call" | custom-call | flops 10737418240 | bytes 10485760 | tf_op jit(solution)/shard_map/branch/pallas_call | solution.py:440
  267.1 14.7 %product.2 = bf16[2048,2048]{1,0:T(8,128)(2,1)} custom-call(bf16[1024,2048]{1,0:T(8,128)(2,1)} %get-tuple-element.106.rows_ref.refs_0_.refs_4_.refs_5_.refs_6_.refs_7_, bf16[1024,2048]{1,0:T(8,128)(2,1)} %get-tuple-element.102.active_ref.refs_1_), custom_call_target="tpu_custom_call" | custom-call | flops 8589934592 | bytes 16777216 | tf_op jit(solution)/shard_map/product/pallas_call | solution.py:848
  291.5 13.9 %upper_grad.1 = (bf16[1024,2048]{1,0:T(8,128)(2,1)}, f32[8,2048]{1,0:T(8,128)}) custom-call(bf16[1024,2048]{1,0:T(8,128)(2,1)} %get-tuple-element.106.rows_ref.refs_0_.refs_4_.refs_5_.refs_6_.refs_7_, bf16[2048,2048]{1,0:T(8,128)(2,1)} %all-gather.8.cloned.1.call-done.refs_2_.weight_ref, bf16[1024,2048]{1,0:T(8,128)(2,1)} %get-tuple-element.107.slope_ref), custom_call_target="tpu_custom_call" | custom-call | flops 8589934592 | bytes 16777216 | tf_op jit(solution)/shard_map/upper_grad/pallas_call | solution.py:506
  305.4 15.0 %second_in_grad.1 = (bf16[1024,2048]{1,0:T(8,128)(2,1)}, f32[8,2048]{1,0:T(8,128)}) custom-call(bf16[1024,2048]{1,0:T(8,128)(2,1)} %get-tuple-element.108.grad_ref.refs_1_, bf16[8,256,2048]{2,1,0:T(8,128)(2,1)} %bitcast.126, bf16[1024,2048]{1,0:T(8,128)(2,1)} %get-tuple-element.109.rows_ref, f32[1024,128]{1,0:T(8,128)} %get-tuple-element.104.stat_ref, ...), custom_call_target="tpu_custom_call" | custom-call | flops 8589934592 | bytes 20971520 | tf_op jit(solution)/shard_map/second_in_grad/pallas_call | solution.py:566
  321.2 15.2 %collective-permute-done.17.refs_3_ = bf16[512,1024]{1,0:T(8,128)(2,1)S(1)} collective-permute-done((bf16[512,1024]{1,0:T(8,128)(2,1)S(1)}, bf16[512,1024]{1,0:T(8,128)(2,1)S(1)}, u32[]{:S(2)}, u32[]{:S(2)}) %collective-permute-start.17) | collective-permute-done | bytes 1048608 | tf_op jit(solution)/shard_map/ppermute | solution.py:425
  337.4 7.9 %joined_grad.1 = (bf16[1024,1536]{1,0:T(8,128)(2,1)}, f32[8,1536]{1,0:T(8,128)}) custom-call(bf16[512,512]{1,0:T(8,128)(2,1)} %get-tuple-element.111.refs_0_, bf16[512,1024]{1,0:T(8,128)(2,1)} %get-tuple-element.112.refs_1_, bf16[2,512,1024]{2,1,0:T(8,128)(2,1)} %collective-permute-done.16.refs_2_, bf16[512,1024]{1,0:T(8,128)(2,1)} %copy-done.12, ...), custom_call_target="tpu_custom_call" | custom-call | flops 15728640 | bytes 15728640 | tf_op jit(solution)/shard_map/joined_grad/pallas_call | solution.py:625
  346.3 17.4 %first_in_grad.1 = (bf16[1032,512]{1,0:T(8,128)(2,1)}, bf16[1032,512]{1,0:T(8,128)(2,1)}, bf16[1032,512]{1,0:T(8,128)(2,1)}, bf16[1032,512]{1,0:T(8,128)(2,1)}, f32[8,2048]{1,0:T(8,128)}) custom-call(s32[4]{0:T(128)} %compare_select_fusion.order, bf16[1024,1536]{1,0:T(8,128)(2,1)} %get-tuple-element.118.grad_ref.refs_8_, bf16[8,256,2048]{2,1,0:T(8,128)(2,1)} %bitcast.91, ...), custom_call_target="tpu_custom_call" | custom-call | flops 6442450944 | bytes 23068672 | tf_op jit(solution)/shard_map/first_in_grad/pallas_call | solution.py:683
  367.4 12.1 %weight_grad.2 = bf16[1056,2048]{1,0:T(8,128)(2,1)} custom-call(s32[4]{0:T(128)} %fusion.17.order, bf16[1024,2048]{1,0:T(8,128)(2,1)} %get-tuple-element.130.rows_ref.refs_0_.refs_1_.refs_2_.refs_3_, bf16[1024,2048]{1,0:T(8,128)(2,1)} %get-tuple-element.130.rows_ref.refs_0_.refs_1_.refs_2_.refs_3_, ...), custom_call_target="tpu_custom_call" | custom-call | flops 4294967296 | bytes 14680064 | tf_op jit(solution)/shard_map/weight_grad/pallas_call | solution.py:795
  379.6 14.9 %product.3 = bf16[2048,2048]{1,0:T(8,128)(2,1)} custom-call(bf16[1024,2048]{1,0:T(8,128)(2,1)} %get-tuple-element.129.rows_ref.refs_0_, bf16[1024,2048]{1,0:T(8,128)(2,1)} %get-tuple-element.108.grad_ref.refs_1_), custom_call_target="tpu_custom_call" | custom-call | flops 8589934592 | bytes 16777216 | tf_op jit(solution)/shard_map/product/pallas_call | solution.py:848
  396.4 2.4 collective-permute-start.20
  402.2 12.1 %weight_grad.3 = (bf16[264,2048]{1,0:T(8,128)(2,1)}, bf16[264,2048]{1,0:T(8,128)(2,1)}, bf16[264,2048]{1,0:T(8,128)(2,1)}, bf16[264,2048]{1,0:T(8,128)(2,1)}) custom-call(s32[4]{0:T(128)} %fusion.18.order, bf16[1024,2048]{1,0:T(8,128)(2,1)} %get-tuple-element.130.rows_ref.refs_0_.refs_1_.refs_2_.refs_3_, ...), custom_call_target="tpu_custom_call" | custom-call | flops 4294967296 | bytes 14680064 | tf_op jit(solution)/shard_map/weight_grad/pallas_call | solution.py:795
  414.4 5.6 %collective-permute-start.24 = (bf16[264,2048]{1,0:T(8,128)(2,1)}, bf16[264,2048]{1,0:T(8,128)(2,1)}, u32[]{:S(2)}, u32[]{:S(2)}) collective-permute-start(bf16[264,2048]{1,0:T(8,128)(2,1)} %get-tuple-element.134), channel_id=1, source_target_pairs={{0,16},{4,20},{8,24},{12,28},{16,0},{20,4},{24,8},{28,12},{1,17},{... | collective-permute-start | bytes 3244040 | tf_op jit(solution)/shard_map/ppermute | solution.py:882
  420.0 2.9 collective-permute-done.19
  423.9 4.4 collective-permute-start.25
  428.4 39.4 %collective-permute-done.20 = bf16[1032,512]{1,0:T(8,128)(2,1)S(1)} collective-permute-done((bf16[1032,512]{1,0:T(8,128)(2,1)}, bf16[1032,512]{1,0:T(8,128)(2,1)S(1)}, u32[]{:S(2)}, u32[]{:S(2)}) %collective-permute-start.20) | collective-permute-done | bytes 1056800 | tf_op jit(solution)/shard_map/ppermute | solution.py:65
  468.8 2.4 convert_add_fusion.2
  471.3 3.6 fusion.7
  474.9 5.1 collective-permute-done.25
  480.0 2.7 convert_add_fusion.1
  482.7 19.1 %collective-permute-start.28 = (f32[8,128]{1,0:T(8,128)S(1)}, f32[8,128]{1,0:T(8,128)S(1)}, u32[]{:S(2)}, u32[]{:S(2)}) collective-permute-start(f32[8,128]{1,0:T(8,128)S(1)} %bitcast.117), channel_id=1, source_target_pairs={{0,3},{1,0},{2,1},{3,2},{4,7},{5,4},{6,5},{7,6},{8,11},{9,8},{10,9... | collective-permute-start | bytes 12296 | tf_op jit(solution)/shard_map/ppermute | solution.py:894
  506.7 2.2 reshape.213
  510.6 2.8 convert_element_type.124
  515.0 2.8 convert_element_type.123
  (200 shorter events, 62.9 us)
Async XLA Ops:
  7.2 113.5 %all-gather.10.cloned.1.call-start = ((), (), s32[]{:S(2)}) async-start(), calls=%async_computation.7 | async-start | bytes 9437184 | tf_op jit(solution)/shard_map/all_gather | solution.py:969
  9.5 10.1 %copy-start.24 = (bf16[256]{0:T(256)(128)(2,1)S(1)}, bf16[256]{0:T(256)(128)(2,1)}, u32[]{:S(2)}) copy-start(bf16[256]{0:T(256)(128)(2,1)} %param.20) | copy-start | bytes 1540
  9.5 10.1 %copy-start.25 = (bf16[256]{0:T(256)(128)(2,1)S(1)}, bf16[256]{0:T(256)(128)(2,1)}, u32[]{:S(2)}) copy-start(bf16[256]{0:T(256)(128)(2,1)} %param.21) | copy-start | bytes 1540
  9.5 10.1 %copy-start.26 = (bf16[256]{0:T(256)(128)(2,1)S(1)}, bf16[256]{0:T(256)(128)(2,1)}, u32[]{:S(2)}) copy-start(bf16[256]{0:T(256)(128)(2,1)} %param.26) | copy-start | bytes 1540
  10.7 131.4 %all-gather.12.cloned.1.call-start = ((), (), s32[]{:S(2)}) async-start(), calls=%async_computation.8 | async-start | bytes 9437184 | tf_op jit(solution)/shard_map/all_gather | solution.py:970
  11.4 183.4 %all-gather.14.cloned.1.call-start = ((), (), s32[]{:S(2)}) async-start(), calls=%async_computation.9 | async-start | bytes 10485760 | tf_op jit(solution)/shard_map/all_gather | solution.py:976
  11.5 28.2 %collective-permute-start.2 = (bf16[1024,512]{1,0:T(8,128)(2,1)S(1)}, bf16[1024,512]{1,0:T(8,128)(2,1)}, u32[]{:S(2)}, u32[]{:S(2)}) collective-permute-start(bf16[1024,512]{1,0:T(8,128)(2,1)S(1)} %bitcast.93), channel_id=1, source_target_pairs={{1,0},{2,1},{3,2},{5,4},{6,5},{7,6},{9,8},{10,9},{11,10},{13,12},{... | collective-permute-start | bytes 3145736 | tf_op jit(solution)/shard_map/ppermute | solution.py:56
  12.8 28.2 %collective-permute-start = (bf16[1024,512]{1,0:T(8,128)(2,1)S(1)}, bf16[1024,512]{1,0:T(8,128)(2,1)}, u32[]{:S(2)}, u32[]{:S(2)}) collective-permute-start(bf16[1024,512]{1,0:T(8,128)(2,1)S(1)} %bitcast.94), channel_id=1, source_target_pairs={{0,1},{1,2},{2,3},{4,5},{5,6},{6,7},{8,9},{9,10},{10,11},{12,13},{... | collective-permute-start | bytes 3145736 | tf_op jit(solution)/shard_map/ppermute | solution.py:55
  19.9 1.3 collective-permute-start.4
  21.3 4.4 collective-permute-start.5
  25.8 23.4 %collective-permute-start.6 = (bf16[8,2048]{1,0:T(8,128)(2,1)S(1)}, bf16[8,2048]{1,0:T(8,128)(2,1)S(1)}, u32[]{:S(2)}, u32[]{:S(2)}) collective-permute-start(bf16[8,2048]{1,0:T(8,128)(2,1)S(1)} %add.115), channel_id=1, source_target_pairs={{0,16},{4,20},{8,24},{12,28},{16,0},{20,4},{24,8},{28,12},{1,17},{... | collective-permute-start | bytes 98312 | tf_op jit(solution)/shard_map/ppermute | solution.py:726
  39.7 26.5 %collective-permute-start.3 = (bf16[1024,512]{1,0:T(8,128)(2,1)}, bf16[1024,512]{1,0:T(8,128)(2,1)}, u32[]{:S(2)}, u32[]{:S(2)}) collective-permute-start(bf16[1024,512]{1,0:T(8,128)(2,1)} %collective-permute-done.2.refs_5_), channel_id=1, source_target_pairs={{1,0},{2,1},{3,2},{5,4},{6,5},{7,6},{9,8},{10,9},{11,10},{13,12},{... | collective-permute-start | bytes 3145736 | tf_op jit(solution)/shard_map/ppermute | solution.py:56
  41.0 26.4 %collective-permute-start.1 = (bf16[1024,512]{1,0:T(8,128)(2,1)}, bf16[1024,512]{1,0:T(8,128)(2,1)}, u32[]{:S(2)}, u32[]{:S(2)}) collective-permute-start(bf16[1024,512]{1,0:T(8,128)(2,1)} %collective-permute-done.refs_0_), channel_id=1, source_target_pairs={{0,1},{1,2},{2,3},{4,5},{5,6},{6,7},{8,9},{9,10},{10,11},{12,13},{... | collective-permute-start | bytes 3145736 | tf_op jit(solution)/shard_map/ppermute | solution.py:55
  47.6 47.1 %copy-start.13 = (bf16[2,512,512]{2,1,0:T(8,128)(2,1)S(1)}, bf16[2,512,512]{2,1,0:T(8,128)(2,1)}, u32[]{:S(2)}) copy-start(bf16[2,512,512]{2,1,0:T(8,128)(2,1)} %param.19) | copy-start | bytes 3145732
  67.4 26.0 %collective-permute-start.7 = (bf16[1024,512]{1,0:T(8,128)(2,1)}, bf16[1024,512]{1,0:T(8,128)(2,1)S(1)}, u32[]{:S(2)}, u32[]{:S(2)}) collective-permute-start(bf16[1024,512]{1,0:T(8,128)(2,1)} %collective-permute-done.3.refs_3_), channel_id=1, source_target_pairs={{1,0},{2,1},{3,2},{5,4},{6,5},{7,6},{9,8},{10,9},{11,10},{13,12},{... | collective-permute-start | bytes 3145736 | tf_op jit(solution)/shard_map/ppermute | solution.py:56
  68.7 26.0 %collective-permute-start.8 = (bf16[1024,512]{1,0:T(8,128)(2,1)}, bf16[1024,512]{1,0:T(8,128)(2,1)S(1)}, u32[]{:S(2)}, u32[]{:S(2)}) collective-permute-start(bf16[1024,512]{1,0:T(8,128)(2,1)} %collective-permute-done.1.refs_2_), channel_id=1, source_target_pairs={{0,1},{1,2},{2,3},{4,5},{5,6},{6,7},{8,9},{9,10},{10,11},{12,13},{... | collective-permute-start | bytes 3145736 | tf_op jit(solution)/shard_map/ppermute | solution.py:55
  94.7 24.8 %collective-permute-start.10 = (bf16[1024,512]{1,0:T(8,128)(2,1)S(1)}, bf16[1024,512]{1,0:T(8,128)(2,1)S(1)}, u32[]{:S(2)}, u32[]{:S(2)}) collective-permute-start(bf16[1024,512]{1,0:T(8,128)(2,1)S(1)} %bitcast.99), channel_id=1, source_target_pairs={{1,0},{2,1},{3,2},{5,4},{6,5},{7,6},{9,8},{10,9},{11,10},{13,12},{... | collective-permute-start | bytes 3145736 | tf_op jit(solution)/shard_map/ppermute | solution.py:967
  96.0 24.7 %collective-permute-start.9 = (bf16[1024,512]{1,0:T(8,128)(2,1)S(1)}, bf16[1024,512]{1,0:T(8,128)(2,1)}, u32[]{:S(2)}, u32[]{:S(2)}) collective-permute-start(bf16[1024,512]{1,0:T(8,128)(2,1)S(1)} %bitcast.100), channel_id=1, source_target_pairs={{0,1},{1,2},{2,3},{4,5},{5,6},{6,7},{8,9},{9,10},{10,11},{12,13},{... | collective-permute-start | bytes 3145736 | tf_op jit(solution)/shard_map/ppermute | solution.py:966
  119.5 15.2 %copy-start.14 = (bf16[1024,512]{1,0:T(8,128)(2,1)}, bf16[1024,512]{1,0:T(8,128)(2,1)S(1)}, u32[]{:S(2)}) copy-start(bf16[1024,512]{1,0:T(8,128)(2,1)S(1)} %collective-permute-done.10.refs_5_) | copy-start | bytes 3145732
  134.6 116.4 %all-gather.8.cloned.1.call-start = ((), (), s32[]{:S(2)}) async-start(), calls=%async_computation.3 | async-start | bytes 9437184 | tf_op jit(solution)/shard_map/all_gather | solution.py:983
  134.7 25.6 %collective-permute-start.12 = (bf16[1024,512]{1,0:T(8,128)(2,1)S(1)}, bf16[1024,512]{1,0:T(8,128)(2,1)S(1)}, u32[]{:S(2)}, u32[]{:S(2)}) collective-permute-start(bf16[1024,512]{1,0:T(8,128)(2,1)S(1)} %collective-permute-done.10.refs_5_), channel_id=1, source_target_pairs={{1,0},{2,1},{3,2},{5,4},{6,5},{7,6},{9,8},{10,9},{11,10},{13,12},{... | collective-permute-start | bytes 3145736 | tf_op jit(solution)/shard_map/ppermute | solution.py:56
  136.0 24.4 %collective-permute-start.11 = (bf16[1024,512]{1,0:T(8,128)(2,1)}, bf16[1024,512]{1,0:T(8,128)(2,1)S(1)}, u32[]{:S(2)}, u32[]{:S(2)}) collective-permute-start(bf16[1024,512]{1,0:T(8,128)(2,1)} %collective-permute-done.9.refs_0_), channel_id=1, source_target_pairs={{0,1},{1,2},{2,3},{4,5},{5,6},{6,7},{8,9},{9,10},{10,11},{12,13},{... | collective-permute-start | bytes 3145736 | tf_op jit(solution)/shard_map/ppermute | solution.py:55
  160.3 24.2 %copy-start.15 = (bf16[1024,512]{1,0:T(8,128)(2,1)}, bf16[1024,512]{1,0:T(8,128)(2,1)S(1)}, u32[]{:S(2)}) copy-start(bf16[1024,512]{1,0:T(8,128)(2,1)S(1)} %collective-permute-done.12.refs_3_) | copy-start | bytes 3145732
  160.3 24.2 %copy-start.16 = (bf16[1024,512]{1,0:T(8,128)(2,1)}, bf16[1024,512]{1,0:T(8,128)(2,1)S(1)}, u32[]{:S(2)}) copy-start(bf16[1024,512]{1,0:T(8,128)(2,1)S(1)} %collective-permute-done.11.refs_2_) | copy-start | bytes 3145732
  160.3 23.0 %collective-permute-start.13 = (bf16[1024,512]{1,0:T(8,128)(2,1)S(1)}, bf16[1024,512]{1,0:T(8,128)(2,1)S(1)}, u32[]{:S(2)}, u32[]{:S(2)}) collective-permute-start(bf16[1024,512]{1,0:T(8,128)(2,1)S(1)} %collective-permute-done.12.refs_3_), channel_id=1, source_target_pairs={{1,0},{2,1},{3,2},{5,4},{6,5},{7,6},{9,8},{10,9},{11,10},{13,12},{... | collective-permute-start | bytes 3145736 | tf_op jit(solution)/shard_map/ppermute | solution.py:56
  161.6 22.9 %collective-permute-start.14 = (bf16[1024,512]{1,0:T(8,128)(2,1)S(1)}, bf16[1024,512]{1,0:T(8,128)(2,1)S(1)}, u32[]{:S(2)}, u32[]{:S(2)}) collective-permute-start(bf16[1024,512]{1,0:T(8,128)(2,1)S(1)} %collective-permute-done.11.refs_2_), channel_id=1, source_target_pairs={{0,1},{1,2},{2,3},{4,5},{5,6},{6,7},{8,9},{9,10},{10,11},{12,13},{... | collective-permute-start | bytes 3145736 | tf_op jit(solution)/shard_map/ppermute | solution.py:55
  194.8 276.4 %reduce-scatter.4.cloned.1.call-start = ((), (), s32[]{:S(2)}) async-start(), calls=%async_computation.4 | async-start | bytes 5242880 | tf_op jit(solution)/shard_map/reduce_scatter | solution.py:1005
  232.7 10.2 %collective-permute-start.15 = (bf16[2,512,1024]{2,1,0:T(8,128)(2,1)}, bf16[2,512,1024]{2,1,0:T(8,128)(2,1)S(1)}, u32[]{:S(2)}, u32[]{:S(2)}) collective-permute-start(bf16[2,512,1024]{2,1,0:T(8,128)(2,1)} %get-tuple-element.101), channel_id=1, source_target_pairs={{0,4},{4,0},{8,12},{12,8},{1,5},{5,1},{9,13},{13,9},{2,6},{6,2},{1... | collective-permute-start | bytes 6291464 | tf_op jit(solution)/shard_map/ppermute | solution.py:423
  242.9 43.4 %copy-start.1 = (bf16[2,512,1024]{2,1,0:T(8,128)(2,1)}, bf16[2,512,1024]{2,1,0:T(8,128)(2,1)S(1)}, u32[]{:S(2)}) copy-start(bf16[2,512,1024]{2,1,0:T(8,128)(2,1)S(1)} %collective-permute-done.15.refs_6_) | copy-start | bytes 6291460
  267.0 243.5 %reduce-scatter.8.cloned.1.call-start = ((), (), s32[]{:S(2)}) async-start(), calls=%async_computation.6 | async-start | bytes 9437184 | tf_op jit(solution)/shard_map/reduce_scatter | solution.py:1012
  281.8 233.2 %reduce-scatter.6.cloned.1.call-start = ((), (), s32[]{:S(2)}) async-start(), calls=%async_computation.5 | async-start | bytes 9437184 | tf_op jit(solution)/shard_map/reduce_scatter | solution.py:1053
  281.9 6.2 %collective-permute-start.16 = (bf16[2,512,1024]{2,1,0:T(8,128)(2,1)}, bf16[2,512,1024]{2,1,0:T(8,128)(2,1)}, u32[]{:S(2)}, u32[]{:S(2)}) collective-permute-start(bf16[2,512,1024]{2,1,0:T(8,128)(2,1)} %get-tuple-element.113), channel_id=1, source_target_pairs={{0,4},{4,0},{8,12},{12,8},{1,5},{5,1},{9,13},{13,9},{2,6},{6,2},{1... | collective-permute-start | bytes 6291464 | tf_op jit(solution)/shard_map/ppermute | solution.py:423
  286.8 34.4 %collective-permute-start.18 = (bf16[512,1024]{1,0:T(8,128)(2,1)S(1)}, bf16[512,1024]{1,0:T(8,128)(2,1)S(1)}, u32[]{:S(2)}, u32[]{:S(2)}) collective-permute-start(bf16[512,1024]{1,0:T(8,128)(2,1)S(1)} %fusion.8), channel_id=1, source_target_pairs={{8,0},{12,4},{9,1},{13,5},{10,2},{14,6},{11,3},{15,7},{24,16},{28,... | collective-permute-start | bytes 3145736 | tf_op jit(solution)/shard_map/ppermute | solution.py:425
  289.8 46.7 %collective-permute-start.17 = (bf16[512,1024]{1,0:T(8,128)(2,1)S(1)}, bf16[512,1024]{1,0:T(8,128)(2,1)S(1)}, u32[]{:S(2)}, u32[]{:S(2)}) collective-permute-start(bf16[512,1024]{1,0:T(8,128)(2,1)S(1)} %fusion.9), channel_id=1, source_target_pairs={{8,0},{12,4},{9,1},{13,5},{10,2},{14,6},{11,3},{15,7},{24,16},{28,... | collective-permute-start | bytes 3145736 | tf_op jit(solution)/shard_map/ppermute | solution.py:425
  321.2 15.2 %copy-start.11 = (bf16[512,1024]{1,0:T(8,128)(2,1)}, bf16[512,1024]{1,0:T(8,128)(2,1)S(1)}, u32[]{:S(2)}) copy-start(bf16[512,1024]{1,0:T(8,128)(2,1)S(1)} %collective-permute-done.18.refs_7_) | copy-start | bytes 3145732
  394.5 7.8 %collective-permute-start.22 = (bf16[1056,2048]{1,0:T(8,128)(2,1)}, bf16[1056,2048]{1,0:T(8,128)(2,1)}, u32[]{:S(2)}, u32[]{:S(2)}) collective-permute-start(bf16[1056,2048]{1,0:T(8,128)(2,1)} %weight_grad.2), channel_id=1, source_target_pairs={{0,4},{4,0},{8,12},{12,8},{16,20},{20,16},{24,28},{28,24},{1,5},{5... | collective-permute-start | bytes 12976136 | tf_op jit(solution)/shard_map/ppermute | solution.py:877
  394.6 28.3 %collective-permute-start.19 = (bf16[1032,512]{1,0:T(8,128)(2,1)}, bf16[1032,512]{1,0:T(8,128)(2,1)S(1)}, u32[]{:S(2)}, u32[]{:S(2)}) collective-permute-start(bf16[1032,512]{1,0:T(8,128)(2,1)} %get-tuple-element.120), channel_id=1, source_target_pairs={{0,1},{1,2},{2,3},{3,0},{4,5},{5,6},{6,7},{7,4},{8,9},{9,10},{10,1... | collective-permute-start | bytes 3170312 | tf_op jit(solution)/shard_map/ppermute | solution.py:65
  396.4 71.4 %collective-permute-start.20 = (bf16[1032,512]{1,0:T(8,128)(2,1)}, bf16[1032,512]{1,0:T(8,128)(2,1)S(1)}, u32[]{:S(2)}, u32[]{:S(2)}) collective-permute-start(bf16[1032,512]{1,0:T(8,128)(2,1)} %get-tuple-element.121), channel_id=1, source_target_pairs={{0,2},{1,3},{2,0},{3,1},{4,6},{5,7},{6,4},{7,5},{8,10},{9,11},{10,... | collective-permute-start | bytes 3170312 | tf_op jit(solution)/shard_map/ppermute | solution.py:65
  398.8 70.0 %collective-permute-start.21 = (bf16[1032,512]{1,0:T(8,128)(2,1)}, bf16[1032,512]{1,0:T(8,128)(2,1)}, u32[]{:S(2)}, u32[]{:S(2)}) collective-permute-start(bf16[1032,512]{1,0:T(8,128)(2,1)} %get-tuple-element.122), channel_id=1, source_target_pairs={{0,3},{1,0},{2,1},{3,2},{4,7},{5,4},{6,5},{7,6},{8,11},{9,8},{10,9... | collective-permute-start | bytes 3170312 | tf_op jit(solution)/shard_map/ppermute | solution.py:65
  401.4 67.4 %copy-start.6 = (bf16[1032,512]{1,0:T(8,128)(2,1)S(1)}, bf16[1032,512]{1,0:T(8,128)(2,1)}, u32[]{:S(2)}) copy-start(bf16[1032,512]{1,0:T(8,128)(2,1)} %get-tuple-element.119) | copy-start | bytes 3170308
  414.3 60.5 %collective-permute-start.23 = (bf16[264,2048]{1,0:T(8,128)(2,1)}, bf16[264,2048]{1,0:T(8,128)(2,1)}, u32[]{:S(2)}, u32[]{:S(2)}) collective-permute-start(bf16[264,2048]{1,0:T(8,128)(2,1)} %get-tuple-element.132), channel_id=1, source_target_pairs={{0,8},{4,12},{8,0},{12,4},{16,24},{20,28},{24,16},{28,20},{1,9},{5... | collective-permute-start | bytes 3244040 | tf_op jit(solution)/shard_map/ppermute | solution.py:882
  414.4 60.4 %collective-permute-start.24 = (bf16[264,2048]{1,0:T(8,128)(2,1)}, bf16[264,2048]{1,0:T(8,128)(2,1)}, u32[]{:S(2)}, u32[]{:S(2)}) collective-permute-start(bf16[264,2048]{1,0:T(8,128)(2,1)} %get-tuple-element.134), channel_id=1, source_target_pairs={{0,16},{4,20},{8,24},{12,28},{16,0},{20,4},{24,8},{28,12},{1,17},{... | collective-permute-start | bytes 3244040 | tf_op jit(solution)/shard_map/ppermute | solution.py:882
  423.9 47.3 %copy-start.3 = (bf16[2,512,512]{2,1,0:T(8,128)(2,1)S(1)}, bf16[2,512,512]{2,1,0:T(8,128)(2,1)}, u32[]{:S(2)}) copy-start(bf16[2,512,512]{2,1,0:T(8,128)(2,1)} %param.17) | copy-start | bytes 3145732
  423.9 56.1 %collective-permute-start.25 = (bf16[264,2048]{1,0:T(8,128)(2,1)}, bf16[264,2048]{1,0:T(8,128)(2,1)}, u32[]{:S(2)}, u32[]{:S(2)}) collective-permute-start(bf16[264,2048]{1,0:T(8,128)(2,1)} %get-tuple-element.136), channel_id=1, source_target_pairs={{0,24},{4,28},{8,16},{12,20},{16,8},{20,12},{24,0},{28,4},{1,25},{... | collective-permute-start | bytes 3244040 | tf_op jit(solution)/shard_map/ppermute | solution.py:882
  482.7 27.3 %collective-permute-start.28 = (f32[8,128]{1,0:T(8,128)S(1)}, f32[8,128]{1,0:T(8,128)S(1)}, u32[]{:S(2)}, u32[]{:S(2)}) collective-permute-start(f32[8,128]{1,0:T(8,128)S(1)} %bitcast.117), channel_id=1, source_target_pairs={{0,3},{1,0},{2,1},{3,2},{4,7},{5,4},{6,5},{7,6},{8,11},{9,8},{10,9... | collective-permute-start | bytes 12296 | tf_op jit(solution)/shard_map/ppermute | solution.py:894
  501.8 8.2 %collective-permute-start.27 = (f32[8,128]{1,0:T(8,128)S(1)}, f32[8,128]{1,0:T(8,128)S(1)}, u32[]{:S(2)}, u32[]{:S(2)}) collective-permute-start(f32[8,128]{1,0:T(8,128)S(1)} %bitcast.118), channel_id=1, source_target_pairs={{0,2},{1,3},{2,0},{3,1},{4,6},{5,7},{6,4},{7,5},{8,10},{9,11},{10,... | collective-permute-start | bytes 12296 | tf_op jit(solution)/shard_map/ppermute | solution.py:894
  503.5 6.5 %collective-permute-start.26 = (f32[8,128]{1,0:T(8,128)S(1)}, f32[8,128]{1,0:T(8,128)S(1)}, u32[]{:S(2)}, u32[]{:S(2)}) collective-permute-start(f32[8,128]{1,0:T(8,128)S(1)} %bitcast.119), channel_id=1, source_target_pairs={{0,1},{1,2},{2,3},{3,0},{4,5},{5,6},{6,7},{7,4},{8,9},{9,10},{10,1... | collective-permute-start | bytes 12296 | tf_op jit(solution)/shard_map/ppermute | solution.py:894
  505.0 12.7 %copy-start.22 = (f32[1,256]{1,0:T(1,128)}, f32[1,256]{1,0:T(1,128)S(1)}, u32[]{:S(2)}) copy-start(f32[1,256]{1,0:T(1,128)S(1)} %get-tuple-element.211) | copy-start | bytes 3076
  (19 other events, 91.8 us)
Sparse Core Ops, SparseCore 0:
  10.8 57.7 all-gather.9
  70.5 54.3 all-gather.11
  134.7 60.0 all-gather.13
  196.5 54.3 all-gather.7
  267.2 83.2 reduce-scatter.3
  354.2 78.8 reduce-scatter.7
  436.5 78.4 reduce-scatter.5
